TPU v7x, 256 devices: a whole 4x4x8 slice. The times are simulated.
256 devices in a mesh: gx: 8 (over z), gy: 4 (over x), gz: 8 (over y, core).
Axes of the slice: x: 4, y: 4, z: 8, core: 2. Of those that a mesh axis runs over, the one named last changes fastest.
Arguments:
- positions: float32 [3, 32, 16, 2048], P(None, 'gx', 'gy', 'gz'), may hold values from -0.5 to 0.5
- charges: float32 [32, 16, 2048], P('gx', 'gy', 'gz'), may hold values from -0.06 to 0.06
- counts: int32 [32, 16, 32], P('gx', 'gy', 'gz'), may hold values from 1 to 64, 1280 in all within a row
- near_flags: int32 [26, 32, 16, 32], P(None, 'gx', 'gy', 'gz'), may hold values 0 or 1
- far_flags: int32 [343, 32, 16, 32], P(None, 'gx', 'gy', 'gz'), may hold values from 0 to 1, as said below
- up_operator: float32 [152, 152], replicated, may hold values from -0.00032461911 to 0.00045446676
- down_operator: float32 [152, 152], replicated, may hold values from -0.00032461911 to 0.00045446676
Outputs:
- potential: float32 [32, 16, 2048], P('gx', 'gy', 'gz')
Inputs may be any that keep to these rules, and one draw needn't show every extreme that they name: far_flags[c, t] is 1 only where d_c is in the octree interaction list of leaf t: some component of d_c has magnitude 2 or more and, along every dimension with leaf index i, the component lies in -2 - (i mod 2) .. 3 - (i mod 2); some entries of that list are left out.
All inputs are finite; a program needn't handle non-finite values. No bound on the sum of `counts` or of `near_flags` on one device may be relied on, other than what follows from the above.
Results may differ from a plain program's by a relative error of at most 0.0003.
Values may be sent and summed in bfloat16 or wider, within the bound.
No kernel may reach another device: no remote copies, remote signals or barrier semaphores. Data moves between devices by JAX's collectives and lax.ppermute only.
A program may use at most 128 MiB of HBM per device.

v0:
```python
import functools

import jax
import jax.numpy as jnp
import ml_dtypes
import numpy as np
from jax import lax
from jax.experimental import pallas as pl
from jax.experimental.pallas import tpu as pltpu
from jax.sharding import PartitionSpec as P

ORDER = 6
SURF = 152
SPAD = 160
WIDE = 256
LEAVES = 4
SLOTS = 64
CLASSES = 343
INNER = 1.05
OUTER = 2.95
SOFTEN = 0.01
HALF = 2.0
BREADTH = 4.0
HIGHEST = lax.Precision.HIGHEST
F32 = jnp.float32
BF16 = jnp.bfloat16
NT = (((1,), (1,)), ((), ()))
STEPS = (("gx", 4), ("gx", 2), ("gx", 1), ("gy", 2), ("gz", 4), ("gz", 2), ("gy", 1), ("gz", 1))


def surface_points():
    points = []
    for i in range(ORDER):
        for j in range(ORDER):
            for k in range(ORDER):
                if min(i, j, k) == 0 or max(i, j, k) == ORDER - 1:
                    points.append((i, j, k))
    return points


def tables():
    points = surface_points()
    spacing = np.linspace(-1.0, 1.0, ORDER)
    g = np.array([[spacing[i] for i in p] for p in points], dtype=np.float32)
    column = np.zeros((3, SPAD, WIDE), np.float32)
    column[:, :SURF, :] = g.T[:, :, None]
    row = np.zeros((8, WIDE), np.float32)
    row[:3, :SURF] = g.T
    where = {p: n for n, p in enumerate(points)}
    mirror = np.full((8, WIDE), -1, np.int32)
    for h in range(8):
        sign = (h >> 2 & 1, h >> 1 & 1, h & 1)
        for n, p in enumerate(points):
            mirror[h, n] = where[tuple(ORDER - 1 - c if f else c for c, f in zip(p, sign))]
    pick = np.zeros((64 * 8, 384), np.float32)
    for a in range(4):
        for b in range(4):
            for c in range(4):
                if max(a, b, c) < 2:
                    continue
                for h in range(8):
                    d = [-v if f else v for v, f in zip((a, b, c), (h >> 2 & 1, h >> 1 & 1, h & 1))]
                    number = (d[0] + 3) * 49 + (d[1] + 3) * 7 + d[2] + 3
                    pick[(a * 16 + b * 4 + c) * 8 + h, number] = 1.0
    return column, row, mirror, pick.astype(ml_dtypes.bfloat16)


def gathered_order():
    offsets = [(0, 0, 0)]
    for axis, distance in STEPS:
        n = ("gx", "gy", "gz").index(axis)
        offsets = offsets + [tuple(v + (distance if i == n else 0) for i, v in enumerate(o)) for o in offsets]
    table = np.zeros((256,), np.int32)
    for m, (x, y, z) in enumerate(offsets):
        table[(x * 4 + y) * 8 + z] = m
    return table


def iota(shape, dim):
    return lax.broadcasted_iota(jnp.int32, shape, dim)


def split2(v):
    hi = v.astype(BF16)
    return hi, (v - hi.astype(F32)).astype(BF16)


def inverse_distance(x, y, z):
    return lax.rsqrt(x * x + y * y + z * z + SOFTEN)


def occupied_row(counts, x, y):
    lane = iota((1, WIDE), 1)
    zone = lane >> 6
    n = jnp.where(
        zone < 2,
        jnp.where(zone == 0, counts[x, y, 0], counts[x, y, 1]),
        jnp.where(zone == 2, counts[x, y, 2], counts[x, y, 3]),
    )
    return ((lane & 63) < n).astype(F32)


def padded_operator(ref, out):
    out[...] = jnp.zeros_like(out)
    out[0:SURF, 0:SURF] = ref[...]


def leaf_squares(column, row, squares):
    for axis in range(3):
        outer = (OUTER * HALF) * column[axis]
        inner = (INNER * 0.5) * row[axis : axis + 1, :]
        for t in range(LEAVES):
            d = outer - ((t - 1.5) + inner)
            squares[axis * LEAVES + t] = d * d + (SOFTEN if axis == 2 else 0.0)


def upward_kernel(
    pos, chg, counts, up, column, row,
    eq_out, own_out, down_out, above_out, block_out,
    terms, operator, squares, acc,
):
    padded_operator(up, operator)
    leaf_squares(column, row, squares)

    for x in range(4):
        for y in range(4):
            r = x * 4 + y
            q = chg[x, y : y + 1, :] * occupied_row(counts, x, y)
            px, py, pz = (pos[c, x, y : y + 1, :] for c in range(3))
            k = (
                inverse_distance(
                    (OUTER * 0.5) * column[0] - px,
                    (OUTER * 0.5) * column[1] - py,
                    (OUTER * 0.5) * column[2] - pz,
                )
                * q
            )
            hi, lo = split2(k)
            terms[0:SPAD, r * WIDE : (r + 1) * WIDE] = hi
            terms[SPAD : 2 * SPAD, r * WIDE : (r + 1) * WIDE] = lo
            own_out[r, 0:1, :] = px
            own_out[r, 1:2, :] = py
            own_out[r, 2:3, :] = pz
            own_out[r, 3:4, :] = q
            for out, at in ((down_out, 0), (above_out, 128)):
                out[r, 2:3, 0:128] = px[:, at : at + 128]
                out[r, 2:3, 128:256] = py[:, at : at + 128]
                out[r, 3:4, 0:128] = pz[:, at : at + 128]
                out[r, 3:4, 128:256] = q[:, at : at + 128]
    gather = ((iota((16 * WIDE, 128), 0) >> 6) == iota((16 * WIDE, 128), 1)).astype(F32).astype(BF16)
    both = jnp.dot(terms[...], gather, preferred_element_type=F32)
    check = both[0:SPAD] + both[SPAD : 2 * SPAD]
    check = jnp.concatenate([check, jnp.zeros((WIDE - SPAD, 128), F32)], axis=0).T[0:64, :]
    up_eq = lax.dot_general(check, operator[...], NT, precision=HIGHEST, preferred_element_type=F32)
    low = up_eq.astype(BF16).astype(F32)
    for r in range(16):
        eq_out[r] = low[r * 4 : r * 4 + 4]
        down_out[r, 0:2, :] = low[r * 4 : r * 4 + 2]
        above_out[r, 0:2, :] = low[r * 4 + 2 : r * 4 + 4]
    acc[...] = jnp.zeros_like(acc)
    for part in range(4):
        rows = slice(part * 40, part * 40 + 40)
        total = jnp.zeros((40, WIDE), F32)
        for x in range(4):
            for y in range(4):
                xy = squares[x, rows, :] + squares[4 + y, rows, :]
                for z in range(4):
                    t = x * 16 + y * 4 + z
                    total = total + lax.rsqrt(xy + squares[8 + z, rows, :]) * up_eq[t : t + 1, :]
        acc[rows, :] = total
    ones = jnp.ones((8, WIDE), F32)
    summed = lax.dot_general(ones, acc[...], NT, precision=HIGHEST, preferred_element_type=F32)
    block = lax.dot_general(summed, operator[...], NT, precision=HIGHEST, preferred_element_type=F32)
    block_out[...] = (BREADTH * block)[0:1, :]


def merge_kernel(eq, own, right, left, eq_out, own_out, down_out, above_out):
    for r in range(16):
        x, y = r // 4, r % 4
        eq_out[r, 0:2, :] = left[r, 0:2, :]
        eq_out[r, 2:6, :] = eq[r]
        eq_out[r, 6:8, :] = right[r, 0:2, :]
        own_out[r, 0:4, :] = own[r]
        first = iota((1, 128), 1) < 64
        for c in range(4):
            at = slice((c % 2) * 128, (c % 2) * 128 + 128)
            line = 2 + c // 2
            own_out[r, 4 + c : 5 + c, 0:128] = jnp.where(first, right[r, line : line + 1, at], left[r, line : line + 1, at])
            own_out[r, 4 + c : 5 + c, 128:256] = jnp.zeros((1, 128), F32)
    for x in range(4):
        for n in range(2):
            down_out[x * 3 + n] = eq_out[x * 4 + n]
            above_out[x * 3 + n] = eq_out[x * 4 + 2 + n]
        down_out[x * 3 + 2] = own_out[x * 4]
        above_out[x * 3 + 2] = own_out[x * 4 + 3]


def eq_tile(refs, x, y):
    eq, _, ylo, yhi, xlo, xhi = refs
    if x < 2:
        return xlo[x * 8 + y]
    if x > 5:
        return xhi[(x - 6) * 8 + y]
    if y < 2:
        return ylo[(x - 2) * 3 + y]
    if y > 5:
        return yhi[(x - 2) * 3 + y - 6]
    return eq[(x - 2) * 4 + y - 2]


def own_tile(refs, x, y):
    _, own, ylo, yhi, xlo, xhi = refs
    if x < 0:
        return xlo[16 + y + 1]
    if x > 3:
        return xhi[16 + y + 1]
    if y < 0:
        return ylo[x * 3 + 2]
    if y > 3:
        return yhi[x * 3 + 2]
    return own[x * 4 + y]


def edge_kernel(eq, own, ylo, yhi, down_out, above_out):
    refs = (eq, own, ylo, yhi, None, None)
    for n in range(2):
        for y in range(8):
            down_out[n * 8 + y] = eq_tile(refs, 2 + n, y)
            above_out[n * 8 + y] = eq_tile(refs, 4 + n, y)
    for y in range(-1, 5):
        down_out[16 + y + 1] = own_tile(refs, 0, y)
        above_out[16 + y + 1] = own_tile(refs, 3, y)


def far_groups():
    groups = {}
    for a in range(4):
        for b in range(4):
            for c in range(4):
                if max(a, b, c) >= 2:
                    key = tuple(v in (1, 2) for v in (a, b, c))
                    groups.setdefault(key, []).append((a, b, c))
    return groups


def far_kernel(
    eq, own, ylo, yhi, xlo, xhi, flags, pick, mirror, column, row,
    out, low, turned, framed, chosen, squares, stacked, matrices, total,
):
    refs = (eq, own, ylo, yhi, xlo, xhi)
    for x in range(8):
        for y in range(0, 8, 2):
            pair = jnp.concatenate([eq_tile(refs, x, y), eq_tile(refs, x, y + 1)], axis=0)
            low[(x * 8 + y) * 8 : (x * 8 + y) * 8 + 16, :] = pair.astype(BF16)
    turn = ((iota((WIDE, WIDE), 0) ^ 7) == iota((WIDE, WIDE), 1)).astype(F32).astype(BF16)
    for n in range(2):
        part = slice(n * WIDE, n * WIDE + WIDE)
        turned[part, :] = jnp.dot(turn, low[part, :], preferred_element_type=F32).astype(BF16)

    def permutation(h):
        return (iota((WIDE, WIDE), 0) == mirror[h : h + 1, :]).astype(F32).astype(BF16)

    for h in range(8):
        source = turned if h & 1 else low
        frame = jnp.dot(source[...], permutation(h), preferred_element_type=F32)
        for x in range(8):
            for y in range(8):
                xf, yf = (7 - x if h & 4 else x), (7 - y if h & 2 else y)
                at = (x * 8 + y) * 8
                for n in range(2):
                    framed.at[n][pl.ds((xf * 8 + yf) * 64 + h, 8, stride=8), :] = frame[
                        at : at + 8, n * 128 : n * 128 + 128
                    ]
    picked = jnp.dot(pick[...], flags[...], preferred_element_type=F32)
    which = iota((512, 128), 0) & 7
    for h in range(8):
        mask = (48 if h & 4 else 0) + (12 if h & 2 else 0) + (3 if h & 1 else 0)
        turn = ((iota((128, 128), 0) ^ mask) == iota((128, 128), 1)).astype(F32).astype(BF16)
        part = jnp.dot(jnp.where(which == h, picked, 0.0).astype(BF16), turn, preferred_element_type=F32)
        chosen[...] = part if h == 0 else chosen[...] + part
    for axis in range(3):
        for d in range(4):
            v = (INNER * 0.5) * row[axis : axis + 1, :] - d - (INNER * 0.5) * column[axis]
            squares[axis * 4 + d] = v * v + (SOFTEN if axis == 2 else 0.0)
    matrices[...] = jnp.zeros_like(matrices)
    total[...] = jnp.zeros_like(total)
    for key, members in far_groups().items():
        ranges = [range(4) if every else (0, 2) for every in key]
        leaves = [(x, y, z) for x in ranges[0] for y in ranges[1] for z in ranges[2]]
        for n, (a, b, c) in enumerate(members):
            m = lax.rsqrt(squares[a] + squares[4 + b] + squares[8 + c])
            matrices[n * WIDE : n * WIDE + SPAD, :] = m.astype(BF16)
            flag = chosen[(a * 16 + b * 4 + c) * 8 : (a * 16 + b * 4 + c) * 8 + 8, :]
            for i in range(0, len(leaves), 2):
                tiles = []
                for x, y, z in leaves[i : i + 2]:
                    at = (((x + 2 + a) * 8 + y + 2 + b) * 8 + z + 2 + c) * 8
                    leaf = x * 16 + y * 4 + z
                    keep = jnp.broadcast_to(flag[:, leaf : leaf + 1], (8, 128))
                    tiles.append([framed[half, at : at + 8, :] * keep for half in range(2)])
                for half in range(2):
                    lanes = slice(n * WIDE + half * 128, n * WIDE + half * 128 + 128)
                    stacked[i * 8 : i * 8 + 16, lanes] = jnp.concatenate([t[half] for t in tiles], axis=0).astype(BF16)
        rows, depth = len(leaves) * 8, len(members) * WIDE
        product = jnp.dot(stacked[0:rows, 0:depth], matrices[0:depth, :], preferred_element_type=F32)
        for i, (x, y, z) in enumerate(leaves):
            leaf = x * 16 + y * 4 + z
            for half in range(2):
                total[half, leaf * 8 : leaf * 8 + 8, :] += product[i * 8 : i * 8 + 8, half * 128 : half * 128 + 128]
    result = jnp.zeros((64, WIDE), F32)
    for h in range(8):
        parts = [total.at[half][pl.ds(h, 64, stride=8), :] for half in range(2)]
        hi, lo = split2(jnp.concatenate(parts, axis=1))
        both = jnp.dot(jnp.concatenate([hi, lo], axis=0), permutation(h), preferred_element_type=F32).astype(BF16)
        mask = (48 if h & 4 else 0) + (12 if h & 2 else 0) + (3 if h & 1 else 0)
        turn = ((iota((64, 128), 0) ^ mask) == (iota((64, 128), 1) & 63)).astype(F32).astype(BF16)
        result = result + jnp.dot(turn, both, preferred_element_type=F32)
    out[...] = result


def near_kernel(own, ylo, yhi, xlo, xhi, flags, out, sources, points, listed, sums):
    refs = (None, own, ylo, yhi, xlo, xhi)
    for x in range(6):
        for y in range(6):
            tile = own_tile(refs, x - 1, y - 1)
            line = jnp.concatenate([tile[0:4, :], tile[4:8, 0:128]], axis=1)
            line = jnp.concatenate([line, line], axis=0)
            third = (iota((8, WIDE), 0) & 3) == 2
            for e, shift in ((0, 64), (1, 0), (2, 320)):
                moved = pltpu.roll(line, shift, 1) if shift else line
                sources[(x * 6 + y) * 3 + e] = moved[:, 0:256] + jnp.where(third, float(e - 1), 0.0)
    same = (iota((64, WIDE), 1) & 63) == iota((64, WIDE), 0)
    block = ((iota((WIDE, WIDE), 0) >> 6) == (iota((WIDE, WIDE), 1) >> 6)).astype(F32).astype(BF16)
    zone = iota((32, WIDE), 1) >> 6

    def one_row(r, carry):
        x, y = r >> 2, r & 3
        pieces = []
        for c in range(3):
            v = own[r, c : c + 1, :]
            for _ in range(3):
                b = v.astype(BF16).astype(F32)
                pieces.append(jnp.where(same, b, 0.0).astype(BF16))
                v = v - b
        spread = jnp.dot(jnp.concatenate(pieces, axis=0), block, preferred_element_type=F32)
        for c in range(3):
            at = c * 192
            points[c] = spread[at : at + 64] + spread[at + 64 : at + 128] + spread[at + 128 : at + 192]
        f = flags[x, y]
        lists = jnp.zeros((32, WIDE), F32)
        for z in range(4):
            lists = jnp.where(zone == z, f[:, z : z + 1], lists)
        listed[...] = lists

        def one_part(p, carry):
            at = pl.multiple_of(p * 16, 16)
            tx, ty, tz = (points[c, pl.ds(at, 16), :] for c in range(3))
            acc = jnp.zeros((16, WIDE), F32)
            n = 0
            for ex in range(3):
                for ey in range(3):
                    for ez in range(3):
                        s = ((x + ex) * 6 + y + ey) * 3 + ez
                        line = sources[s]
                        sx = line[0:1] + float(ex - 1)
                        sy = line[1:2] + float(ey - 1)
                        k = inverse_distance(tx - sx, ty - sy, tz - line[2:3])
                        if (ex, ey, ez) == (1, 1, 1):
                            me = (iota((16, WIDE), 1) & 63) == iota((16, WIDE), 0) + at
                            acc = acc + jnp.where(me, 0.0, k) * line[3:4]
                        else:
                            acc = acc + k * (line[3:4] * listed[n : n + 1, :])
                            n += 1
            sums[pl.ds(at, 16), :] = acc
            return carry

        lax.fori_loop(0, 4, one_part, 0)
        hi, lo = split2(sums[...])
        both = jnp.dot(jnp.concatenate([hi, lo], axis=0), block, preferred_element_type=F32)
        picked = jnp.where(same, both[0:64] + both[64:128], 0.0)
        out[pl.ds(r, 1), :] = jnp.sum(picked, axis=0, keepdims=True)
        return carry

    lax.fori_loop(0, 16, one_row, 0)


def last_kernel(
    order, counts, gathered, far, near, pos, down, column, row,
    out, operator, squares, offsets, acc, checks,
):
    padded_operator(down, operator)
    at = 0
    for axis, n in enumerate((8, 4, 8)):
        base = (INNER * HALF) * column[axis] - (INNER * HALF) * row[axis : axis + 1, :]
        for i in range(n):
            delta = (i + n // 2) % n - n // 2
            v = base - float(delta * 4)
            offsets[at + i] = v * v + (SOFTEN if axis == 2 else 0.0)
        at += n
    acc[...] = jnp.zeros_like(acc)

    def pair(i, carry):
        x, y = i >> 2, i & 3
        lines = []
        for z in range(8):
            m = order[i * 8 + z]
            lines.append(gathered[pl.ds(m, 1), :] * jnp.where(m == 0, 0.0, 1.0))
        for part in range(4):
            rows = slice(part * 40, part * 40 + 40)
            xy = offsets[x, rows, :] + offsets[8 + y, rows, :]
            total = acc[rows, :]
            for z in range(8):
                total = total + lax.rsqrt(xy + offsets[12 + z, rows, :]) * lines[z]
            acc[rows, :] = total
        return carry

    lax.fori_loop(0, 32, pair, 0)
    ones = jnp.ones((WIDE, WIDE), F32)
    summed = jnp.dot(acc[...], ones, precision=HIGHEST, preferred_element_type=F32)
    local = BREADTH * jnp.dot(operator[...], summed, precision=HIGHEST, preferred_element_type=F32)
    leaf_squares(column, row, squares)
    checks[...] = jnp.zeros_like(checks)
    for x in range(4):
        for y in range(4):
            lines = [jnp.zeros((8, WIDE), F32)] * 4
            for part in range(4):
                rows = slice(part * 40, part * 40 + 40)
                xy = squares[x, rows, :] + squares[4 + y, rows, :]
                weight = local[rows]
                for z in range(4):
                    v = lax.rsqrt(xy + squares[8 + z, rows, :]) * weight
                    for s in range(5):
                        lines[z] = lines[z] + v[s * 8 : s * 8 + 8]
            for z in range(4):
                t = x * 16 + y * 4 + z
                checks[t : t + 1, :] = jnp.sum(lines[z], axis=0, keepdims=True)
    checks[0:64, :] += far[...]
    local = jnp.dot(operator[...], checks[...].T, precision=HIGHEST, preferred_element_type=F32)
    hi, lo = split2(local[0:SPAD])
    both = jnp.concatenate([hi, lo], axis=0)
    for x in range(4):
        for y in range(4):
            r = x * 4 + y
            spread = (iota((128, WIDE), 0) == r * 4 + (iota((128, WIDE), 1) >> 6)).astype(F32).astype(BF16)
            wide = jnp.dot(both, spread, preferred_element_type=F32)
            px, py, pz = (pos[c, x, y : y + 1, :] for c in range(3))
            k = inverse_distance(
                (OUTER * 0.5) * column[0] - px,
                (OUTER * 0.5) * column[1] - py,
                (OUTER * 0.5) * column[2] - pz,
            )
            line = jnp.sum(k * (wide[0:SPAD] + wide[SPAD : 2 * SPAD]), axis=0, keepdims=True)
            out[x, y : y + 1, :] = occupied_row(counts, x, y) * (line + near[r : r + 1, :])


def call(body, outs, scratch, memory, name, *args):
    spaces = {"v": pltpu.VMEM, "s": pltpu.SMEM}
    return pl.pallas_call(
        body,
        out_shape=[jax.ShapeDtypeStruct(s, F32) for s in outs],
        in_specs=[pl.BlockSpec(memory_space=spaces[m]) for m in memory],
        out_specs=[pl.BlockSpec(memory_space=pltpu.VMEM) for _ in outs],
        scratch_shapes=[pltpu.VMEM(s, d) for s, d in scratch],
        compiler_params=pltpu.CompilerParams(vmem_limit_bytes=58 << 20),
        name=name,
    )(*args)


def exchanged(axis, down, above):
    n = lax.axis_size(axis)
    from_above = lax.ppermute(down, axis, [((i + 1) % n, i) for i in range(n)])
    from_below = lax.ppermute(above, axis, [(i, (i + 1) % n) for i in range(n)])
    return from_above, from_below


def body(positions, charges, counts, near_flags, far_flags, up_operator, down_operator):
    column, row, mirror, pick = (jnp.asarray(t) for t in tables())
    order = jnp.asarray(gathered_order())
    eq, own, down, above, block = call(
        upward_kernel,
        [(16, 4, WIDE), (16, 4, WIDE), (16, 4, WIDE), (16, 4, WIDE), (1, WIDE)],
        [((2 * SPAD, 16 * WIDE), BF16), ((WIDE, WIDE), F32), ((12, SPAD, WIDE), F32), ((WIDE, WIDE), F32)],
        "vvsvvv", "upward", positions, charges, counts, up_operator, column, row,
    )
    right, left = exchanged("gz", down, above)
    eq, own, down, above = call(
        merge_kernel, [(16, 8, WIDE), (16, 8, WIDE), (12, 8, WIDE), (12, 8, WIDE)], [], "vvvv", "merge", eq, own, right, left
    )
    yhi, ylo = exchanged("gy", down, above)
    down, above = call(edge_kernel, [(22, 8, WIDE), (22, 8, WIDE)], [], "vvvv", "edge", eq, own, ylo, yhi)
    xhi, xlo = exchanged("gx", down, above)
    gathered = block
    for axis, distance in STEPS:
        n = lax.axis_size(axis)
        other = lax.ppermute(gathered, axis, [((i + distance) % n, i) for i in range(n)])
        gathered = jnp.concatenate([gathered, other], axis=0)
    flags = jnp.pad(far_flags.reshape(CLASSES, 64).astype(BF16), ((0, 384 - CLASSES), (0, 64)))
    (far,) = call(
        far_kernel,
        [(64, WIDE)],
        [
            ((512, WIDE), BF16), ((512, WIDE), BF16), ((2, 4096, 128), F32), ((512, 128), F32),
            ((12, SPAD, WIDE), F32), ((512, 8 * WIDE), BF16), ((8 * WIDE, WIDE), BF16), ((2, 512, 128), F32),
        ],
        "vvvvvvvvvvv", "far", eq, own, ylo, yhi, xlo, xhi, flags, pick, mirror, column, row,
    )
    listed = jnp.pad(near_flags.transpose(1, 2, 0, 3).astype(F32), ((0, 0), (0, 0), (0, 6), (0, 0)))
    (near,) = call(
        near_kernel,
        [(16, WIDE)],
        [((108, 8, WIDE), F32), ((3, 64, WIDE), F32), ((32, WIDE), F32), ((64, WIDE), F32)],
        "vvvvvv", "near", own, ylo, yhi, xlo, xhi, listed,
    )
    (potential,) = call(
        last_kernel,
        [(4, 4, WIDE)],
        [((WIDE, WIDE), F32), ((12, SPAD, WIDE), F32), ((20, SPAD, WIDE), F32), ((WIDE, WIDE), F32), ((128, WIDE), F32)],
        "ssvvvvvvv", "last", order, counts, gathered, far, near, positions, down_operator, column, row,
    )
    return potential


def solution(mesh):
    return jax.shard_map(
        body,
        mesh=mesh,
        in_specs=(
            P(None, "gx", "gy", "gz"),
            P("gx", "gy", "gz"),
            P("gx", "gy", "gz"),
            P(None, "gx", "gy", "gz"),
            P(None, "gx", "gy", "gz"),
            P(),
            P(),
        ),
        out_specs=P("gx", "gy", "gz"),
        check_vma=False,
    )
```

profile of v0, /device:TPU:1, one launch (start us, length us, event | category | flops | bytes accessed | tf_op | source)
XLA Modules:
  0.0 110.4 jit_solution(15488331987999920785)
XLA Ops:
  0.0 6.8 %upward.1 = (f32[16,4,256]{2,1,0:T(4,128)}, f32[16,4,256]{2,1,0:T(4,128)}, f32[16,4,256]{2,1,0:T(4,128)}, f32[16,4,256]{2,1,0:T(4,128)}, f32[1,256]{1,0:T(1,128)}) custom-call(f32[3,4,4,256]{3,2,1,0:T(4,128)} %pos.3, f32[4,4,256]{2,1,0:T(4,128)} %chg.1, s32[4,4,4]{2,1,0:T(4,128)} %counts.3, f32[152,152]{1,0:T(8,128)} %up.1, ...), custom_call_target="tpu_custom_call" | custom-call | tf_op jit(solution)/shard_map/upward/pallas_call | solution.py:458
  6.8 0.0 copy-start.5
  6.8 0.7 copy-done.5
  7.4 7.7 %collective-permute-start = (f32[1,256]{1,0:T(1,128)S(1)}, f32[1,256]{1,0:T(1,128)S(1)}, u32[]{:S(2)}, u32[]{:S(2)}) collective-permute-start(f32[1,256]{1,0:T(1,128)S(1)} %copy-done.5), channel_id=1, source_target_pairs={{128,0},{160,32},{192,64},{224,96},{0,128},{32,160},{64,192},{96,2... | collective-permute-start | bytes 3080 | tf_op jit(solution)/shard_map/ppermute | solution.py:495
  15.2 1.0 collective-permute-done
  16.1 4.5 %collective-permute-start.1 = (f32[2,256]{1,0:T(2,128)S(1)}, f32[2,256]{1,0:T(2,128)S(1)}, u32[]{:S(2)}, u32[]{:S(2)}) collective-permute-start(f32[2,256]{1,0:T(2,128)S(1)} %pad_maximum_fusion.2), channel_id=1, source_target_pairs={{64,0},{96,32},{128,64},{160,96},{192,128},{224,160},{0,192},{32,2... | collective-permute-start | bytes 6152 | tf_op jit(solution)/shard_map/ppermute | solution.py:495
  20.6 2.1 %collective-permute-start.8 = (f32[16,4,256]{2,1,0:T(4,128)}, f32[16,4,256]{2,1,0:T(4,128)S(1)}, u32[]{:S(2)}, u32[]{:S(2)}) collective-permute-start(f32[16,4,256]{2,1,0:T(4,128)} %get-tuple-element.19), channel_id=1, source_target_pairs={{1,0},{2,1},{3,2},{4,3},{5,4},{6,5},{7,6},{0,7},{9,8},{10,9},{11,1... | collective-permute-start | bytes 196616 | tf_op jit(solution)/shard_map/ppermute | solution.py:471
  22.7 1.2 %collective-permute-start.9 = (f32[16,4,256]{2,1,0:T(4,128)}, f32[16,4,256]{2,1,0:T(4,128)S(1)}, u32[]{:S(2)}, u32[]{:S(2)}) collective-permute-start(f32[16,4,256]{2,1,0:T(4,128)} %get-tuple-element.20), channel_id=1, source_target_pairs={{0,1},{1,2},{2,3},{3,4},{4,5},{5,6},{6,7},{7,0},{8,9},{9,10},{10,1... | collective-permute-start | bytes 196616 | tf_op jit(solution)/shard_map/ppermute | solution.py:472
  23.9 0.0 collective-permute-done.1
  23.9 0.9 collective-permute-start.2
  24.8 1.3 %collective-permute-done.8.right = f32[16,4,256]{2,1,0:T(4,128)S(1)} collective-permute-done((f32[16,4,256]{2,1,0:T(4,128)}, f32[16,4,256]{2,1,0:T(4,128)S(1)}, u32[]{:S(2)}, u32[]{:S(2)}) %collective-permute-start.8) | collective-permute-done | bytes 65568 | tf_op jit(solution)/shard_map/ppermute | solution.py:471
  26.1 0.0 copy-start.6
  26.1 0.0 collective-permute-done.9.left
  26.1 0.0 copy-start.7
  26.1 0.6 copy-done.6
  26.7 0.0 copy-done.7
  26.7 1.8 %merge.1 = (f32[16,8,256]{2,1,0:T(8,128)}, f32[16,8,256]{2,1,0:T(8,128)}, f32[12,8,256]{2,1,0:T(8,128)}, f32[12,8,256]{2,1,0:T(8,128)}) custom-call(f32[16,4,256]{2,1,0:T(4,128)} %get-tuple-element.17.eq, f32[16,4,256]{2,1,0:T(4,128)} %get-tuple-element.18.own, f32[16,4,256]{2,1,0:T(4,128)} %copy-done.6, f32[16,4,256]{2,1,0:T(4,128)} %copy-done.7), custom_call_target="tpu_custom_call" | custom-call | tf_op jit(solution)/shard_map/merge/pallas_call | solution.py:458
  28.5 1.2 %collective-permute-start.10 = (f32[12,8,256]{2,1,0:T(8,128)}, f32[12,8,256]{2,1,0:T(8,128)S(1)}, u32[]{:S(2)}, u32[]{:S(2)}) collective-permute-start(f32[12,8,256]{2,1,0:T(8,128)} %get-tuple-element.23), channel_id=1, source_target_pairs={{0,8},{8,16},{16,24},{24,0},{1,9},{9,17},{17,25},{25,1},{2,10},{10... | collective-permute-start | bytes 294920 | tf_op jit(solution)/shard_map/ppermute | solution.py:472
  29.7 1.5 %collective-permute-start.11 = (f32[12,8,256]{2,1,0:T(8,128)}, f32[12,8,256]{2,1,0:T(8,128)S(1)}, u32[]{:S(2)}, u32[]{:S(2)}) collective-permute-start(f32[12,8,256]{2,1,0:T(8,128)} %get-tuple-element.24), channel_id=1, source_target_pairs={{8,0},{16,8},{24,16},{0,24},{9,1},{17,9},{25,17},{1,25},{10,2},{18... | collective-permute-start | bytes 294920 | tf_op jit(solution)/shard_map/ppermute | solution.py:471
  31.2 0.0 collective-permute-done.2
  31.2 1.6 %collective-permute-start.3 = (f32[8,256]{1,0:T(8,128)S(1)}, f32[8,256]{1,0:T(8,128)S(1)}, u32[]{:S(2)}, u32[]{:S(2)}) collective-permute-start(f32[8,256]{1,0:T(8,128)S(1)} %pad_maximum_fusion), channel_id=1, source_target_pairs={{16,0},{24,8},{0,16},{8,24},{17,1},{25,9},{1,17},{9,25},{18,2},{26... | collective-permute-start | bytes 24584 | tf_op jit(solution)/shard_map/ppermute | solution.py:495
  32.8 2.5 %collective-permute-done.3 = f32[8,256]{1,0:T(8,128)S(1)} collective-permute-done((f32[8,256]{1,0:T(8,128)S(1)}, f32[8,256]{1,0:T(8,128)S(1)}, u32[]{:S(2)}, u32[]{:S(2)}) %collective-permute-start.3) | collective-permute-done | bytes 8224 | tf_op jit(solution)/shard_map/ppermute | solution.py:495
  35.3 3.1 %collective-permute-start.4 = (f32[16,256]{1,0:T(8,128)S(1)}, f32[16,256]{1,0:T(8,128)S(1)}, u32[]{:S(2)}, u32[]{:S(2)}) collective-permute-start(f32[16,256]{1,0:T(8,128)S(1)} %concatenate.34), channel_id=1, source_target_pairs={{4,0},{5,1},{6,2},{7,3},{0,4},{1,5},{2,6},{3,7},{12,8},{13,9},{14,... | collective-permute-start | bytes 49160 | tf_op jit(solution)/shard_map/ppermute | solution.py:495
  38.4 1.1 %collective-permute-done.4 = f32[16,256]{1,0:T(8,128)S(1)} collective-permute-done((f32[16,256]{1,0:T(8,128)S(1)}, f32[16,256]{1,0:T(8,128)S(1)}, u32[]{:S(2)}, u32[]{:S(2)}) %collective-permute-start.4) | collective-permute-done | bytes 16416 | tf_op jit(solution)/shard_map/ppermute | solution.py:495
  39.5 2.5 %collective-permute-start.5 = (f32[32,256]{1,0:T(8,128)S(1)}, f32[32,256]{1,0:T(8,128)S(1)}, u32[]{:S(2)}, u32[]{:S(2)}) collective-permute-start(f32[32,256]{1,0:T(8,128)S(1)} %concatenate.35), channel_id=1, source_target_pairs={{2,0},{3,1},{4,2},{5,3},{6,4},{7,5},{0,6},{1,7},{10,8},{11,9},{12,... | collective-permute-start | bytes 98312 | tf_op jit(solution)/shard_map/ppermute | solution.py:495
  42.1 1.0 collective-permute-done.5
  43.1 1.2 %collective-permute-start.6 = (f32[64,256]{1,0:T(8,128)S(1)}, f32[64,256]{1,0:T(8,128)S(1)}, u32[]{:S(2)}, u32[]{:S(2)}) collective-permute-start(f32[64,256]{1,0:T(8,128)S(1)} %concatenate.36), channel_id=1, source_target_pairs={{8,0},{16,8},{24,16},{0,24},{9,1},{17,9},{25,17},{1,25},{10,2},{18... | collective-permute-start | bytes 196616 | tf_op jit(solution)/shard_map/ppermute | solution.py:495
  44.4 0.0 collective-permute-done.10.ylo
  44.4 0.0 copy-start
  44.4 0.0 collective-permute-done.11.yhi
  44.4 0.0 copy-start.1
  44.4 0.6 copy-done
  45.0 0.0 copy-done.1
  45.0 1.8 %edge.1 = (f32[22,8,256]{2,1,0:T(8,128)}, f32[22,8,256]{2,1,0:T(8,128)}) custom-call(f32[16,8,256]{2,1,0:T(8,128)} %get-tuple-element.21.eq, f32[16,8,256]{2,1,0:T(8,128)} %get-tuple-element.22.own, f32[12,8,256]{2,1,0:T(8,128)} %copy-done, f32[12,8,256]{2,1,0:T(8,128)} %copy-done.1), custom_call_target="tpu_custom_call" | custom-call | tf_op jit(solution)/shard_map/edge/pallas_call | solution.py:458
  46.9 0.8 collective-permute-start.12
  47.7 0.0 copy-start.8
  47.7 1.8 %collective-permute-start.13 = (f32[22,8,256]{2,1,0:T(8,128)}, f32[22,8,256]{2,1,0:T(8,128)S(1)}, u32[]{:S(2)}, u32[]{:S(2)}) collective-permute-start(f32[22,8,256]{2,1,0:T(8,128)} %get-tuple-element.26), channel_id=1, source_target_pairs={{32,0},{64,32},{96,64},{128,96},{160,128},{192,160},{224,192},{0,2... | collective-permute-start | bytes 540680 | tf_op jit(solution)/shard_map/ppermute | solution.py:471
  49.5 0.0 collective-permute-done.6
  49.6 7.0 %collective-permute-start.7 = (f32[128,256]{1,0:T(8,128)S(1)}, f32[128,256]{1,0:T(8,128)S(1)}, u32[]{:S(2)}, u32[]{:S(2)}) collective-permute-start(f32[128,256]{1,0:T(8,128)S(1)} %concatenate.37), channel_id=1, source_target_pairs={{1,0},{2,1},{3,2},{4,3},{5,4},{6,5},{7,6},{0,7},{9,8},{10,9},{11,1... | collective-permute-start | bytes 393224 | tf_op jit(solution)/shard_map/ppermute | solution.py:495
  56.5 0.0 copy-done.8
  56.5 0.0 copy-start.4
  56.6 0.2 copy.16
  56.8 0.7 copy-done.4
  57.5 0.1 copy.15
  57.6 0.7 pad.9.flags
  58.4 0.7 pad.8.flags
  59.0 0.8 collective-permute-done.7
  59.8 3.7 %concatenate.38.gathered = f32[256,256]{1,0:T(8,128)} concatenate(f32[1,256]{1,0:T(1,128)S(1)} %copy-done.5, f32[1,256]{1,0:T(1,128)S(1)} %collective-permute-done, f32[2,256]{1,0:T(2,128)S(1)} %collective-permute-done.1, f32[4,256]{1,0:T(4,128)S(1)} %collective-permute-done.2, f32[8,256]{1,0:T(8,128)S(1)} %collective-permute-done.3, f32[16,256]{1,0:T(8,128)S(1)} %collective-permute-done.4, ...), dimensions={0} | concatenate | bytes 524288 | tf_op jit(solution)/shard_map/concatenate | solution.py:496
  63.5 0.0 collective-permute-done.12.xlo
  63.5 0.0 copy-start.2
  63.5 0.0 collective-permute-done.13.xhi
  63.5 0.7 copy-done.2
  64.1 0.0 copy-start.3
  64.1 0.7 copy-done.3
  64.8 23.2 %near.1 = f32[16,256]{1,0:T(8,128)} custom-call(f32[16,8,256]{2,1,0:T(8,128)} %get-tuple-element.22.own, f32[12,8,256]{2,1,0:T(8,128)} %copy-done, f32[12,8,256]{2,1,0:T(8,128)} %copy-done.1, f32[22,8,256]{2,1,0:T(8,128)} %copy-done.2, f32[22,8,256]{2,1,0:T(8,128)} %copy-done.3, f32[4,4,32,4]{3,2,1,0:T(8,128)} %pad.9.flags), custom_call_target="tpu_custom_call" | custom-call | tf_op jit(solution)/shard_map/near/pallas_call | solution.py:458
  88.0 8.2 %far.1 = f32[64,256]{1,0:T(8,128)} custom-call(f32[16,8,256]{2,1,0:T(8,128)} %get-tuple-element.21.eq, f32[16,8,256]{2,1,0:T(8,128)} %get-tuple-element.22.own, f32[12,8,256]{2,1,0:T(8,128)} %copy-done, f32[12,8,256]{2,1,0:T(8,128)} %copy-done.1, f32[22,8,256]{2,1,0:T(8,128)} %copy-done.2, f32[22,8,256]{2,1,0:T(8,128)} %copy-done.3, ...), custom_call_target="tpu_custom_call" | custom-call | tf_op jit(solution)/shard_map/far/pallas_call | solution.py:458
  96.2 14.2 %last.1 = f32[4,4,256]{2,1,0:T(4,128)} custom-call(s32[256]{0:T(256)} %constant.19.clone.order, s32[4,4,4]{2,1,0:T(4,128)} %counts.3, f32[256,256]{1,0:T(8,128)} %concatenate.38.gathered, f32[64,256]{1,0:T(8,128)} %far.1, f32[16,256]{1,0:T(8,128)} %near.1, f32[3,4,4,256]{3,2,1,0:T(4,128)} %pos.3, f32[152,152]{1,0:T(8,128)} %down.1, ...), custom_call_target="tpu_custom_call" | custom-call | tf_op jit(solution)/shard_map/last/pallas_call | solution.py:458
  (10 shorter events, 0.2 us)
Async XLA Ops:
  6.8 0.7 copy-start.5
  7.4 8.7 %collective-permute-start = (f32[1,256]{1,0:T(1,128)S(1)}, f32[1,256]{1,0:T(1,128)S(1)}, u32[]{:S(2)}, u32[]{:S(2)}) collective-permute-start(f32[1,256]{1,0:T(1,128)S(1)} %copy-done.5), channel_id=1, source_target_pairs={{128,0},{160,32},{192,64},{224,96},{0,128},{32,160},{64,192},{96,2... | collective-permute-start | bytes 3080 | tf_op jit(solution)/shard_map/ppermute | solution.py:495
  16.1 7.8 %collective-permute-start.1 = (f32[2,256]{1,0:T(2,128)S(1)}, f32[2,256]{1,0:T(2,128)S(1)}, u32[]{:S(2)}, u32[]{:S(2)}) collective-permute-start(f32[2,256]{1,0:T(2,128)S(1)} %pad_maximum_fusion.2), channel_id=1, source_target_pairs={{64,0},{96,32},{128,64},{160,96},{192,128},{224,160},{0,192},{32,2... | collective-permute-start | bytes 6152 | tf_op jit(solution)/shard_map/ppermute | solution.py:495
  20.6 5.4 %collective-permute-start.8 = (f32[16,4,256]{2,1,0:T(4,128)}, f32[16,4,256]{2,1,0:T(4,128)S(1)}, u32[]{:S(2)}, u32[]{:S(2)}) collective-permute-start(f32[16,4,256]{2,1,0:T(4,128)} %get-tuple-element.19), channel_id=1, source_target_pairs={{1,0},{2,1},{3,2},{4,3},{5,4},{6,5},{7,6},{0,7},{9,8},{10,9},{11,1... | collective-permute-start | bytes 196616 | tf_op jit(solution)/shard_map/ppermute | solution.py:471
  22.7 3.3 %collective-permute-start.9 = (f32[16,4,256]{2,1,0:T(4,128)}, f32[16,4,256]{2,1,0:T(4,128)S(1)}, u32[]{:S(2)}, u32[]{:S(2)}) collective-permute-start(f32[16,4,256]{2,1,0:T(4,128)} %get-tuple-element.20), channel_id=1, source_target_pairs={{0,1},{1,2},{2,3},{3,4},{4,5},{5,6},{6,7},{7,0},{8,9},{9,10},{10,1... | collective-permute-start | bytes 196616 | tf_op jit(solution)/shard_map/ppermute | solution.py:472
  23.9 7.2 %collective-permute-start.2 = (f32[4,256]{1,0:T(4,128)S(1)}, f32[4,256]{1,0:T(4,128)S(1)}, u32[]{:S(2)}, u32[]{:S(2)}) collective-permute-start(f32[4,256]{1,0:T(4,128)S(1)} %pad_maximum_fusion.1), channel_id=1, source_target_pairs={{32,0},{64,32},{96,64},{128,96},{160,128},{192,160},{224,192},{0,2... | collective-permute-start | bytes 12296 | tf_op jit(solution)/shard_map/ppermute | solution.py:495
  26.1 0.6 copy-start.6
  26.1 0.6 copy-start.7
  28.5 15.9 %collective-permute-start.10 = (f32[12,8,256]{2,1,0:T(8,128)}, f32[12,8,256]{2,1,0:T(8,128)S(1)}, u32[]{:S(2)}, u32[]{:S(2)}) collective-permute-start(f32[12,8,256]{2,1,0:T(8,128)} %get-tuple-element.23), channel_id=1, source_target_pairs={{0,8},{8,16},{16,24},{24,0},{1,9},{9,17},{17,25},{25,1},{2,10},{10... | collective-permute-start | bytes 294920 | tf_op jit(solution)/shard_map/ppermute | solution.py:472
  29.7 14.7 %collective-permute-start.11 = (f32[12,8,256]{2,1,0:T(8,128)}, f32[12,8,256]{2,1,0:T(8,128)S(1)}, u32[]{:S(2)}, u32[]{:S(2)}) collective-permute-start(f32[12,8,256]{2,1,0:T(8,128)} %get-tuple-element.24), channel_id=1, source_target_pairs={{8,0},{16,8},{24,16},{0,24},{9,1},{17,9},{25,17},{1,25},{10,2},{18... | collective-permute-start | bytes 294920 | tf_op jit(solution)/shard_map/ppermute | solution.py:471
  31.2 4.1 %collective-permute-start.3 = (f32[8,256]{1,0:T(8,128)S(1)}, f32[8,256]{1,0:T(8,128)S(1)}, u32[]{:S(2)}, u32[]{:S(2)}) collective-permute-start(f32[8,256]{1,0:T(8,128)S(1)} %pad_maximum_fusion), channel_id=1, source_target_pairs={{16,0},{24,8},{0,16},{8,24},{17,1},{25,9},{1,17},{9,25},{18,2},{26... | collective-permute-start | bytes 24584 | tf_op jit(solution)/shard_map/ppermute | solution.py:495
  35.3 4.2 %collective-permute-start.4 = (f32[16,256]{1,0:T(8,128)S(1)}, f32[16,256]{1,0:T(8,128)S(1)}, u32[]{:S(2)}, u32[]{:S(2)}) collective-permute-start(f32[16,256]{1,0:T(8,128)S(1)} %concatenate.34), channel_id=1, source_target_pairs={{4,0},{5,1},{6,2},{7,3},{0,4},{1,5},{2,6},{3,7},{12,8},{13,9},{14,... | collective-permute-start | bytes 49160 | tf_op jit(solution)/shard_map/ppermute | solution.py:495
  39.5 3.5 %collective-permute-start.5 = (f32[32,256]{1,0:T(8,128)S(1)}, f32[32,256]{1,0:T(8,128)S(1)}, u32[]{:S(2)}, u32[]{:S(2)}) collective-permute-start(f32[32,256]{1,0:T(8,128)S(1)} %concatenate.35), channel_id=1, source_target_pairs={{2,0},{3,1},{4,2},{5,3},{6,4},{7,5},{0,6},{1,7},{10,8},{11,9},{12,... | collective-permute-start | bytes 98312 | tf_op jit(solution)/shard_map/ppermute | solution.py:495
  43.1 6.4 %collective-permute-start.6 = (f32[64,256]{1,0:T(8,128)S(1)}, f32[64,256]{1,0:T(8,128)S(1)}, u32[]{:S(2)}, u32[]{:S(2)}) collective-permute-start(f32[64,256]{1,0:T(8,128)S(1)} %concatenate.36), channel_id=1, source_target_pairs={{8,0},{16,8},{24,16},{0,24},{9,1},{17,9},{25,17},{1,25},{10,2},{18... | collective-permute-start | bytes 196616 | tf_op jit(solution)/shard_map/ppermute | solution.py:495
  44.4 0.6 copy-start
  44.4 0.7 copy-start.1
  46.9 16.6 %collective-permute-start.12 = (f32[22,8,256]{2,1,0:T(8,128)}, f32[22,8,256]{2,1,0:T(8,128)S(1)}, u32[]{:S(2)}, u32[]{:S(2)}) collective-permute-start(f32[22,8,256]{2,1,0:T(8,128)} %get-tuple-element.25), channel_id=1, source_target_pairs={{0,32},{32,64},{64,96},{96,128},{128,160},{160,192},{192,224},{224... | collective-permute-start | bytes 540680 | tf_op jit(solution)/shard_map/ppermute | solution.py:472
  47.7 8.9 %copy-start.8 = (s32[26,4,4,4]{0,3,2,1:T(4,128)S(1)}, s32[26,4,4,4]{0,3,2,1:T(4,128)}, u32[]{:S(2)}) copy-start(s32[26,4,4,4]{0,3,2,1:T(4,128)} %param.15) | copy-start | bytes 19972
  47.7 15.8 %collective-permute-start.13 = (f32[22,8,256]{2,1,0:T(8,128)}, f32[22,8,256]{2,1,0:T(8,128)S(1)}, u32[]{:S(2)}, u32[]{:S(2)}) collective-permute-start(f32[22,8,256]{2,1,0:T(8,128)} %get-tuple-element.26), channel_id=1, source_target_pairs={{32,0},{64,32},{96,64},{128,96},{160,128},{192,160},{224,192},{0,2... | collective-permute-start | bytes 540680 | tf_op jit(solution)/shard_map/ppermute | solution.py:471
  49.6 10.2 %collective-permute-start.7 = (f32[128,256]{1,0:T(8,128)S(1)}, f32[128,256]{1,0:T(8,128)S(1)}, u32[]{:S(2)}, u32[]{:S(2)}) collective-permute-start(f32[128,256]{1,0:T(8,128)S(1)} %concatenate.37), channel_id=1, source_target_pairs={{1,0},{2,1},{3,2},{4,3},{5,4},{6,5},{7,6},{0,7},{9,8},{10,9},{11,1... | collective-permute-start | bytes 393224 | tf_op jit(solution)/shard_map/ppermute | solution.py:495
  56.5 0.9 copy-start.4
  63.5 0.7 copy-start.2
  64.1 0.7 copy-start.3
where the time goes:
time: 111 us; the launch traced here: 110 us
  Pallas kernels  56 us (50%)
  starting transfers between devices  37.2 us (34%)
  local copies, waits for them, and re-layouts  9.53 us (9%)
  waiting for transfers between devices  7.61 us (7%)
    pallas_call x6, Pallas kernels, call(): pl.pallas_call(body, out_shape=[jax.ShapeDtypeStruct(s, F32) for s in out...  56 us
    ppermute x8, starting transfers between devices, body(): lax.ppermute(gathered, axis, [((i + distance) % n, i) for i in range(n)])  28.6 us
    ppermute x8, waiting for transfers between devices, body(): lax.ppermute(gathered, axis, [((i + distance) % n, i) for i in range(n)])  6.34 us
    ppermute x3, starting transfers between devices, exchanged(): from_above = lax.ppermute(down, axis, [((i + 1) % n, i) for i in range(n)])  5.42 us
    unnamed x18, local copies, waits for them, and re-layouts  3.97 us
    concatenate x5, local copies, waits for them, and re-layouts, body(): gathered = jnp.concatenate([gathered, other], axis=0)  3.78 us
    ppermute x3, starting transfers between devices, exchanged(): from_below = lax.ppermute(above, axis, [(i, (i + 1) % n) for i in range(n)])  3.22 us
  transfers between devices with their start and end apart: 14, of which 6 were waited for; matrix products, arithmetic and copies ran while one was open for 5% of the time, Pallas kernels for 3%

commit v1 on v0

v1 whole, which is shorter than its diff:
```python
import functools

import jax
import jax.numpy as jnp
import ml_dtypes
import numpy as np
from jax import lax
from jax.experimental import pallas as pl
from jax.experimental.pallas import tpu as pltpu
from jax.sharding import PartitionSpec as P

ORDER = 6
SURF = 152
SPAD = 160
WIDE = 256
LEAVES = 4
SLOTS = 64
CLASSES = 343
INNER = 1.05
OUTER = 2.95
SOFTEN = 0.01
HALF = 2.0
BREADTH = 4.0
HIGHEST = lax.Precision.HIGHEST
F32 = jnp.float32
BF16 = jnp.bfloat16
NT = (((1,), (1,)), ((), ()))
RING8 = (-1, 0, 1, 2, 3, -4, -3, -2)
RING4 = (-1, 0, 1, -2)
SELF = (1 * 4 + 1) * 8 + 1


def surface_points():
    points = []
    for i in range(ORDER):
        for j in range(ORDER):
            for k in range(ORDER):
                if min(i, j, k) == 0 or max(i, j, k) == ORDER - 1:
                    points.append((i, j, k))
    return points


def tables():
    points = surface_points()
    spacing = np.linspace(-1.0, 1.0, ORDER)
    g = np.array([[spacing[i] for i in p] for p in points], dtype=np.float32)
    column = np.zeros((3, SPAD, WIDE), np.float32)
    column[:, :SURF, :] = g.T[:, :, None]
    row = np.zeros((8, WIDE), np.float32)
    row[:3, :SURF] = g.T
    tail = np.tile(row[:, 128:160], (1, 4))
    where = {p: n for n, p in enumerate(points)}
    mirror = np.full((8, WIDE), -1, np.int32)
    for h in range(8):
        sign = (h >> 2 & 1, h >> 1 & 1, h & 1)
        for n, p in enumerate(points):
            mirror[h, n] = where[tuple(ORDER - 1 - c if f else c for c, f in zip(p, sign))]
    pick = np.zeros((64 * 8, 384), np.float32)
    for a in range(4):
        for b in range(4):
            for c in range(4):
                if max(a, b, c) < 2:
                    continue
                for h in range(8):
                    d = [-v if f else v for v, f in zip((a, b, c), (h >> 2 & 1, h >> 1 & 1, h & 1))]
                    number = (d[0] + 3) * 49 + (d[1] + 3) * 7 + d[2] + 3
                    pick[(a * 16 + b * 4 + c) * 8 + h, number] = 1.0
    return column, row, tail, mirror, pick.astype(ml_dtypes.bfloat16)


def iota(shape, dim):
    return lax.broadcasted_iota(jnp.int32, shape, dim)


def split2(v):
    hi = v.astype(BF16)
    return hi, (v - hi.astype(F32)).astype(BF16)


def inverse_distance(x, y, z):
    return lax.rsqrt(x * x + y * y + z * z + SOFTEN)


def occupied_row(counts, x, y):
    lane = iota((1, WIDE), 1)
    zone = lane >> 6
    n = jnp.where(
        zone < 2,
        jnp.where(zone == 0, counts[x, y, 0], counts[x, y, 1]),
        jnp.where(zone == 2, counts[x, y, 2], counts[x, y, 3]),
    )
    return ((lane & 63) < n).astype(F32)


def padded_operator(ref, out):
    out[...] = jnp.zeros_like(out)
    out[0:SURF, 0:SURF] = ref[...]


def leaf_squares(column, row, tail, squares):
    segment = (iota((1, 128), 1) >> 5).astype(F32)
    for axis in range(3):
        outer = (OUTER * HALF) * column[axis, :, 0:128]
        inner = (INNER * 0.5) * row[axis : axis + 1, 0:128]
        last = (INNER * 0.5) * tail[axis : axis + 1, :]
        soft = SOFTEN if axis == 2 else 0.0
        for t in range(LEAVES):
            d = outer - ((t - 1.5) + inner)
            squares[axis * LEAVES + t, :, 0:128] = d * d + soft
            if axis < 2:
                d = outer - ((t - 1.5) + last)
                squares[axis * LEAVES + t, :, 128:256] = d * d
            elif t == 0:
                d = outer - ((segment - 1.5) + last)
                squares[axis * LEAVES, :, 128:256] = d * d + soft


def upward_kernel(
    pos, chg, counts, up, column, row, tail,
    below, above,
    terms, operator, squares, acc, leaves,
):
    padded_operator(up, operator)
    leaf_squares(column, row, tail, squares)
    for x in range(4):
        for y in range(4):
            r = x * 4 + y
            q = chg[x, y : y + 1, :] * occupied_row(counts, x, y)
            px, py, pz = (pos[c, x, y : y + 1, :] for c in range(3))
            k = (
                inverse_distance(
                    (OUTER * 0.5) * column[0] - px,
                    (OUTER * 0.5) * column[1] - py,
                    (OUTER * 0.5) * column[2] - pz,
                )
                * q
            )
            hi, lo = split2(k)
            terms[0:SPAD, r * WIDE : (r + 1) * WIDE] = hi
            terms[SPAD : 2 * SPAD, r * WIDE : (r + 1) * WIDE] = lo
            for c, v in enumerate((px, py, pz, q)):
                below[16 + r, c : c + 1, :] = v[:, 0:128]
                above[16 + r, c : c + 1, :] = v[:, 128:256]
    gather = ((iota((16 * WIDE, 128), 0) >> 6) == iota((16 * WIDE, 128), 1)).astype(F32).astype(BF16)
    both = jnp.dot(terms[...], gather, preferred_element_type=F32)
    check = both[0:SPAD] + both[SPAD : 2 * SPAD]
    check = jnp.concatenate([check, jnp.zeros((WIDE - SPAD, 128), F32)], axis=0).T[0:64, :]
    up_eq = lax.dot_general(check, operator[...], NT, precision=HIGHEST, preferred_element_type=F32)
    low = up_eq.astype(BF16).astype(F32)
    for r in range(16):
        for out, at in ((below, 0), (above, 2)):
            pair = low[r * 4 + at : r * 4 + at + 2]
            out[r, 0:2, :] = pair[:, 0:128]
            out[r, 2:4, :] = pair[:, 128:256]
    leaves[0] = up_eq[:, 128:256]
    lines = leaves.at[0][pl.ds(0, 16, stride=4), :]
    for z in range(1, 4):
        lines = lines + pltpu.roll(leaves.at[0][pl.ds(z, 16, stride=4), :], 32 * z, 1)
    acc[...] = jnp.zeros_like(acc)
    for part in range(4):
        rows = slice(part * 40, part * 40 + 40)
        first, last = jnp.zeros((40, 128), F32), jnp.zeros((40, 128), F32)
        for x in range(4):
            for y in range(4):
                xy = squares[x, rows, 0:128] + squares[4 + y, rows, 0:128]
                for z in range(4):
                    t = x * 16 + y * 4 + z
                    first = first + lax.rsqrt(xy + squares[8 + z, rows, 0:128]) * up_eq[t : t + 1, 0:128]
                xy = squares[x, rows, 128:256] + squares[4 + y, rows, 128:256]
                r = x * 4 + y
                last = last + lax.rsqrt(xy + squares[8, rows, 128:256]) * lines[r : r + 1, :]
        acc[rows, 0:128] = first
        acc[rows, 128:256] = last
    ones = jnp.ones((8, WIDE), F32)
    summed = lax.dot_general(ones, acc[...], NT, precision=HIGHEST, preferred_element_type=F32)
    block = BREADTH * lax.dot_general(summed, operator[...], NT, precision=HIGHEST, preferred_element_type=F32)
    for out in (below, above):
        out[32, 0:1, :] = block[0:1, 0:128]
        out[32, 1:2, :] = block[0:1, 128:256]
        out[32, 2:4, :] = jnp.zeros((2, 128), F32)


def eq_record(refs, x, y, s):
    own, ylo, yhi, xlo, xhi = refs
    if x < 2:
        return xlo[(s * 2 + x) * 8 + y]
    if x > 5:
        return xhi[(s * 2 + x - 6) * 8 + y]
    if y < 2:
        return ylo[s * 8 + (x - 2) * 2 + y]
    if y > 5:
        return yhi[s * 8 + (x - 2) * 2 + y - 6]
    return own[s][(x - 2) * 4 + y - 2]


def particle_record(refs, x, y, s):
    own, ylo, yhi, xlo, xhi = refs
    if x < 0:
        return xlo[64 + s * 6 + y + 1]
    if x > 3:
        return xhi[64 + s * 6 + y + 1]
    if y < 0:
        return ylo[32 + s * 4 + x]
    if y > 3:
        return yhi[32 + s * 4 + x]
    return own[s][16 + x * 4 + y]


def far_groups():
    groups = {}
    for a in range(4):
        for b in range(4):
            for c in range(4):
                if max(a, b, c) >= 2:
                    key = tuple(v in (1, 2) for v in (a, b, c))
                    groups.setdefault(key, []).append((a, b, c))
    return groups


def far_kernel(
    z0, z1, z2, z3, ylo, yhi, xlo, xhi, flags, pick, mirror, column, row,
    out, halo, low, turned, framed, chosen, squares, stacked, matrices, total,
):
    refs = ((z0, z1, z2, z3), ylo, yhi, xlo, xhi)
    for x in range(8):
        for y in range(8):
            for pair in range(4):
                record = eq_record(refs, x, y, pair)
                at = (x * 8 + y) * 8 + pair * 2
                halo[0, at : at + 2, :] = record[0:2]
                halo[1, at : at + 2, :] = record[2:4]
    for half in range(2):
        low[:, half * 128 : half * 128 + 128] = halo[half].astype(BF16)
    turn = ((iota((WIDE, WIDE), 0) ^ 7) == iota((WIDE, WIDE), 1)).astype(F32).astype(BF16)
    for n in range(2):
        part = slice(n * WIDE, n * WIDE + WIDE)
        turned[part, :] = jnp.dot(turn, low[part, :], preferred_element_type=F32).astype(BF16)

    def permutation(h):
        return (iota((WIDE, WIDE), 0) == mirror[h : h + 1, :]).astype(F32).astype(BF16)

    for h in range(8):
        source = turned if h & 1 else low
        frame = jnp.dot(source[...], permutation(h), preferred_element_type=F32)
        for x in range(8):
            for y in range(8):
                xf, yf = (7 - x if h & 4 else x), (7 - y if h & 2 else y)
                at = (x * 8 + y) * 8
                for n in range(2):
                    framed.at[n][pl.ds((xf * 8 + yf) * 64 + h, 8, stride=8), :] = frame[
                        at : at + 8, n * 128 : n * 128 + 128
                    ]
    picked = jnp.dot(pick[...], flags[...], preferred_element_type=F32)
    which = iota((512, 128), 0) & 7
    for h in range(8):
        mask = (48 if h & 4 else 0) + (12 if h & 2 else 0) + (3 if h & 1 else 0)
        turn = ((iota((128, 128), 0) ^ mask) == iota((128, 128), 1)).astype(F32).astype(BF16)
        part = jnp.dot(jnp.where(which == h, picked, 0.0).astype(BF16), turn, preferred_element_type=F32)
        chosen[...] = part if h == 0 else chosen[...] + part
    for axis in range(3):
        for d in range(4):
            v = (INNER * 0.5) * row[axis : axis + 1, :] - d - (INNER * 0.5) * column[axis]
            squares[axis * 4 + d] = v * v + (SOFTEN if axis == 2 else 0.0)
    matrices[...] = jnp.zeros_like(matrices)
    total[...] = jnp.zeros_like(total)
    for key, members in far_groups().items():
        ranges = [range(4) if every else (0, 2) for every in key]
        leaves = [(x, y, z) for x in ranges[0] for y in ranges[1] for z in ranges[2]]
        for n, (a, b, c) in enumerate(members):
            m = lax.rsqrt(squares[a] + squares[4 + b] + squares[8 + c])
            matrices[n * WIDE : n * WIDE + SPAD, :] = m.astype(BF16)
            flag = chosen[(a * 16 + b * 4 + c) * 8 : (a * 16 + b * 4 + c) * 8 + 8, :]
            for i in range(0, len(leaves), 2):
                tiles = []
                for x, y, z in leaves[i : i + 2]:
                    at = (((x + 2 + a) * 8 + y + 2 + b) * 8 + z + 2 + c) * 8
                    leaf = x * 16 + y * 4 + z
                    keep = jnp.broadcast_to(flag[:, leaf : leaf + 1], (8, 128))
                    tiles.append([framed[half, at : at + 8, :] * keep for half in range(2)])
                for half in range(2):
                    lanes = slice(n * WIDE + half * 128, n * WIDE + half * 128 + 128)
                    stacked[i * 8 : i * 8 + 16, lanes] = jnp.concatenate([t[half] for t in tiles], axis=0).astype(BF16)
        rows, depth = len(leaves) * 8, len(members) * WIDE
        product = jnp.dot(stacked[0:rows, 0:depth], matrices[0:depth, :], preferred_element_type=F32)
        for i, (x, y, z) in enumerate(leaves):
            leaf = x * 16 + y * 4 + z
            for half in range(2):
                total[half, leaf * 8 : leaf * 8 + 8, :] += product[i * 8 : i * 8 + 8, half * 128 : half * 128 + 128]
    result = jnp.zeros((64, WIDE), F32)
    for h in range(8):
        parts = [total.at[half][pl.ds(h, 64, stride=8), :] for half in range(2)]
        hi, lo = split2(jnp.concatenate(parts, axis=1))
        both = jnp.dot(jnp.concatenate([hi, lo], axis=0), permutation(h), preferred_element_type=F32).astype(BF16)
        mask = (48 if h & 4 else 0) + (12 if h & 2 else 0) + (3 if h & 1 else 0)
        turn = ((iota((64, 128), 0) ^ mask) == (iota((64, 128), 1) & 63)).astype(F32).astype(BF16)
        result = result + jnp.dot(turn, both, preferred_element_type=F32)
    out[...] = result


def near_kernel(
    first_row, rows_here, z0, z1, z2, z3, ylo, yhi, xlo, xhi, flags,
    out, lines, sources, points, listed, shifted, sums,
):
    refs = ((z0, z1, z2, z3), ylo, yhi, xlo, xhi)
    for x in range(6):
        for y in range(6):
            for pair in range(4):
                record = particle_record(refs, x - 1, y - 1, pair)
                for c in range(4):
                    lines[c, x * 6 + y : x * 6 + y + 1, pair * 128 : pair * 128 + 128] = record[c : c + 1]
    for c in range(4):
        whole = lines[c]
        half_turn = pltpu.roll(whole, 64, 1)
        for e, (line, at) in enumerate(((half_turn, 128), (whole, 128), (half_turn, 256))):
            if c == 2:
                line = line + float(e - 1)
            for half in range(2):
                sources.at[c, half][pl.ds(e, 40, stride=3), :] = line[:, at + half * 128 : at + half * 128 + 128]
    same = (iota((64, WIDE), 1) & 63) == iota((64, WIDE), 0)
    block = ((iota((WIDE, WIDE), 0) >> 6) == (iota((WIDE, WIDE), 1) >> 6)).astype(F32).astype(BF16)
    zone = iota((32, WIDE), 1) >> 6
    step_y = (iota((9, WIDE), 0) // 3 - 1).astype(F32)

    def one_row(i, carry):
        r = i + first_row
        x, y = r >> 2, r & 3
        pieces = []
        for c in range(3):
            v = jnp.concatenate([z1[16 + r, c : c + 1, :], z2[16 + r, c : c + 1, :]], axis=1)
            for _ in range(3):
                b = v.astype(BF16).astype(F32)
                pieces.append(jnp.where(same, b, 0.0).astype(BF16))
                v = v - b
        spread = jnp.dot(jnp.concatenate(pieces, axis=0), block, preferred_element_type=F32)
        square = jnp.full((64, WIDE), SOFTEN, F32)
        for c in range(3):
            at = c * 192
            v = spread[at : at + 64] + spread[at + 64 : at + 128] + spread[at + 128 : at + 192]
            square = square + v * v
            points[c] = -2.0 * v
        points[3] = square
        f = flags[x, y]
        lists = jnp.zeros((32, WIDE), F32)
        for z in range(4):
            lists = jnp.where(zone == z, f[:, z : z + 1], lists)
        listed[...] = lists
        for ex in range(3):
            at = ((x + ex) * 6 + y) * 3
            sx, sy, sz, q = (
                jnp.concatenate([sources.at[c, half][pl.ds(at, 9), :] for half in range(2)], axis=1) for c in range(4)
            )
            sx = sx + float(ex - 1)
            sy = sy + step_y
            shifted[0, ex * 9 : ex * 9 + 9, :] = sx
            shifted[1, ex * 9 : ex * 9 + 9, :] = sy
            shifted[2, ex * 9 : ex * 9 + 9, :] = sz
            shifted[3, ex * 9 : ex * 9 + 9, :] = sx * sx + sy * sy + sz * sz
            shifted[4, ex * 9 : ex * 9 + 9, :] = q * listed[ex * 9 : ex * 9 + 9, :]
        for part in range(2):
            for half in range(2):
                lanes = slice(half * 128, half * 128 + 128)
                rows = slice(part * 32, part * 32 + 32)
                tx, ty, tz, tt = (points[c, rows, lanes] for c in range(4))
                acc = jnp.zeros((32, 128), F32)
                for n in range(27):
                    sx, sy, sz, ss, q = (shifted[c, n : n + 1, lanes] for c in range(5))
                    k = lax.rsqrt((tt + ss) + tx * sx + ty * sy + tz * sz)
                    if n == 13:
                        k = jnp.where(same[rows, lanes], 0.0, k)
                    acc = acc + k * q
                sums[rows, lanes] = acc
        hi, lo = split2(sums[...])
        both = jnp.dot(jnp.concatenate([hi, lo], axis=0), block, preferred_element_type=F32)
        picked = jnp.where(same, both[0:64] + both[64:128], 0.0)
        out[pl.ds(i, 1), :] = jnp.sum(picked, axis=0, keepdims=True)
        return carry

    lax.fori_loop(0, rows_here, one_row, 0)


def last_kernel(
    counts, gathered, far, near0, near1, pos, down, column, row, tail,
    out, operator, squares, offsets, tails, acc, checks, ends,
):
    padded_operator(down, operator)
    segment = iota((1, 128), 1) >> 5
    at = 0
    for axis, ring in enumerate((RING8, RING4, RING8)):
        outer = (INNER * HALF) * column[axis, :, 0:128]
        base = outer - (INNER * HALF) * row[axis : axis + 1, 0:128]
        end = outer - (INNER * HALF) * tail[axis : axis + 1, :]
        soft = SOFTEN if axis == 2 else 0.0
        for i, delta in enumerate(ring):
            v = base - float(delta * 4)
            offsets[at + i] = v * v + soft
            if axis < 2:
                v = end - float(delta * 4)
                tails[at + i] = v * v
            elif i % 4 == 0:
                d = ring[i : i + 4]
                shift = jnp.where(
                    segment < 2, jnp.where(segment == 0, d[0], d[1]), jnp.where(segment == 2, d[2], d[3])
                ).astype(F32)
                v = end - 4.0 * shift
                tails[at + i // 4] = v * v + soft
        at += len(ring)
    acc[...] = jnp.zeros_like(acc)

    def pair(i, carry):
        x, y = i >> 2, i & 3
        lines, ends = [], [jnp.zeros((1, 128), F32)] * 2
        for z in range(8):
            m = i * 8 + z
            both = gathered[m] * jnp.where(m == SELF, 0.0, 1.0)
            lines.append(both[0:1])
            end = both[1:2]
            ends[z // 4] = ends[z // 4] + (pltpu.roll(end, 32 * (z % 4), 1) if z % 4 else end)
        for part in range(4):
            rows = slice(part * 40, part * 40 + 40)
            xy = offsets[x, rows, :] + offsets[8 + y, rows, :]
            total = acc[rows, 0:128]
            for z in range(8):
                total = total + lax.rsqrt(xy + offsets[12 + z, rows, :]) * lines[z]
            acc[rows, 0:128] = total
            xy = tails[x, rows, :] + tails[8 + y, rows, :]
            total = acc[rows, 128:256]
            for z in range(2):
                total = total + lax.rsqrt(xy + tails[12 + z, rows, :]) * ends[z]
            acc[rows, 128:256] = total
        return carry

    lax.fori_loop(0, 32, pair, 0)
    ones = jnp.ones((WIDE, WIDE), F32)
    summed = jnp.dot(acc[...], ones, precision=HIGHEST, preferred_element_type=F32)
    local = BREADTH * jnp.dot(operator[...], summed, precision=HIGHEST, preferred_element_type=F32)
    leaf_squares(column, row, tail, squares)
    checks[...] = jnp.zeros_like(checks)
    for x in range(4):
        for y in range(4):
            lines = [jnp.zeros((8, 128), F32)] * 5
            for part in range(4):
                rows = slice(part * 40, part * 40 + 40)
                weight = local[rows, 0:128]
                for z in range(5):
                    lanes = slice(0, 128) if z < 4 else slice(128, 256)
                    xy = squares[x, rows, lanes] + squares[4 + y, rows, lanes]
                    v = lax.rsqrt(xy + squares[8 + z % 4, rows, lanes]) * weight
                    for s in range(5):
                        lines[z] = lines[z] + v[s * 8 : s * 8 + 8]
            for z in range(4):
                t = x * 16 + y * 4 + z
                checks[0, t : t + 1, :] = jnp.sum(lines[z], axis=0, keepdims=True)
            r = x * 4 + y
            ends[r : r + 1, :] = jnp.sum(lines[4], axis=0, keepdims=True)
    used = iota((16, 128), 1) < SURF - 128
    for z in range(4):
        part = pltpu.roll(ends[...], 128 - 32 * z, 1) if z else ends[...]
        checks.at[1][pl.ds(z, 16, stride=4), :] = jnp.where(used, part, 0.0)
    both = jnp.concatenate([checks[0], checks[1]], axis=1)
    both = both + jnp.concatenate([far[...], jnp.zeros((64, WIDE), F32)], axis=0)
    local = jnp.dot(operator[...], both.T, precision=HIGHEST, preferred_element_type=F32)
    hi, lo = split2(local[0:SPAD])
    both = jnp.concatenate([hi, lo], axis=0)
    for x in range(4):
        for y in range(4):
            r = x * 4 + y
            spread = (iota((128, WIDE), 0) == r * 4 + (iota((128, WIDE), 1) >> 6)).astype(F32).astype(BF16)
            wide = jnp.dot(both, spread, preferred_element_type=F32)
            px, py, pz = (pos[c, x, y : y + 1, :] for c in range(3))
            k = inverse_distance(
                (OUTER * 0.5) * column[0] - px,
                (OUTER * 0.5) * column[1] - py,
                (OUTER * 0.5) * column[2] - pz,
            )
            line = jnp.sum(k * (wide[0:SPAD] + wide[SPAD : 2 * SPAD]), axis=0, keepdims=True)
            near = near0 if r < 8 else near1
            out[x, y : y + 1, :] = occupied_row(counts, x, y) * (line + near[r % 8 : r % 8 + 1, :])


def call(body, outs, scratch, memory, name, work, *args):
    spaces = {"v": pltpu.VMEM, "s": pltpu.SMEM}
    return pl.pallas_call(
        body,
        out_shape=[jax.ShapeDtypeStruct(s, F32) for s in outs],
        in_specs=[pl.BlockSpec(memory_space=spaces[m]) for m in memory],
        out_specs=[pl.BlockSpec(memory_space=pltpu.VMEM) for _ in outs],
        scratch_shapes=[pltpu.VMEM(s, d) for s, d in scratch],
        compiler_params=pltpu.CompilerParams(vmem_limit_bytes=40 << 20),
        cost_estimate=pl.CostEstimate(flops=work * 1000000, transcendentals=0, bytes_accessed=1 << 20),
        name=name,
    )(*args)


def shifted(array, axis, distance):
    n = lax.axis_size(axis)
    return lax.ppermute(array, axis, [((i + distance) % n, i) for i in range(n)])


def body(positions, charges, counts, near_flags, far_flags, up_operator, down_operator):
    column, row, tail, mirror, pick = (jnp.asarray(t) for t in tables())
    below, above = call(
        upward_kernel,
        [(33, 4, 128), (33, 4, 128)],
        [
            ((2 * SPAD, 16 * WIDE), BF16), ((WIDE, WIDE), F32), ((12, SPAD, WIDE), F32),
            ((WIDE, WIDE), F32), ((1, 64, 128), F32),
        ],
        "vvsvvvv", "upward", 6000, positions, charges, counts, up_operator, column, row, tail,
    )
    own = (shifted(above, "gz", -1), below, above, shifted(below, "gz", 1))

    grid = [[v[k * 16 : k * 16 + 16].reshape(4, 4, 4, 128) for v in own] for k in range(2)]
    blocks = [own[n][32:33] for n in (0, 1, 3)]

    def to_y(low, one):
        parts = [v[:, low : low + 2].reshape(8, 4, 128) for v in grid[0]]
        parts += [v[:, one].reshape(4, 4, 128) for v in grid[1]]
        return jnp.concatenate(parts + blocks, axis=0)

    ylo = shifted(to_y(2, 3), "gy", -1)
    yhi = shifted(to_y(0, 0), "gy", 1)
    blocks = jnp.concatenate([ylo[48:51]] + blocks + [yhi[48:51]], axis=0)

    def to_x(low, one):
        parts = []
        for s in range(4):
            sides = [v[s * 8 : s * 8 + 8].reshape(4, 2, 4, 128)[low : low + 2] for v in (ylo, yhi)]
            parts.append(jnp.concatenate([sides[0], grid[0][s][low : low + 2], sides[1]], axis=1).reshape(16, 4, 128))
        for s in range(4):
            at = 32 + s * 4 + one
            parts += [ylo[at : at + 1], grid[1][s][one], yhi[at : at + 1]]
        return jnp.concatenate(parts + [blocks], axis=0)

    xlo = shifted(to_x(2, 3), "gx", -1)
    xhi = shifted(to_x(0, 0), "gx", 1)
    halo = (*own, ylo, yhi, xlo, xhi)

    held = jnp.concatenate([xlo[88:97], blocks, xhi[88:97]], axis=0)[:, 0:2]
    held = jnp.concatenate([held, shifted(held, "gx", 3), shifted(held[9:27], "gx", -3)], axis=0)
    held = held.reshape(8, 3, 3, 2, 128)
    held = jnp.concatenate([held, shifted(held[:, 1], "gy", 2)[:, None]], axis=1)
    forward, back = shifted(held, "gz", 3), shifted(held[:, :, 1:3], "gz", -3)
    gathered = jnp.concatenate([held, forward, back], axis=2).reshape(256, 2, 128)

    flags = jnp.pad(far_flags.reshape(CLASSES, 64).astype(BF16), ((0, 384 - CLASSES), (0, 64)))
    (far,) = call(
        far_kernel,
        [(64, WIDE)],
        [
            ((2, 512, 128), F32),
            ((512, WIDE), BF16), ((512, WIDE), BF16), ((2, 4096, 128), F32), ((512, 128), F32),
            ((12, SPAD, WIDE), F32), ((512, 8 * WIDE), BF16), ((8 * WIDE, WIDE), BF16), ((2, 512, 128), F32),
        ],
        "v" * 13, "far", 7000, *halo, flags, pick, mirror, column, row,
    )
    near_flags = near_flags.astype(F32)
    centre = jnp.ones((1, *near_flags.shape[1:]), F32)
    listed = jnp.concatenate([near_flags[0:13], centre, near_flags[13:26], jnp.zeros((5, *near_flags.shape[1:]), F32)], axis=0)
    listed = listed.transpose(1, 2, 0, 3)
    near = []
    for n in range(2):
        near += call(
            functools.partial(near_kernel, 8 * n, 8),
            [(8, WIDE)],
            [
                ((4, 40, 512), F32), ((4, 2, 120, 128), F32), ((4, 64, WIDE), F32), ((32, WIDE), F32),
                ((5, 32, WIDE), F32), ((64, WIDE), F32),
            ],
            "v" * 9, "near", 6000, *halo, listed,
        )
    (potential,) = call(
        last_kernel,
        [(4, 4, WIDE)],
        [
            ((WIDE, WIDE), F32), ((12, SPAD, WIDE), F32), ((20, SPAD, 128), F32), ((14, SPAD, 128), F32),
            ((WIDE, WIDE), F32), ((2, 128, 128), F32), ((16, 128), F32),
        ],
        "svvvvvvvvv", "last", 9000, counts, gathered, far, near[0], near[1], positions, down_operator, column, row, tail,
    )
    return potential


def solution(mesh):
    return jax.shard_map(
        body,
        mesh=mesh,
        in_specs=(
            P(None, "gx", "gy", "gz"),
            P("gx", "gy", "gz"),
            P("gx", "gy", "gz"),
            P(None, "gx", "gy", "gz"),
            P(None, "gx", "gy", "gz"),
            P(),
            P(),
        ),
        out_specs=P("gx", "gy", "gz"),
        check_vma=False,
    )
```

time: 111 us -> 88.2 us (0.79)
  Pallas kernels: 56 us -> 40.5 us
  starting transfers between devices: 37.2 us -> 22.9 us
  waiting for transfers between devices: 7.61 us -> 15.9 us
  local copies, waits for them, and re-layouts: 9.53 us -> 7.49 us
    pallas_call x6 -> x5, Pallas kernels: 56 us -> 40.5 us  [call(): pl.pallas_call(body, out_shape=[jax.ShapeDtypeStruct(s, F32) for s in out...]
    ppermute x14 -> x11, starting transfers between devices: 37.2 us -> 22.9 us  [shifted(): lax.ppermute(array, axis, [((i + distance) % n, i) for i in range(n)])]
    ppermute x14 -> x11, waiting for transfers between devices: 7.61 us -> 15.9 us  [shifted(): lax.ppermute(array, axis, [((i + distance) % n, i) for i in range(n)])]
    concatenate x5 -> x6, local copies, waits for them, and re-layouts: 3.78 us -> 0.36 us  [the longest x3 0.33 us: body(): jnp.concatenate([near_flags[0:13], centre, near_flags[13:26], jnp.zeros((...]
    unnamed x18 -> x74, local copies, waits for them, and re-layouts: 3.97 us -> 6.77 us
  transfers between devices with their start and end apart: 14 -> 11, of which waited for: 6 -> 4; matrix products, arithmetic and copies ran while one was open for 5% -> 1% of each run, Pallas kernels for 3% -> 28%
where the time goes in v1:
time: 88.2 us; the launch traced here: 87.8 us
  Pallas kernels  40.5 us (46%)
  starting transfers between devices  22.9 us (26%)
  waiting for transfers between devices  15.9 us (18%)
  local copies, waits for them, and re-layouts  7.49 us (8%)
    pallas_call x5, Pallas kernels, call(): pl.pallas_call(body, out_shape=[jax.ShapeDtypeStruct(s, F32) for s in out...  40.5 us
    ppermute x11, starting transfers between devices, shifted(): lax.ppermute(array, axis, [((i + distance) % n, i) for i in range(n)])  22.9 us
    ppermute x11, waiting for transfers between devices, shifted(): lax.ppermute(array, axis, [((i + distance) % n, i) for i in range(n)])  15.9 us
    unnamed x74, local copies, waits for them, and re-layouts  6.77 us
  transfers between devices with their start and end apart: 11, of which 4 were waited for; matrix products, arithmetic and copies ran while one was open for 1% of the time, Pallas kernels for 28%

profile of v1, /device:TPU:1, one launch (start us, length us, event | category | flops | bytes accessed | tf_op | source)
XLA Modules:
  0.0 87.8 jit_solution(1171211616601045270)
XLA Ops:
  0.0 0.0 copy-start.10
  0.0 0.0 copy-start.12
  0.0 0.7 copy-done.10
  0.7 0.0 copy-done.12
  0.7 0.0 copy-start
  0.7 0.9 %copy-done = f32[152,152]{1,0:T(8,128)S(1)} copy-done((f32[152,152]{1,0:T(8,128)S(1)}, f32[152,152]{1,0:T(8,128)}, u32[]{:S(2)}) %copy-start) | copy-done | bytes 92440
  1.6 0.0 copy-start.2
  1.6 0.8 copy-done.2
  2.4 0.0 copy-start.4
  2.4 0.7 copy-done.4
  3.1 0.0 copy-start.5
  3.1 0.7 copy-done.5
  3.8 0.0 copy-start.7
  3.8 1.0 %copy-done.7 = f32[3,160,256]{2,1,0:T(8,128)S(1)} copy-done((f32[3,160,256]{2,1,0:T(8,128)S(1)}, f32[3,160,256]{2,1,0:T(8,128)}, u32[]{:S(2)}) %copy-start.7) | copy-done | bytes 491544
  4.9 5.1 %upward.1 = (f32[33,4,128]{2,1,0:T(4,128)S(1)}, f32[33,4,128]{2,1,0:T(4,128)S(1)}) custom-call(f32[3,4,4,256]{3,2,1,0:T(4,128)S(1)} %copy-done.2, f32[4,4,256]{2,1,0:T(4,128)S(1)} %copy-done.4, s32[4,4,4]{2,1,0:T(4,128)S(1)} %copy-done.5, f32[152,152]{1,0:T(8,128)S(1)} %copy-done, f32[3,160,256]{2,1,0:T(8,128)S(1)} %copy-done.7, f32[8,256]{1,0:T(8,128)S(1)} %copy-done.10, ...), custom_call_target="tpu_custom_call" | custom-call | flops 6000000000 | bytes 1048576 | tf_op jit(solution)/shard_map/upward/pallas_call | solution.py:482
  9.9 2.7 %collective-permute-start = (f32[33,4,128]{2,1,0:T(4,128)S(1)}, f32[33,4,128]{2,1,0:T(4,128)S(1)}, u32[]{:S(2)}, u32[]{:S(2)}) collective-permute-start(f32[33,4,128]{2,1,0:T(4,128)S(1)} %get-tuple-element.7.z2), channel_id=1, source_target_pairs={{7,0},{0,1},{1,2},{2,3},{3,4},{4,5},{5,6},{6,7},{15,8},{8,9},{9,10... | collective-permute-start | bytes 202760 | tf_op jit(solution)/shard_map/ppermute | solution.py:496
  12.6 0.6 collective-permute-start.1
  13.2 0.0 copy-start.14
  13.3 0.7 copy-done.14
  14.0 0.1 pad.8.clone
  14.1 0.1 pad.6.clone
  14.2 0.0 collective-permute-done.z0
  14.2 2.2 %collective-permute-done.1.z3 = f32[33,4,128]{2,1,0:T(4,128)S(1)} collective-permute-done((f32[33,4,128]{2,1,0:T(4,128)S(1)}, f32[33,4,128]{2,1,0:T(4,128)S(1)}, u32[]{:S(2)}, u32[]{:S(2)}) %collective-permute-start.1) | collective-permute-done | bytes 67616 | tf_op jit(solution)/shard_map/ppermute | solution.py:496
  16.6 1.3 %collective-permute-start.2 = (f32[51,4,128]{2,1,0:T(4,128)S(1)}, f32[51,4,128]{2,1,0:T(4,128)S(1)}, u32[]{:S(2)}, u32[]{:S(2)}) collective-permute-start(f32[51,4,128]{2,1,0:T(4,128)S(1)} %get-tuple-element.75), channel_id=1, source_target_pairs={{24,0},{0,8},{8,16},{16,24},{25,1},{1,9},{9,17},{17,25},{26,2},{2,... | collective-permute-start | bytes 313352 | tf_op jit(solution)/shard_map/ppermute | solution.py:496
  17.9 1.5 %collective-permute-start.3 = (f32[51,4,128]{2,1,0:T(4,128)S(1)}, f32[51,4,128]{2,1,0:T(4,128)S(1)}, u32[]{:S(2)}, u32[]{:S(2)}) collective-permute-start(f32[51,4,128]{2,1,0:T(4,128)S(1)} %get-tuple-element.74), channel_id=1, source_target_pairs={{8,0},{16,8},{24,16},{0,24},{9,1},{17,9},{25,17},{1,25},{10,2},{18... | collective-permute-start | bytes 313352 | tf_op jit(solution)/shard_map/ppermute | solution.py:496
  19.3 2.1 %collective-permute-done.2.ylo = f32[51,4,128]{2,1,0:T(4,128)S(1)} collective-permute-done((f32[51,4,128]{2,1,0:T(4,128)S(1)}, f32[51,4,128]{2,1,0:T(4,128)S(1)}, u32[]{:S(2)}, u32[]{:S(2)}) %collective-permute-start.2) | collective-permute-done | bytes 104480 | tf_op jit(solution)/shard_map/ppermute | solution.py:496
  21.4 0.0 collective-permute-done.3.yhi
  21.9 2.7 %collective-permute-start.4 = (f32[97,4,128]{2,1,0:T(4,128)S(1)}, f32[97,4,128]{2,1,0:T(4,128)S(1)}, u32[]{:S(2)}, u32[]{:S(2)}) collective-permute-start(f32[97,4,128]{2,1,0:T(4,128)S(1)} %constant_dynamic-update-slice_fusion.22), channel_id=1, source_target_pairs={{224,0},{0,32},{32,64},{64,96},{96,128},{128,160},{160,192},{192,2... | collective-permute-start | bytes 595976 | tf_op jit(solution)/shard_map/ppermute | solution.py:496
  24.6 0.0 copy-start.13
  24.6 0.1 fusion.11
  24.7 8.3 %collective-permute-done.4.xlo = f32[97,4,128]{2,1,0:T(4,128)S(1)} collective-permute-done((f32[97,4,128]{2,1,0:T(4,128)S(1)}, f32[97,4,128]{2,1,0:T(4,128)S(1)}, u32[]{:S(2)}, u32[]{:S(2)}) %collective-permute-start.4) | collective-permute-done | bytes 198688 | tf_op jit(solution)/shard_map/ppermute | solution.py:496
  33.1 1.2 %collective-permute-start.5 = (f32[97,4,128]{2,1,0:T(4,128)S(1)}, f32[97,4,128]{2,1,0:T(4,128)S(1)}, u32[]{:S(2)}, u32[]{:S(2)}) collective-permute-start(f32[97,4,128]{2,1,0:T(4,128)S(1)} %get-tuple-element.12), channel_id=1, source_target_pairs={{32,0},{64,32},{96,64},{128,96},{160,128},{192,160},{224,192},{0,2... | collective-permute-start | bytes 595976 | tf_op jit(solution)/shard_map/ppermute | solution.py:496
  34.3 0.1 maximum_maximum_fusion
  34.4 0.0 copy-start.8
  34.4 0.2 copy.45
  34.6 0.0 copy-done.13
  34.6 0.0 copy-start.9
  34.6 0.1 copy.44
  34.8 3.4 %collective-permute-done.5.xhi = f32[97,4,128]{2,1,0:T(4,128)S(1)} collective-permute-done((f32[97,4,128]{2,1,0:T(4,128)S(1)}, f32[97,4,128]{2,1,0:T(4,128)S(1)}, u32[]{:S(2)}, u32[]{:S(2)}) %collective-permute-start.5) | collective-permute-done | bytes 198688 | tf_op jit(solution)/shard_map/ppermute | solution.py:496
  38.2 1.7 %collective-permute-start.6 = (f32[27,2,128]{2,1,0:T(2,128)S(1)}, f32[27,2,128]{2,1,0:T(2,128)S(1)}, u32[]{:S(2)}, u32[]{:S(2)}) collective-permute-start(f32[27,2,128]{2,1,0:T(2,128)S(1)} %slice.560), channel_id=1, source_target_pairs={{96,0},{128,32},{160,64},{192,96},{224,128},{0,160},{32,192},{64,2... | collective-permute-start | bytes 82952 | tf_op jit(solution)/shard_map/ppermute | solution.py:496
  39.9 0.0 copy-start.11
  39.9 1.9 %collective-permute-start.7 = (f32[18,2,128]{2,1,0:T(2,128)S(1)}, f32[18,2,128]{2,1,0:T(2,128)S(1)}, u32[]{:S(2)}, u32[]{:S(2)}) collective-permute-start(f32[18,2,128]{2,1,0:T(2,128)S(1)} %slice.561), channel_id=1, source_target_pairs={{160,0},{192,32},{224,64},{0,96},{32,128},{64,160},{96,192},{128,2... | collective-permute-start | bytes 55304 | tf_op jit(solution)/shard_map/ppermute | solution.py:496
  41.8 0.0 copy-done.8
  41.8 0.0 copy-done.9
  41.8 0.0 copy-done.11
  41.8 6.2 %far.1 = f32[64,256]{1,0:T(8,128)S(1)} custom-call(f32[33,4,128]{2,1,0:T(4,128)S(1)} %collective-permute-done.z0, f32[33,4,128]{2,1,0:T(4,128)S(1)} %get-tuple-element.8.z1, f32[33,4,128]{2,1,0:T(4,128)S(1)} %get-tuple-element.7.z2, f32[33,4,128]{2,1,0:T(4,128)S(1)} %collective-permute-done.1.z3, f32[51,4,128]{2,1,0:T(4,128)S(1)} %collective-permute-done.2.ylo, ...), custom_call_target="tpu_custom_call" | custom-call | flops 7000000000 | bytes 1048576 | tf_op jit(solution)/shard_map/far/pallas_call | solution.py:482
  48.1 0.0 collective-permute-done.7
  48.1 0.0 collective-permute-done.6
  48.1 1.3 %collective-permute-start.8 = (f32[8,3,2,128]{3,2,1,0:T(2,128)S(1)}, f32[8,3,2,128]{3,2,1,0:T(2,128)S(1)}, u32[]{:S(2)}, u32[]{:S(2)}) collective-permute-start(f32[8,3,2,128]{3,2,1,0:T(2,128)S(1)} %slice_bitcast_fusion), channel_id=1, source_target_pairs={{16,0},{24,8},{0,16},{8,24},{17,1},{25,9},{1,17},{9,25},{18,2},{26... | collective-permute-start | bytes 73736 | tf_op jit(solution)/shard_map/ppermute | solution.py:496
  49.5 9.3 %near.3.near1 = f32[8,256]{1,0:T(8,128)S(1)} custom-call(f32[33,4,128]{2,1,0:T(4,128)S(1)} %collective-permute-done.z0, f32[33,4,128]{2,1,0:T(4,128)S(1)} %get-tuple-element.8.z1, f32[33,4,128]{2,1,0:T(4,128)S(1)} %get-tuple-element.7.z2, f32[33,4,128]{2,1,0:T(4,128)S(1)} %collective-permute-done.1.z3, f32[51,4,128]{2,1,0:T(4,128)S(1)} %collective-permute-done.2.ylo, ...), custom_call_target="tpu_custom_call" | custom-call | flops 6000000000 | bytes 1048576 | tf_op jit(solution)/shard_map/near/pallas_call | solution.py:482
  58.8 0.0 collective-permute-done.8
  58.9 7.4 %collective-permute-start.9 = (f32[8,4,3,2,128]{4,3,2,1,0:T(2,128)S(1)}, f32[8,4,3,2,128]{4,3,2,1,0:T(2,128)S(1)}, u32[]{:S(2)}, u32[]{:S(2)}) collective-permute-start(f32[8,4,3,2,128]{4,3,2,1,0:T(2,128)S(1)} %pad_maximum_fusion.1), channel_id=1, source_target_pairs={{3,0},{4,1},{5,2},{6,3},{7,4},{0,5},{1,6},{2,7},{11,8},{12,9},{13,... | collective-permute-start | bytes 294920 | tf_op jit(solution)/shard_map/ppermute | solution.py:496
  66.3 0.6 collective-permute-start.10
  66.9 9.3 %near.2.near0 = f32[8,256]{1,0:T(8,128)S(1)} custom-call(f32[33,4,128]{2,1,0:T(4,128)S(1)} %collective-permute-done.z0, f32[33,4,128]{2,1,0:T(4,128)S(1)} %get-tuple-element.8.z1, f32[33,4,128]{2,1,0:T(4,128)S(1)} %get-tuple-element.7.z2, f32[33,4,128]{2,1,0:T(4,128)S(1)} %collective-permute-done.1.z3, f32[51,4,128]{2,1,0:T(4,128)S(1)} %collective-permute-done.2.ylo, ...), custom_call_target="tpu_custom_call" | custom-call | flops 6000000000 | bytes 1048576 | tf_op jit(solution)/shard_map/near/pallas_call | solution.py:482
  76.3 0.0 copy-start.1
  76.3 0.0 copy-start.3
  76.3 0.0 copy-start.6
  76.3 0.0 collective-permute-done.10
  76.3 0.0 collective-permute-done.9
  76.3 0.1 pad_maximum_fusion
  76.4 0.7 copy-done.1
  77.2 0.0 copy-done.3
  77.2 0.0 copy-done.6
  77.2 10.6 %last.1 = f32[4,4,256]{2,1,0:T(4,128)} custom-call(s32[4,4,4]{2,1,0:T(4,128)S(1)} %copy-done.6, f32[256,2,128]{2,1,0:T(2,128)S(1)} %bitcast.109, f32[64,256]{1,0:T(8,128)S(1)} %far.1, f32[8,256]{1,0:T(8,128)S(1)} %near.2.near0, f32[8,256]{1,0:T(8,128)S(1)} %near.3.near1, f32[3,4,4,256]{3,2,1,0:T(4,128)S(1)} %copy-done.3, f32[152,152]{1,0:T(8,128)S(1)} %copy-done.1, ...), custom_call_target="tpu_custom_call" | custom-call | flops 8999999488 | bytes 1048576 | tf_op jit(solution)/shard_map/last/pallas_call | solution.py:482
  (78 shorter events, 0.8 us)
Async XLA Ops:
  0.0 0.7 copy-start.10
  0.0 0.7 copy-start.12
  0.7 0.9 %copy-start = (f32[152,152]{1,0:T(8,128)S(1)}, f32[152,152]{1,0:T(8,128)}, u32[]{:S(2)}) copy-start(f32[152,152]{1,0:T(8,128)} %up.1) | copy-start | bytes 277252
  1.6 0.8 copy-start.2
  2.4 0.7 copy-start.4
  3.1 0.7 copy-start.5
  3.8 1.0 %copy-start.7 = (f32[3,160,256]{2,1,0:T(8,128)S(1)}, f32[3,160,256]{2,1,0:T(8,128)}, u32[]{:S(2)}) copy-start(f32[3,160,256]{2,1,0:T(8,128)} %constant.17.clone.column) | copy-start | bytes 1474564
  9.9 4.2 %collective-permute-start = (f32[33,4,128]{2,1,0:T(4,128)S(1)}, f32[33,4,128]{2,1,0:T(4,128)S(1)}, u32[]{:S(2)}, u32[]{:S(2)}) collective-permute-start(f32[33,4,128]{2,1,0:T(4,128)S(1)} %get-tuple-element.7.z2), channel_id=1, source_target_pairs={{7,0},{0,1},{1,2},{2,3},{3,4},{4,5},{5,6},{6,7},{15,8},{8,9},{9,10... | collective-permute-start | bytes 202760 | tf_op jit(solution)/shard_map/ppermute | solution.py:496
  12.6 3.7 %collective-permute-start.1 = (f32[33,4,128]{2,1,0:T(4,128)S(1)}, f32[33,4,128]{2,1,0:T(4,128)S(1)}, u32[]{:S(2)}, u32[]{:S(2)}) collective-permute-start(f32[33,4,128]{2,1,0:T(4,128)S(1)} %get-tuple-element.8.z1), channel_id=1, source_target_pairs={{1,0},{2,1},{3,2},{4,3},{5,4},{6,5},{7,6},{0,7},{9,8},{10,9},{11,1... | collective-permute-start | bytes 202760 | tf_op jit(solution)/shard_map/ppermute | solution.py:496
  13.2 0.8 copy-start.14
  16.6 4.8 %collective-permute-start.2 = (f32[51,4,128]{2,1,0:T(4,128)S(1)}, f32[51,4,128]{2,1,0:T(4,128)S(1)}, u32[]{:S(2)}, u32[]{:S(2)}) collective-permute-start(f32[51,4,128]{2,1,0:T(4,128)S(1)} %get-tuple-element.75), channel_id=1, source_target_pairs={{24,0},{0,8},{8,16},{16,24},{25,1},{1,9},{9,17},{17,25},{26,2},{2,... | collective-permute-start | bytes 313352 | tf_op jit(solution)/shard_map/ppermute | solution.py:496
  17.9 3.5 %collective-permute-start.3 = (f32[51,4,128]{2,1,0:T(4,128)S(1)}, f32[51,4,128]{2,1,0:T(4,128)S(1)}, u32[]{:S(2)}, u32[]{:S(2)}) collective-permute-start(f32[51,4,128]{2,1,0:T(4,128)S(1)} %get-tuple-element.74), channel_id=1, source_target_pairs={{8,0},{16,8},{24,16},{0,24},{9,1},{17,9},{25,17},{1,25},{10,2},{18... | collective-permute-start | bytes 313352 | tf_op jit(solution)/shard_map/ppermute | solution.py:496
  21.9 11.1 %collective-permute-start.4 = (f32[97,4,128]{2,1,0:T(4,128)S(1)}, f32[97,4,128]{2,1,0:T(4,128)S(1)}, u32[]{:S(2)}, u32[]{:S(2)}) collective-permute-start(f32[97,4,128]{2,1,0:T(4,128)S(1)} %constant_dynamic-update-slice_fusion.22), channel_id=1, source_target_pairs={{224,0},{0,32},{32,64},{64,96},{96,128},{128,160},{160,192},{192,2... | collective-permute-start | bytes 595976 | tf_op jit(solution)/shard_map/ppermute | solution.py:496
  24.6 10.0 %copy-start.13 = (s32[343,4,4,4]{0,3,2,1:T(4,128)S(1)}, s32[343,4,4,4]{0,3,2,1:T(4,128)}, u32[]{:S(2)}) copy-start(s32[343,4,4,4]{0,3,2,1:T(4,128)} %param.16) | copy-start | bytes 263428
  33.1 5.1 %collective-permute-start.5 = (f32[97,4,128]{2,1,0:T(4,128)S(1)}, f32[97,4,128]{2,1,0:T(4,128)S(1)}, u32[]{:S(2)}, u32[]{:S(2)}) collective-permute-start(f32[97,4,128]{2,1,0:T(4,128)S(1)} %get-tuple-element.12), channel_id=1, source_target_pairs={{32,0},{64,32},{96,64},{128,96},{160,128},{192,160},{224,192},{0,2... | collective-permute-start | bytes 595976 | tf_op jit(solution)/shard_map/ppermute | solution.py:496
  34.4 7.4 %copy-start.8 = (f32[3,160,256]{2,1,0:T(8,128)S(1)}, f32[3,160,256]{2,1,0:T(8,128)}, u32[]{:S(2)}) copy-start(f32[3,160,256]{2,1,0:T(8,128)} %constant.17.clone.column) | copy-start | bytes 1474564
  34.6 7.2 %copy-start.9 = (bf16[512,384]{1,0:T(8,128)(2,1)S(1)}, bf16[512,384]{1,0:T(8,128)(2,1)}, u32[]{:S(2)}) copy-start(bf16[512,384]{1,0:T(8,128)(2,1)} %constant.21.clone.pick) | copy-start | bytes 1179652
  38.2 9.9 %collective-permute-start.6 = (f32[27,2,128]{2,1,0:T(2,128)S(1)}, f32[27,2,128]{2,1,0:T(2,128)S(1)}, u32[]{:S(2)}, u32[]{:S(2)}) collective-permute-start(f32[27,2,128]{2,1,0:T(2,128)S(1)} %slice.560), channel_id=1, source_target_pairs={{96,0},{128,32},{160,64},{192,96},{224,128},{0,160},{32,192},{64,2... | collective-permute-start | bytes 82952 | tf_op jit(solution)/shard_map/ppermute | solution.py:496
  39.9 1.9 %copy-start.11 = (s32[8,256]{1,0:T(8,128)S(1)}, s32[8,256]{1,0:T(8,128)}, u32[]{:S(2)}) copy-start(s32[8,256]{1,0:T(8,128)} %constant.20.clone.mirror) | copy-start | bytes 24580
  39.9 8.2 %collective-permute-start.7 = (f32[18,2,128]{2,1,0:T(2,128)S(1)}, f32[18,2,128]{2,1,0:T(2,128)S(1)}, u32[]{:S(2)}, u32[]{:S(2)}) collective-permute-start(f32[18,2,128]{2,1,0:T(2,128)S(1)} %slice.561), channel_id=1, source_target_pairs={{160,0},{192,32},{224,64},{0,96},{32,128},{64,160},{96,192},{128,2... | collective-permute-start | bytes 55304 | tf_op jit(solution)/shard_map/ppermute | solution.py:496
  48.1 10.7 %collective-permute-start.8 = (f32[8,3,2,128]{3,2,1,0:T(2,128)S(1)}, f32[8,3,2,128]{3,2,1,0:T(2,128)S(1)}, u32[]{:S(2)}, u32[]{:S(2)}) collective-permute-start(f32[8,3,2,128]{3,2,1,0:T(2,128)S(1)} %slice_bitcast_fusion), channel_id=1, source_target_pairs={{16,0},{24,8},{0,16},{8,24},{17,1},{25,9},{1,17},{9,25},{18,2},{26... | collective-permute-start | bytes 73736 | tf_op jit(solution)/shard_map/ppermute | solution.py:496
  58.9 17.4 %collective-permute-start.9 = (f32[8,4,3,2,128]{4,3,2,1,0:T(2,128)S(1)}, f32[8,4,3,2,128]{4,3,2,1,0:T(2,128)S(1)}, u32[]{:S(2)}, u32[]{:S(2)}) collective-permute-start(f32[8,4,3,2,128]{4,3,2,1,0:T(2,128)S(1)} %pad_maximum_fusion.1), channel_id=1, source_target_pairs={{3,0},{4,1},{5,2},{6,3},{7,4},{0,5},{1,6},{2,7},{11,8},{12,9},{13,... | collective-permute-start | bytes 294920 | tf_op jit(solution)/shard_map/ppermute | solution.py:496
  66.3 10.0 %collective-permute-start.10 = (f32[8,4,2,2,128]{4,3,2,1,0:T(2,128)S(1)}, f32[8,4,2,2,128]{4,3,2,1,0:T(2,128)S(1)}, u32[]{:S(2)}, u32[]{:S(2)}) collective-permute-start(f32[8,4,2,2,128]{4,3,2,1,0:T(2,128)S(1)} %fusion), channel_id=1, source_target_pairs={{5,0},{6,1},{7,2},{0,3},{1,4},{2,5},{3,6},{4,7},{13,8},{14,9},{15,... | collective-permute-start | bytes 196616 | tf_op jit(solution)/shard_map/ppermute | solution.py:496
  76.3 0.9 %copy-start.1 = (f32[152,152]{1,0:T(8,128)S(1)}, f32[152,152]{1,0:T(8,128)}, u32[]{:S(2)}) copy-start(f32[152,152]{1,0:T(8,128)} %down.1) | copy-start | bytes 277252
  76.3 0.9 %copy-start.3 = (f32[3,4,4,256]{3,2,1,0:T(4,128)S(1)}, f32[3,4,4,256]{3,2,1,0:T(4,128)}, u32[]{:S(2)}) copy-start(f32[3,4,4,256]{3,2,1,0:T(4,128)} %pos.3) | copy-start | bytes 147460
  76.3 0.9 %copy-start.6 = (s32[4,4,4]{2,1,0:T(4,128)S(1)}, s32[4,4,4]{2,1,0:T(4,128)}, u32[]{:S(2)}) copy-start(s32[4,4,4]{2,1,0:T(4,128)} %counts.3) | copy-start | bytes 772

commit v2 on v1

--- a/solution.py
+++ b/solution.py
@@ -297,15 +297,17 @@
     out[...] = result
 
 
-def near_kernel(
-    first_row, rows_here, z0, z1, z2, z3, ylo, yhi, xlo, xhi, flags,
-    out, lines, sources, points, listed, shifted, sums,
-):
-    refs = ((z0, z1, z2, z3), ylo, yhi, xlo, xhi)
-    for x in range(6):
+def near_kernel(first, planes, *refs):
+    *halo, flags, out, lines, sources, points, shifted, sums = refs
+    refs = (halo[0:4], *halo[4:])
+    if len(halo) == 6:
+        refs = (*refs, None, None)
+    z1, z2 = halo[1], halo[2]
+    count = (planes + 2) * 6
+    for x in range(planes + 2):
         for y in range(6):
             for pair in range(4):
-                record = particle_record(refs, x - 1, y - 1, pair)
+                record = particle_record(refs, x + first - 1, y - 1, pair)
                 for c in range(4):
                     lines[c, x * 6 + y : x * 6 + y + 1, pair * 128 : pair * 128 + 128] = record[c : c + 1]
     for c in range(4):
@@ -315,15 +317,15 @@
             if c == 2:
                 line = line + float(e - 1)
             for half in range(2):
-                sources.at[c, half][pl.ds(e, 40, stride=3), :] = line[:, at + half * 128 : at + half * 128 + 128]
+                lanes = slice(at + half * 128, at + half * 128 + 128)
+                sources.at[c, half][pl.ds(e, count, stride=3), :] = line[0:count, lanes]
     same = (iota((64, WIDE), 1) & 63) == iota((64, WIDE), 0)
     block = ((iota((WIDE, WIDE), 0) >> 6) == (iota((WIDE, WIDE), 1) >> 6)).astype(F32).astype(BF16)
     zone = iota((32, WIDE), 1) >> 6
     step_y = (iota((9, WIDE), 0) // 3 - 1).astype(F32)
-
-    def one_row(i, carry):
-        r = i + first_row
-        x, y = r >> 2, r & 3
+    for i in range(planes * 4):
+        r = first * 4 + i
+        x, y = i // 4, i % 4
         pieces = []
         for c in range(3):
             v = jnp.concatenate([z1[16 + r, c : c + 1, :], z2[16 + r, c : c + 1, :]], axis=1)
@@ -337,49 +339,50 @@
             at = c * 192
             v = spread[at : at + 64] + spread[at + 64 : at + 128] + spread[at + 128 : at + 192]
             square = square + v * v
-            points[c] = -2.0 * v
-        points[3] = square
-        f = flags[x, y]
+            points[i, c] = -2.0 * v
+        points[i, 3] = square
+        f = flags[x + first, y]
         lists = jnp.zeros((32, WIDE), F32)
         for z in range(4):
             lists = jnp.where(zone == z, f[:, z : z + 1], lists)
-        listed[...] = lists
         for ex in range(3):
             at = ((x + ex) * 6 + y) * 3
+            here = slice(ex * 9, ex * 9 + 9)
             sx, sy, sz, q = (
-                jnp.concatenate([sources.at[c, half][pl.ds(at, 9), :] for half in range(2)], axis=1) for c in range(4)
+                jnp.concatenate([sources[c, half, at : at + 9, :] for half in range(2)], axis=1) for c in range(4)
             )
             sx = sx + float(ex - 1)
             sy = sy + step_y
-            shifted[0, ex * 9 : ex * 9 + 9, :] = sx
-            shifted[1, ex * 9 : ex * 9 + 9, :] = sy
-            shifted[2, ex * 9 : ex * 9 + 9, :] = sz
-            shifted[3, ex * 9 : ex * 9 + 9, :] = sx * sx + sy * sy + sz * sz
-            shifted[4, ex * 9 : ex * 9 + 9, :] = q * listed[ex * 9 : ex * 9 + 9, :]
-        for part in range(2):
-            for half in range(2):
-                lanes = slice(half * 128, half * 128 + 128)
-                rows = slice(part * 32, part * 32 + 32)
-                tx, ty, tz, tt = (points[c, rows, lanes] for c in range(4))
-                acc = jnp.zeros((32, 128), F32)
-                for n in range(27):
-                    sx, sy, sz, ss, q = (shifted[c, n : n + 1, lanes] for c in range(5))
-                    k = lax.rsqrt((tt + ss) + tx * sx + ty * sy + tz * sz)
-                    if n == 13:
-                        k = jnp.where(same[rows, lanes], 0.0, k)
-                    acc = acc + k * q
-                sums[rows, lanes] = acc
-        hi, lo = split2(sums[...])
+            shifted[i, 0, here, :] = sx
+            shifted[i, 1, here, :] = sy
+            shifted[i, 2, here, :] = sz
+            shifted[i, 3, here, :] = sx * sx + sy * sy + sz * sz
+            shifted[i, 4, here, :] = q * lists[here]
+
+    def one_row(i, carry):
+        for half in range(2):
+            lanes = slice(half * 128, half * 128 + 128)
+            tx, ty, tz, tt = (points[i, c, :, lanes] for c in range(4))
+            acc = jnp.zeros((64, 128), F32)
+            for n in range(27):
+                sx, sy, sz, ss, q = (shifted[i, c, n : n + 1, lanes] for c in range(5))
+                k = lax.rsqrt((tt + ss) + tx * sx + ty * sy + tz * sz)
+                if n == 13:
+                    k = jnp.where(same[:, lanes], 0.0, k)
+                acc = acc + k * q
+            sums[i, :, lanes] = acc
+        return carry
+
+    lax.fori_loop(0, planes * 4, one_row, 0)
+    for i in range(planes * 4):
+        hi, lo = split2(sums[i])
         both = jnp.dot(jnp.concatenate([hi, lo], axis=0), block, preferred_element_type=F32)
         picked = jnp.where(same, both[0:64] + both[64:128], 0.0)
-        out[pl.ds(i, 1), :] = jnp.sum(picked, axis=0, keepdims=True)
-        return carry
-
-    lax.fori_loop(0, rows_here, one_row, 0)
+        out[i : i + 1, :] = jnp.sum(picked, axis=0, keepdims=True)
 
 
 def last_kernel(
-    counts, gathered, far, near0, near1, pos, down, column, row, tail,
+    counts, gathered, far, near0, near12, near3, pos, down, column, row, tail,
     out, operator, squares, offsets, tails, acc, checks, ends,
 ):
     padded_operator(down, operator)
@@ -473,11 +476,11 @@
                 (OUTER * 0.5) * column[2] - pz,
             )
             line = jnp.sum(k * (wide[0:SPAD] + wide[SPAD : 2 * SPAD]), axis=0, keepdims=True)
-            near = near0 if r < 8 else near1
-            out[x, y : y + 1, :] = occupied_row(counts, x, y) * (line + near[r % 8 : r % 8 + 1, :])
-
-
-def call(body, outs, scratch, memory, name, work, *args):
+            near, i = (near0, r) if x == 0 else (near3, r - 12) if x == 3 else (near12, r - 4)
+            out[x, y : y + 1, :] = occupied_row(counts, x, y) * (line + near[i : i + 1, :])
+
+
+def call(body, outs, scratch, memory, name, work, *args, vmem=40):
     spaces = {"v": pltpu.VMEM, "s": pltpu.SMEM}
     return pl.pallas_call(
         body,
@@ -485,7 +488,7 @@
         in_specs=[pl.BlockSpec(memory_space=spaces[m]) for m in memory],
         out_specs=[pl.BlockSpec(memory_space=pltpu.VMEM) for _ in outs],
         scratch_shapes=[pltpu.VMEM(s, d) for s, d in scratch],
-        compiler_params=pltpu.CompilerParams(vmem_limit_bytes=40 << 20),
+        compiler_params=pltpu.CompilerParams(vmem_limit_bytes=vmem << 20),
         cost_estimate=pl.CostEstimate(flops=work * 1000000, transcendentals=0, bytes_accessed=1 << 20),
         name=name,
     )(*args)
@@ -505,7 +508,7 @@
             ((2 * SPAD, 16 * WIDE), BF16), ((WIDE, WIDE), F32), ((12, SPAD, WIDE), F32),
             ((WIDE, WIDE), F32), ((1, 64, 128), F32),
         ],
-        "vvsvvvv", "upward", 6000, positions, charges, counts, up_operator, column, row, tail,
+        "vvsvvvv", "upward", 6000, positions, charges, counts, up_operator, column, row, tail, vmem=59,
     )
     own = (shifted(above, "gz", -1), below, above, shifted(below, "gz", 1))
 
@@ -531,8 +534,9 @@
             parts += [ylo[at : at + 1], grid[1][s][one], yhi[at : at + 1]]
         return jnp.concatenate(parts + [blocks], axis=0)
 
-    xlo = shifted(to_x(2, 3), "gx", -1)
-    xhi = shifted(to_x(0, 0), "gx", 1)
+    up, down = lax.optimization_barrier((to_x(2, 3), to_x(0, 0)))
+    xlo = shifted(up, "gx", -1)
+    xhi = shifted(down, "gx", 1)
     halo = (*own, ylo, yhi, xlo, xhi)
 
     held = jnp.concatenate([xlo[88:97], blocks, xhi[88:97]], axis=0)[:, 0:2]
@@ -557,17 +561,21 @@
     centre = jnp.ones((1, *near_flags.shape[1:]), F32)
     listed = jnp.concatenate([near_flags[0:13], centre, near_flags[13:26], jnp.zeros((5, *near_flags.shape[1:]), F32)], axis=0)
     listed = listed.transpose(1, 2, 0, 3)
-    near = []
-    for n in range(2):
-        near += call(
-            functools.partial(near_kernel, 8 * n, 8),
-            [(8, WIDE)],
+
+    def near(first, planes, halo):
+        count = (planes + 2) * 6
+        (result,) = call(
+            functools.partial(near_kernel, first, planes),
+            [(planes * 4, WIDE)],
             [
-                ((4, 40, 512), F32), ((4, 2, 120, 128), F32), ((4, 64, WIDE), F32), ((32, WIDE), F32),
-                ((5, 32, WIDE), F32), ((64, WIDE), F32),
+                ((4, count + -count % 8, 512), F32), ((4, 2, count * 3, 128), F32), ((planes * 4, 4, 64, WIDE), F32),
+                ((planes * 4, 5, 32, WIDE), F32), ((planes * 4, 64, WIDE), F32),
             ],
-            "v" * 9, "near", 6000, *halo, listed,
+            "v" * (len(halo) + 1), "near", 3000 * planes, *halo, listed,
         )
+        return result
+
+    inner, low, high = near(1, 2, halo[0:6]), near(0, 1, halo), near(3, 1, halo)
     (potential,) = call(
         last_kernel,
         [(4, 4, WIDE)],
@@ -575,7 +583,7 @@
             ((WIDE, WIDE), F32), ((12, SPAD, WIDE), F32), ((20, SPAD, 128), F32), ((14, SPAD, 128), F32),
             ((WIDE, WIDE), F32), ((2, 128, 128), F32), ((16, 128), F32),
         ],
-        "svvvvvvvvv", "last", 9000, counts, gathered, far, near[0], near[1], positions, down_operator, column, row, tail,
+        "svvvvvvvvvv", "last", 9000, counts, gathered, far, low, inner, high, positions, down_operator, column, row, tail,
     )
     return potential
 

time: 88.2 us -> 67.7 us (0.77)
  waiting for transfers between devices: 15.9 us -> 3.55 us
  Pallas kernels: 40.5 us -> 35.7 us
  local copies, waits for them, and re-layouts: 7.49 us -> 3.43 us
    ppermute x11, waiting for transfers between devices: 15.9 us -> 3.55 us  [shifted(): lax.ppermute(array, axis, [((i + distance) % n, i) for i in range(n)])]
    unnamed x74 -> x68, local copies, waits for them, and re-layouts: 6.77 us -> 1.91 us
    pallas_call x5 -> x6, Pallas kernels: 40.5 us -> 35.7 us  [call(): pl.pallas_call(body, out_shape=[jax.ShapeDtypeStruct(s, F32) for s in out...]
  transfers between devices with their start and end apart: 11 -> 11, of which waited for: 4 -> 3; matrix products, arithmetic and copies ran while one was open for 1% -> 2% of each run, Pallas kernels for 28% -> 28%
where the time goes in v2:
time: 67.7 us; the launch traced here: 67.4 us
  Pallas kernels  35.7 us (53%)
  starting transfers between devices  23.7 us (35%)
  waiting for transfers between devices  3.55 us (5%)
  local copies, waits for them, and re-layouts  3.43 us (5%)
    pallas_call x6, Pallas kernels, call(): pl.pallas_call(body, out_shape=[jax.ShapeDtypeStruct(s, F32) for s in out...  35.7 us
    ppermute x11, starting transfers between devices, shifted(): lax.ppermute(array, axis, [((i + distance) % n, i) for i in range(n)])  23.7 us
    ppermute x11, waiting for transfers between devices, shifted(): lax.ppermute(array, axis, [((i + distance) % n, i) for i in range(n)])  3.55 us
    unnamed x68, local copies, waits for them, and re-layouts  1.91 us
  transfers between devices with their start and end apart: 11, of which 3 were waited for; matrix products, arithmetic and copies ran while one was open for 2% of the time, Pallas kernels for 28%

profile of v2, /device:TPU:1, one launch (start us, length us, event | category | flops | bytes accessed | tf_op | source)
XLA Modules:
  0.0 67.4 jit_solution(15105324790864525009)
XLA Ops:
  0.0 6.2 %upward.1 = (f32[33,4,128]{2,1,0:T(4,128)}, f32[33,4,128]{2,1,0:T(4,128)}) custom-call(f32[3,4,4,256]{3,2,1,0:T(4,128)} %pos.3, f32[4,4,256]{2,1,0:T(4,128)} %chg.1, s32[4,4,4]{2,1,0:T(4,128)} %counts.3, f32[152,152]{1,0:T(8,128)} %up.1, f32[3,160,256]{2,1,0:T(8,128)} %constant.17.clone.column, f32[8,256]{1,0:T(8,128)} %constant.18.clone.row, ...), custom_call_target="tpu_custom_call" | custom-call | flops 6000000000 | bytes 1048576 | tf_op jit(solution)/shard_map/upward/pallas_call | solution.py:485
  6.2 2.7 %collective-permute-start = (f32[33,4,128]{2,1,0:T(4,128)}, f32[33,4,128]{2,1,0:T(4,128)S(1)}, u32[]{:S(2)}, u32[]{:S(2)}) collective-permute-start(f32[33,4,128]{2,1,0:T(4,128)} %get-tuple-element.9.z2.refs_2_), channel_id=1, source_target_pairs={{7,0},{0,1},{1,2},{2,3},{3,4},{4,5},{5,6},{6,7},{15,8},{8,9},{9,10... | collective-permute-start | bytes 202760 | tf_op jit(solution)/shard_map/ppermute | solution.py:499
  8.9 0.0 copy-start
  8.9 0.0 copy-start.1
  8.9 0.6 collective-permute-start.1
  9.5 0.8 %fusion.8 = (f32[16,4,128]{2,1,0:T(4,128)S(1)}, f32[16,4,128]{2,1,0:T(4,128)S(1)}, f32[16,4,128]{2,1,0:T(4,128)S(1)}, f32[16,4,128]{2,1,0:T(4,128)S(1)}) fusion(f32[33,4,128]{2,1,0:T(4,128)} %get-tuple-element.9.z2.refs_2_, f32[33,4,128]{2,1,0:T(4,128)} %get-tuple-element.10.z1.refs_1_), kind=kLoop, calls=%fused_computation.108 | loop fusion | bytes 262144 | tf_op jit(solution)/shard_map/slice | solution.py:515
  10.3 0.0 copy-done
  10.3 0.0 copy-done.1
  10.3 0.0 copy-start.11
  10.3 0.7 %copy-done.11 = s32[26,4,4,4]{0,3,2,1:T(4,128)S(1)} copy-done((s32[26,4,4,4]{0,3,2,1:T(4,128)S(1)}, s32[26,4,4,4]{0,3,2,1:T(4,128)}, u32[]{:S(2)}) %copy-start.11) | copy-done | bytes 6680
  11.1 0.1 fusion.11
  11.2 0.1 pad.8.clone
  11.3 0.1 pad.6.clone
  11.3 0.1 maximum_maximum_fusion
  11.4 0.0 copy-start.10
  11.4 0.2 copy.45
  11.6 0.7 %copy-done.10 = s32[343,4,4,4]{0,3,2,1:T(4,128)S(1)} copy-done((s32[343,4,4,4]{0,3,2,1:T(4,128)S(1)}, s32[343,4,4,4]{0,3,2,1:T(4,128)}, u32[]{:S(2)}) %copy-start.10) | copy-done | bytes 87832
  12.4 0.1 copy.44
  12.5 0.0 collective-permute-done.z0.refs_0_
  12.6 0.2 collective-permute-done.1.z3.refs_3_
  13.0 1.3 %collective-permute-start.2 = (f32[51,4,128]{2,1,0:T(4,128)S(1)}, f32[51,4,128]{2,1,0:T(4,128)S(1)}, u32[]{:S(2)}, u32[]{:S(2)}) collective-permute-start(f32[51,4,128]{2,1,0:T(4,128)S(1)} %get-tuple-element.84), channel_id=1, source_target_pairs={{24,0},{0,8},{8,16},{16,24},{25,1},{1,9},{9,17},{17,25},{26,2},{2,... | collective-permute-start | bytes 313352 | tf_op jit(solution)/shard_map/ppermute | solution.py:499
  14.3 1.5 %collective-permute-start.3 = (f32[51,4,128]{2,1,0:T(4,128)S(1)}, f32[51,4,128]{2,1,0:T(4,128)S(1)}, u32[]{:S(2)}, u32[]{:S(2)}) collective-permute-start(f32[51,4,128]{2,1,0:T(4,128)S(1)} %get-tuple-element.83), channel_id=1, source_target_pairs={{8,0},{16,8},{24,16},{0,24},{9,1},{17,9},{25,17},{1,25},{10,2},{18... | collective-permute-start | bytes 313352 | tf_op jit(solution)/shard_map/ppermute | solution.py:499
  15.8 2.1 %collective-permute-done.2.ylo.refs_4_ = f32[51,4,128]{2,1,0:T(4,128)S(1)} collective-permute-done((f32[51,4,128]{2,1,0:T(4,128)S(1)}, f32[51,4,128]{2,1,0:T(4,128)S(1)}, u32[]{:S(2)}, u32[]{:S(2)}) %collective-permute-start.2) | collective-permute-done | bytes 104480 | tf_op jit(solution)/shard_map/ppermute | solution.py:499
  17.8 0.0 collective-permute-done.3.yhi.refs_5_
  18.3 1.7 %collective-permute-start.4 = (f32[97,4,128]{2,1,0:T(4,128)S(1)}, f32[97,4,128]{2,1,0:T(4,128)S(1)}, u32[]{:S(2)}, u32[]{:S(2)}) collective-permute-start(f32[97,4,128]{2,1,0:T(4,128)S(1)} %get-tuple-element.11), channel_id=1, source_target_pairs={{224,0},{0,32},{32,64},{64,96},{96,128},{128,160},{160,192},{192,2... | collective-permute-start | bytes 595976 | tf_op jit(solution)/shard_map/ppermute | solution.py:499
  20.1 4.0 %collective-permute-start.5 = (f32[97,4,128]{2,1,0:T(4,128)S(1)}, f32[97,4,128]{2,1,0:T(4,128)S(1)}, u32[]{:S(2)}, u32[]{:S(2)}) collective-permute-start(f32[97,4,128]{2,1,0:T(4,128)S(1)} %get-tuple-element.12), channel_id=1, source_target_pairs={{32,0},{64,32},{96,64},{128,96},{160,128},{192,160},{224,192},{0,2... | collective-permute-start | bytes 595976 | tf_op jit(solution)/shard_map/ppermute | solution.py:499
  24.1 0.0 copy-start.5
  24.1 0.0 copy-start.6
  24.1 6.3 %near.4.near12 = f32[8,256]{1,0:T(8,128)S(1)} custom-call(f32[33,4,128]{2,1,0:T(4,128)S(1)} %collective-permute-done.z0.refs_0_, f32[33,4,128]{2,1,0:T(4,128)S(1)} %copy-done, f32[33,4,128]{2,1,0:T(4,128)S(1)} %copy-done.1, f32[33,4,128]{2,1,0:T(4,128)S(1)} %collective-permute-done.1.z3.refs_3_, f32[51,4,128]{2,1,0:T(4,128)S(1)} %collective-permute-done.2.ylo.refs_4_, ...), custom_call_target="tpu_custom_call" | custom-call | flops 6000000000 | bytes 1048576 | tf_op jit(solution)/shard_map/near/pallas_call | solution.py:485
  30.4 0.0 collective-permute-done.4.xlo.refs_6_
  30.4 0.0 collective-permute-done.5.xhi.refs_7_
  30.5 2.3 %collective-permute-start.6 = (f32[27,2,128]{2,1,0:T(2,128)S(1)}, f32[27,2,128]{2,1,0:T(2,128)S(1)}, u32[]{:S(2)}, u32[]{:S(2)}) collective-permute-start(f32[27,2,128]{2,1,0:T(2,128)S(1)} %slice.560), channel_id=1, source_target_pairs={{96,0},{128,32},{160,64},{192,96},{224,128},{0,160},{32,192},{64,2... | collective-permute-start | bytes 82952 | tf_op jit(solution)/shard_map/ppermute | solution.py:499
  32.8 0.0 copy-start.7
  32.8 0.0 copy-start.8
  32.9 1.3 %collective-permute-start.7 = (f32[18,2,128]{2,1,0:T(2,128)S(1)}, f32[18,2,128]{2,1,0:T(2,128)S(1)}, u32[]{:S(2)}, u32[]{:S(2)}) collective-permute-start(f32[18,2,128]{2,1,0:T(2,128)S(1)} %slice.561), channel_id=1, source_target_pairs={{160,0},{192,32},{224,64},{0,96},{32,128},{64,160},{96,192},{128,2... | collective-permute-start | bytes 55304 | tf_op jit(solution)/shard_map/ppermute | solution.py:499
  34.1 0.0 copy-done.5
  34.1 0.0 copy-done.6
  34.1 0.0 copy-done.7
  34.1 0.0 copy-done.8
  34.1 6.2 %far.1 = f32[64,256]{1,0:T(8,128)S(1)} custom-call(f32[33,4,128]{2,1,0:T(4,128)S(1)} %collective-permute-done.z0.refs_0_, f32[33,4,128]{2,1,0:T(4,128)S(1)} %copy-done, f32[33,4,128]{2,1,0:T(4,128)S(1)} %copy-done.1, f32[33,4,128]{2,1,0:T(4,128)S(1)} %collective-permute-done.1.z3.refs_3_, f32[51,4,128]{2,1,0:T(4,128)S(1)} %collective-permute-done.2.ylo.refs_4_, ...), custom_call_target="tpu_custom_call" | custom-call | flops 7000000000 | bytes 1048576 | tf_op jit(solution)/shard_map/far/pallas_call | solution.py:485
  40.4 0.0 collective-permute-done.7
  40.4 0.0 collective-permute-done.6
  40.5 2.8 %collective-permute-start.8 = (f32[8,3,2,128]{3,2,1,0:T(2,128)S(1)}, f32[8,3,2,128]{3,2,1,0:T(2,128)S(1)}, u32[]{:S(2)}, u32[]{:S(2)}) collective-permute-start(f32[8,3,2,128]{3,2,1,0:T(2,128)S(1)} %slice_bitcast_fusion), channel_id=1, source_target_pairs={{16,0},{24,8},{0,16},{8,24},{17,1},{25,9},{1,17},{9,25},{18,2},{26... | collective-permute-start | bytes 73736 | tf_op jit(solution)/shard_map/ppermute | solution.py:499
  43.3 3.2 %near.5.near3 = f32[4,256]{1,0:T(4,128)S(1)} custom-call(f32[33,4,128]{2,1,0:T(4,128)S(1)} %collective-permute-done.z0.refs_0_, f32[33,4,128]{2,1,0:T(4,128)S(1)} %copy-done, f32[33,4,128]{2,1,0:T(4,128)S(1)} %copy-done.1, f32[33,4,128]{2,1,0:T(4,128)S(1)} %collective-permute-done.1.z3.refs_3_, f32[51,4,128]{2,1,0:T(4,128)S(1)} %collective-permute-done.2.ylo.refs_4_, ...), custom_call_target="tpu_custom_call" | custom-call | flops 3000000000 | bytes 1048576 | tf_op jit(solution)/shard_map/near/pallas_call | solution.py:485
  46.5 0.0 collective-permute-done.8
  46.6 5.2 %collective-permute-start.9 = (f32[8,4,3,2,128]{4,3,2,1,0:T(2,128)S(1)}, f32[8,4,3,2,128]{4,3,2,1,0:T(2,128)S(1)}, u32[]{:S(2)}, u32[]{:S(2)}) collective-permute-start(f32[8,4,3,2,128]{4,3,2,1,0:T(2,128)S(1)} %pad_maximum_fusion.1), channel_id=1, source_target_pairs={{3,0},{4,1},{5,2},{6,3},{7,4},{0,5},{1,6},{2,7},{11,8},{12,9},{13,... | collective-permute-start | bytes 294920 | tf_op jit(solution)/shard_map/ppermute | solution.py:499
  51.8 0.4 collective-permute-start.10
  52.2 3.2 %near.3.near0 = f32[4,256]{1,0:T(4,128)S(1)} custom-call(f32[33,4,128]{2,1,0:T(4,128)S(1)} %collective-permute-done.z0.refs_0_, f32[33,4,128]{2,1,0:T(4,128)S(1)} %copy-done, f32[33,4,128]{2,1,0:T(4,128)S(1)} %copy-done.1, f32[33,4,128]{2,1,0:T(4,128)S(1)} %collective-permute-done.1.z3.refs_3_, f32[51,4,128]{2,1,0:T(4,128)S(1)} %collective-permute-done.2.ylo.refs_4_, ...), custom_call_target="tpu_custom_call" | custom-call | flops 3000000000 | bytes 1048576 | tf_op jit(solution)/shard_map/near/pallas_call | solution.py:485
  55.4 0.0 copy-start.2
  55.4 0.0 copy-start.3
  55.4 0.0 copy-start.4
  55.4 0.0 copy-start.9
  55.4 1.2 %collective-permute-done.10 = f32[8,4,2,2,128]{4,3,2,1,0:T(2,128)S(1)} collective-permute-done((f32[8,4,2,2,128]{4,3,2,1,0:T(2,128)S(1)}, f32[8,4,2,2,128]{4,3,2,1,0:T(2,128)S(1)}, u32[]{:S(2)}, u32[]{:S(2)}) %collective-permute-start.10) | collective-permute-done | bytes 65568 | tf_op jit(solution)/shard_map/ppermute | solution.py:499
  56.7 0.0 collective-permute-done.9
  56.7 0.1 pad_maximum_fusion
  56.8 0.0 copy-done.2
  56.8 0.0 copy-done.3
  56.8 0.0 copy-done.4
  56.8 0.0 copy-done.9
  56.8 10.6 %last.1 = f32[4,4,256]{2,1,0:T(4,128)} custom-call(s32[4,4,4]{2,1,0:T(4,128)S(1)} %copy-done.4, f32[256,2,128]{2,1,0:T(2,128)S(1)} %bitcast.110, f32[64,256]{1,0:T(8,128)S(1)} %far.1, f32[4,256]{1,0:T(4,128)S(1)} %near.3.near0, f32[8,256]{1,0:T(8,128)S(1)} %near.4.near12, f32[4,256]{1,0:T(4,128)S(1)} %near.5.near3, f32[3,4,4,256]{3,2,1,0:T(4,128)S(1)} %copy-done.3, ...), custom_call_target="tpu_custom_call" | custom-call | flops 8999999488 | bytes 1048576 | tf_op jit(solution)/shard_map/last/pallas_call | solution.py:485
  (77 shorter events, 0.8 us)
Async XLA Ops:
  6.2 6.3 %collective-permute-start = (f32[33,4,128]{2,1,0:T(4,128)}, f32[33,4,128]{2,1,0:T(4,128)S(1)}, u32[]{:S(2)}, u32[]{:S(2)}) collective-permute-start(f32[33,4,128]{2,1,0:T(4,128)} %get-tuple-element.9.z2.refs_2_), channel_id=1, source_target_pairs={{7,0},{0,1},{1,2},{2,3},{3,4},{4,5},{5,6},{6,7},{15,8},{8,9},{9,10... | collective-permute-start | bytes 202760 | tf_op jit(solution)/shard_map/ppermute | solution.py:499
  8.9 1.4 %copy-start = (f32[33,4,128]{2,1,0:T(4,128)S(1)}, f32[33,4,128]{2,1,0:T(4,128)}, u32[]{:S(2)}) copy-start(f32[33,4,128]{2,1,0:T(4,128)} %get-tuple-element.10.z1.refs_1_) | copy-start | bytes 202756
  8.9 1.4 %copy-start.1 = (f32[33,4,128]{2,1,0:T(4,128)S(1)}, f32[33,4,128]{2,1,0:T(4,128)}, u32[]{:S(2)}) copy-start(f32[33,4,128]{2,1,0:T(4,128)} %get-tuple-element.9.z2.refs_2_) | copy-start | bytes 202756
  8.9 3.9 %collective-permute-start.1 = (f32[33,4,128]{2,1,0:T(4,128)}, f32[33,4,128]{2,1,0:T(4,128)S(1)}, u32[]{:S(2)}, u32[]{:S(2)}) collective-permute-start(f32[33,4,128]{2,1,0:T(4,128)} %get-tuple-element.10.z1.refs_1_), channel_id=1, source_target_pairs={{1,0},{2,1},{3,2},{4,3},{5,4},{6,5},{7,6},{0,7},{9,8},{10,9},{11,1... | collective-permute-start | bytes 202760 | tf_op jit(solution)/shard_map/ppermute | solution.py:499
  10.3 0.8 %copy-start.11 = (s32[26,4,4,4]{0,3,2,1:T(4,128)S(1)}, s32[26,4,4,4]{0,3,2,1:T(4,128)}, u32[]{:S(2)}) copy-start(s32[26,4,4,4]{0,3,2,1:T(4,128)} %param.15) | copy-start | bytes 19972
  11.4 0.9 %copy-start.10 = (s32[343,4,4,4]{0,3,2,1:T(4,128)S(1)}, s32[343,4,4,4]{0,3,2,1:T(4,128)}, u32[]{:S(2)}) copy-start(s32[343,4,4,4]{0,3,2,1:T(4,128)} %param.16) | copy-start | bytes 263428
  13.0 4.8 %collective-permute-start.2 = (f32[51,4,128]{2,1,0:T(4,128)S(1)}, f32[51,4,128]{2,1,0:T(4,128)S(1)}, u32[]{:S(2)}, u32[]{:S(2)}) collective-permute-start(f32[51,4,128]{2,1,0:T(4,128)S(1)} %get-tuple-element.84), channel_id=1, source_target_pairs={{24,0},{0,8},{8,16},{16,24},{25,1},{1,9},{9,17},{17,25},{26,2},{2,... | collective-permute-start | bytes 313352 | tf_op jit(solution)/shard_map/ppermute | solution.py:499
  14.3 3.5 %collective-permute-start.3 = (f32[51,4,128]{2,1,0:T(4,128)S(1)}, f32[51,4,128]{2,1,0:T(4,128)S(1)}, u32[]{:S(2)}, u32[]{:S(2)}) collective-permute-start(f32[51,4,128]{2,1,0:T(4,128)S(1)} %get-tuple-element.83), channel_id=1, source_target_pairs={{8,0},{16,8},{24,16},{0,24},{9,1},{17,9},{25,17},{1,25},{10,2},{18... | collective-permute-start | bytes 313352 | tf_op jit(solution)/shard_map/ppermute | solution.py:499
  18.3 12.0 %collective-permute-start.4 = (f32[97,4,128]{2,1,0:T(4,128)S(1)}, f32[97,4,128]{2,1,0:T(4,128)S(1)}, u32[]{:S(2)}, u32[]{:S(2)}) collective-permute-start(f32[97,4,128]{2,1,0:T(4,128)S(1)} %get-tuple-element.11), channel_id=1, source_target_pairs={{224,0},{0,32},{32,64},{64,96},{96,128},{128,160},{160,192},{192,2... | collective-permute-start | bytes 595976 | tf_op jit(solution)/shard_map/ppermute | solution.py:499
  20.1 10.4 %collective-permute-start.5 = (f32[97,4,128]{2,1,0:T(4,128)S(1)}, f32[97,4,128]{2,1,0:T(4,128)S(1)}, u32[]{:S(2)}, u32[]{:S(2)}) collective-permute-start(f32[97,4,128]{2,1,0:T(4,128)S(1)} %get-tuple-element.12), channel_id=1, source_target_pairs={{32,0},{64,32},{96,64},{128,96},{160,128},{192,160},{224,192},{0,2... | collective-permute-start | bytes 595976 | tf_op jit(solution)/shard_map/ppermute | solution.py:499
  24.1 10.0 %copy-start.5 = (f32[3,160,256]{2,1,0:T(8,128)S(1)}, f32[3,160,256]{2,1,0:T(8,128)}, u32[]{:S(2)}) copy-start(f32[3,160,256]{2,1,0:T(8,128)} %constant.17.clone.column) | copy-start | bytes 1474564
  24.1 10.0 %copy-start.6 = (bf16[512,384]{1,0:T(8,128)(2,1)S(1)}, bf16[512,384]{1,0:T(8,128)(2,1)}, u32[]{:S(2)}) copy-start(bf16[512,384]{1,0:T(8,128)(2,1)} %constant.21.clone.pick) | copy-start | bytes 1179652
  30.5 9.9 %collective-permute-start.6 = (f32[27,2,128]{2,1,0:T(2,128)S(1)}, f32[27,2,128]{2,1,0:T(2,128)S(1)}, u32[]{:S(2)}, u32[]{:S(2)}) collective-permute-start(f32[27,2,128]{2,1,0:T(2,128)S(1)} %slice.560), channel_id=1, source_target_pairs={{96,0},{128,32},{160,64},{192,96},{224,128},{0,160},{32,192},{64,2... | collective-permute-start | bytes 82952 | tf_op jit(solution)/shard_map/ppermute | solution.py:499
  32.8 1.3 %copy-start.7 = (f32[8,256]{1,0:T(8,128)S(1)}, f32[8,256]{1,0:T(8,128)}, u32[]{:S(2)}) copy-start(f32[8,256]{1,0:T(8,128)} %constant.18.clone.row) | copy-start | bytes 24580
  32.8 1.3 %copy-start.8 = (s32[8,256]{1,0:T(8,128)S(1)}, s32[8,256]{1,0:T(8,128)}, u32[]{:S(2)}) copy-start(s32[8,256]{1,0:T(8,128)} %constant.20.clone.mirror) | copy-start | bytes 24580
  32.9 7.5 %collective-permute-start.7 = (f32[18,2,128]{2,1,0:T(2,128)S(1)}, f32[18,2,128]{2,1,0:T(2,128)S(1)}, u32[]{:S(2)}, u32[]{:S(2)}) collective-permute-start(f32[18,2,128]{2,1,0:T(2,128)S(1)} %slice.561), channel_id=1, source_target_pairs={{160,0},{192,32},{224,64},{0,96},{32,128},{64,160},{96,192},{128,2... | collective-permute-start | bytes 55304 | tf_op jit(solution)/shard_map/ppermute | solution.py:499
  40.5 6.0 %collective-permute-start.8 = (f32[8,3,2,128]{3,2,1,0:T(2,128)S(1)}, f32[8,3,2,128]{3,2,1,0:T(2,128)S(1)}, u32[]{:S(2)}, u32[]{:S(2)}) collective-permute-start(f32[8,3,2,128]{3,2,1,0:T(2,128)S(1)} %slice_bitcast_fusion), channel_id=1, source_target_pairs={{16,0},{24,8},{0,16},{8,24},{17,1},{25,9},{1,17},{9,25},{18,2},{26... | collective-permute-start | bytes 73736 | tf_op jit(solution)/shard_map/ppermute | solution.py:499
  46.6 10.1 %collective-permute-start.9 = (f32[8,4,3,2,128]{4,3,2,1,0:T(2,128)S(1)}, f32[8,4,3,2,128]{4,3,2,1,0:T(2,128)S(1)}, u32[]{:S(2)}, u32[]{:S(2)}) collective-permute-start(f32[8,4,3,2,128]{4,3,2,1,0:T(2,128)S(1)} %pad_maximum_fusion.1), channel_id=1, source_target_pairs={{3,0},{4,1},{5,2},{6,3},{7,4},{0,5},{1,6},{2,7},{11,8},{12,9},{13,... | collective-permute-start | bytes 294920 | tf_op jit(solution)/shard_map/ppermute | solution.py:499
  51.8 4.9 %collective-permute-start.10 = (f32[8,4,2,2,128]{4,3,2,1,0:T(2,128)S(1)}, f32[8,4,2,2,128]{4,3,2,1,0:T(2,128)S(1)}, u32[]{:S(2)}, u32[]{:S(2)}) collective-permute-start(f32[8,4,2,2,128]{4,3,2,1,0:T(2,128)S(1)} %fusion), channel_id=1, source_target_pairs={{5,0},{6,1},{7,2},{0,3},{1,4},{2,5},{3,6},{4,7},{13,8},{14,9},{15,... | collective-permute-start | bytes 196616 | tf_op jit(solution)/shard_map/ppermute | solution.py:499
  55.4 1.4 %copy-start.2 = (f32[152,152]{1,0:T(8,128)S(1)}, f32[152,152]{1,0:T(8,128)}, u32[]{:S(2)}) copy-start(f32[152,152]{1,0:T(8,128)} %down.1) | copy-start | bytes 277252
  55.4 1.4 %copy-start.3 = (f32[3,4,4,256]{3,2,1,0:T(4,128)S(1)}, f32[3,4,4,256]{3,2,1,0:T(4,128)}, u32[]{:S(2)}) copy-start(f32[3,4,4,256]{3,2,1,0:T(4,128)} %pos.3) | copy-start | bytes 147460
  55.4 1.4 %copy-start.4 = (s32[4,4,4]{2,1,0:T(4,128)S(1)}, s32[4,4,4]{2,1,0:T(4,128)}, u32[]{:S(2)}) copy-start(s32[4,4,4]{2,1,0:T(4,128)} %counts.3) | copy-start | bytes 772
  55.4 1.4 %copy-start.9 = (f32[8,128]{1,0:T(8,128)S(1)}, f32[8,128]{1,0:T(8,128)}, u32[]{:S(2)}) copy-start(f32[8,128]{1,0:T(8,128)} %constant.19.clone.tail) | copy-start | bytes 12292

commit v3 on v2

--- a/solution.py
+++ b/solution.py
@@ -24,7 +24,6 @@
 HIGHEST = lax.Precision.HIGHEST
 F32 = jnp.float32
 BF16 = jnp.bfloat16
-NT = (((1,), (1,)), ((), ()))
 RING8 = (-1, 0, 1, 2, 3, -4, -3, -2)
 RING4 = (-1, 0, 1, -2)
 SELF = (1 * 4 + 1) * 8 + 1
@@ -44,11 +43,16 @@
     points = surface_points()
     spacing = np.linspace(-1.0, 1.0, ORDER)
     g = np.array([[spacing[i] for i in p] for p in points], dtype=np.float32)
-    column = np.zeros((3, SPAD, WIDE), np.float32)
+    column = np.zeros((3, SPAD, 128), np.float32)
     column[:, :SURF, :] = g.T[:, :, None]
     row = np.zeros((8, WIDE), np.float32)
     row[:3, :SURF] = g.T
     tail = np.tile(row[:, 128:160], (1, 4))
+    nodes = np.zeros((SPAD, 128), np.float32)
+    for n, p in enumerate(points + [points[0]] * (SPAD - SURF)):
+        for part in range(3):
+            for axis in range(3):
+                nodes[n, part * 24 + axis * 8 + p[axis]] = 1.0
     where = {p: n for n, p in enumerate(points)}
     mirror = np.full((8, WIDE), -1, np.int32)
     for h in range(8):
@@ -65,7 +69,7 @@
                     d = [-v if f else v for v, f in zip((a, b, c), (h >> 2 & 1, h >> 1 & 1, h & 1))]
                     number = (d[0] + 3) * 49 + (d[1] + 3) * 7 + d[2] + 3
                     pick[(a * 16 + b * 4 + c) * 8 + h, number] = 1.0
-    return column, row, tail, mirror, pick.astype(ml_dtypes.bfloat16)
+    return column, row, tail, nodes.astype(ml_dtypes.bfloat16), mirror, pick.astype(ml_dtypes.bfloat16)
 
 
 def iota(shape, dim):
@@ -77,8 +81,21 @@
     return hi, (v - hi.astype(F32)).astype(BF16)
 
 
-def inverse_distance(x, y, z):
-    return lax.rsqrt(x * x + y * y + z * z + SOFTEN)
+def surface_terms(px, py, pz, nodes):
+    step = iota((8, WIDE), 0).astype(F32) * (OUTER / (ORDER - 1)) - OUTER * 0.5
+    parts = []
+    for n, p in enumerate((px, py, pz)):
+        d = step - p
+        parts.append(d * d + (SOFTEN if n == 2 else 0.0))
+    rest = jnp.concatenate(parts, axis=0)
+    parts = []
+    for _ in range(3):
+        b = rest.astype(BF16).astype(F32)
+        parts.append(b)
+        rest = rest - b
+    parts.append(jnp.zeros((128 - 72, WIDE), F32))
+    squares = jnp.concatenate(parts, axis=0).astype(BF16)
+    return lax.rsqrt(jnp.dot(nodes, squares, preferred_element_type=F32))
 
 
 def occupied_row(counts, x, y):
@@ -100,7 +117,7 @@
 def leaf_squares(column, row, tail, squares):
     segment = (iota((1, 128), 1) >> 5).astype(F32)
     for axis in range(3):
-        outer = (OUTER * HALF) * column[axis, :, 0:128]
+        outer = (OUTER * HALF) * column[axis]
         inner = (INNER * 0.5) * row[axis : axis + 1, 0:128]
         last = (INNER * 0.5) * tail[axis : axis + 1, :]
         soft = SOFTEN if axis == 2 else 0.0
@@ -116,25 +133,19 @@
 
 
 def upward_kernel(
-    pos, chg, counts, up, column, row, tail,
+    pos, chg, counts, up, column, row, tail, nodes,
     below, above,
-    terms, operator, squares, acc, leaves,
+    terms, operator, squares, leaves,
 ):
     padded_operator(up, operator)
+    flipped = operator[...].T
     leaf_squares(column, row, tail, squares)
     for x in range(4):
         for y in range(4):
             r = x * 4 + y
             q = chg[x, y : y + 1, :] * occupied_row(counts, x, y)
             px, py, pz = (pos[c, x, y : y + 1, :] for c in range(3))
-            k = (
-                inverse_distance(
-                    (OUTER * 0.5) * column[0] - px,
-                    (OUTER * 0.5) * column[1] - py,
-                    (OUTER * 0.5) * column[2] - pz,
-                )
-                * q
-            )
+            k = surface_terms(px, py, pz, nodes[...]) * q
             hi, lo = split2(k)
             terms[0:SPAD, r * WIDE : (r + 1) * WIDE] = hi
             terms[SPAD : 2 * SPAD, r * WIDE : (r + 1) * WIDE] = lo
@@ -145,7 +156,7 @@
     both = jnp.dot(terms[...], gather, preferred_element_type=F32)
     check = both[0:SPAD] + both[SPAD : 2 * SPAD]
     check = jnp.concatenate([check, jnp.zeros((WIDE - SPAD, 128), F32)], axis=0).T[0:64, :]
-    up_eq = lax.dot_general(check, operator[...], NT, precision=HIGHEST, preferred_element_type=F32)
+    up_eq = jnp.dot(check, flipped, precision=HIGHEST, preferred_element_type=F32)
     low = up_eq.astype(BF16).astype(F32)
     for r in range(16):
         for out, at in ((below, 0), (above, 2)):
@@ -156,7 +167,7 @@
     lines = leaves.at[0][pl.ds(0, 16, stride=4), :]
     for z in range(1, 4):
         lines = lines + pltpu.roll(leaves.at[0][pl.ds(z, 16, stride=4), :], 32 * z, 1)
-    acc[...] = jnp.zeros_like(acc)
+    block = jnp.zeros((8, WIDE), F32)
     for part in range(4):
         rows = slice(part * 40, part * 40 + 40)
         first, last = jnp.zeros((40, 128), F32), jnp.zeros((40, 128), F32)
@@ -169,11 +180,10 @@
                 xy = squares[x, rows, 128:256] + squares[4 + y, rows, 128:256]
                 r = x * 4 + y
                 last = last + lax.rsqrt(xy + squares[8, rows, 128:256]) * lines[r : r + 1, :]
-        acc[rows, 0:128] = first
-        acc[rows, 128:256] = last
-    ones = jnp.ones((8, WIDE), F32)
-    summed = lax.dot_general(ones, acc[...], NT, precision=HIGHEST, preferred_element_type=F32)
-    block = BREADTH * lax.dot_general(summed, operator[...], NT, precision=HIGHEST, preferred_element_type=F32)
+        weight = BREADTH * jnp.sum(first + last, axis=1, keepdims=True)
+        for n in range(part * 40, part * 40 + 40, 8):
+            block = block + flipped[n : n + 8] * weight[n - part * 40 : n - part * 40 + 8]
+    block = jnp.sum(block, axis=0, keepdims=True)
     for out in (below, above):
         out[32, 0:1, :] = block[0:1, 0:128]
         out[32, 1:2, :] = block[0:1, 128:256]
@@ -259,8 +269,10 @@
         chosen[...] = part if h == 0 else chosen[...] + part
     for axis in range(3):
         for d in range(4):
-            v = (INNER * 0.5) * row[axis : axis + 1, :] - d - (INNER * 0.5) * column[axis]
-            squares[axis * 4 + d] = v * v + (SOFTEN if axis == 2 else 0.0)
+            for half in range(2):
+                lanes = slice(half * 128, half * 128 + 128)
+                v = (INNER * 0.5) * row[axis : axis + 1, lanes] - d - (INNER * 0.5) * column[axis]
+                squares[axis * 4 + d, :, lanes] = v * v + (SOFTEN if axis == 2 else 0.0)
     matrices[...] = jnp.zeros_like(matrices)
     total[...] = jnp.zeros_like(total)
     for key, members in far_groups().items():
@@ -382,14 +394,15 @@
 
 
 def last_kernel(
-    counts, gathered, far, near0, near12, near3, pos, down, column, row, tail,
+    counts, gathered, far, near0, near12, near3, pos, down, column, row, tail, nodes,
     out, operator, squares, offsets, tails, acc, checks, ends,
 ):
     padded_operator(down, operator)
+    flipped = operator[...].T
     segment = iota((1, 128), 1) >> 5
     at = 0
     for axis, ring in enumerate((RING8, RING4, RING8)):
-        outer = (INNER * HALF) * column[axis, :, 0:128]
+        outer = (INNER * HALF) * column[axis]
         base = outer - (INNER * HALF) * row[axis : axis + 1, 0:128]
         end = outer - (INNER * HALF) * tail[axis : axis + 1, :]
         soft = SOFTEN if axis == 2 else 0.0
@@ -433,9 +446,9 @@
         return carry
 
     lax.fori_loop(0, 32, pair, 0)
-    ones = jnp.ones((WIDE, WIDE), F32)
-    summed = jnp.dot(acc[...], ones, precision=HIGHEST, preferred_element_type=F32)
-    local = BREADTH * jnp.dot(operator[...], summed, precision=HIGHEST, preferred_element_type=F32)
+    weight = BREADTH * jnp.sum(acc[0:SPAD, 0:128] + acc[0:SPAD, 128:256], axis=1, keepdims=True)
+    line = jnp.sum(flipped[0:SPAD] * weight, axis=0, keepdims=True)
+    local = jnp.broadcast_to(line, (128, WIDE)).T
     leaf_squares(column, row, tail, squares)
     checks[...] = jnp.zeros_like(checks)
     for x in range(4):
@@ -446,7 +459,8 @@
                 weight = local[rows, 0:128]
                 for z in range(5):
                     lanes = slice(0, 128) if z < 4 else slice(128, 256)
-                    xy = squares[x, rows, lanes] + squares[4 + y, rows, lanes]
+                    if z % 4 == 0:
+                        xy = squares[x, rows, lanes] + squares[4 + y, rows, lanes]
                     v = lax.rsqrt(xy + squares[8 + z % 4, rows, lanes]) * weight
                     for s in range(5):
                         lines[z] = lines[z] + v[s * 8 : s * 8 + 8]
@@ -460,8 +474,8 @@
         part = pltpu.roll(ends[...], 128 - 32 * z, 1) if z else ends[...]
         checks.at[1][pl.ds(z, 16, stride=4), :] = jnp.where(used, part, 0.0)
     both = jnp.concatenate([checks[0], checks[1]], axis=1)
-    both = both + jnp.concatenate([far[...], jnp.zeros((64, WIDE), F32)], axis=0)
-    local = jnp.dot(operator[...], both.T, precision=HIGHEST, preferred_element_type=F32)
+    local = jnp.dot(both[0:64] + far[...], flipped, precision=HIGHEST, preferred_element_type=F32)
+    local = jnp.concatenate([local, jnp.zeros((64, WIDE), F32)], axis=0).T
     hi, lo = split2(local[0:SPAD])
     both = jnp.concatenate([hi, lo], axis=0)
     for x in range(4):
@@ -470,11 +484,7 @@
             spread = (iota((128, WIDE), 0) == r * 4 + (iota((128, WIDE), 1) >> 6)).astype(F32).astype(BF16)
             wide = jnp.dot(both, spread, preferred_element_type=F32)
             px, py, pz = (pos[c, x, y : y + 1, :] for c in range(3))
-            k = inverse_distance(
-                (OUTER * 0.5) * column[0] - px,
-                (OUTER * 0.5) * column[1] - py,
-                (OUTER * 0.5) * column[2] - pz,
-            )
+            k = surface_terms(px, py, pz, nodes[...])
             line = jnp.sum(k * (wide[0:SPAD] + wide[SPAD : 2 * SPAD]), axis=0, keepdims=True)
             near, i = (near0, r) if x == 0 else (near3, r - 12) if x == 3 else (near12, r - 4)
             out[x, y : y + 1, :] = occupied_row(counts, x, y) * (line + near[i : i + 1, :])
@@ -500,15 +510,15 @@
 
 
 def body(positions, charges, counts, near_flags, far_flags, up_operator, down_operator):
-    column, row, tail, mirror, pick = (jnp.asarray(t) for t in tables())
+    column, row, tail, nodes, mirror, pick = (jnp.asarray(t) for t in tables())
     below, above = call(
         upward_kernel,
         [(33, 4, 128), (33, 4, 128)],
         [
             ((2 * SPAD, 16 * WIDE), BF16), ((WIDE, WIDE), F32), ((12, SPAD, WIDE), F32),
-            ((WIDE, WIDE), F32), ((1, 64, 128), F32),
+            ((1, 64, 128), F32),
         ],
-        "vvsvvvv", "upward", 6000, positions, charges, counts, up_operator, column, row, tail, vmem=59,
+        "vvsvvvvv", "upward", 6000, positions, charges, counts, up_operator, column, row, tail, nodes, vmem=59,
     )
     own = (shifted(above, "gz", -1), below, above, shifted(below, "gz", 1))
 
@@ -520,8 +530,9 @@
         parts += [v[:, one].reshape(4, 4, 128) for v in grid[1]]
         return jnp.concatenate(parts + blocks, axis=0)
 
-    ylo = shifted(to_y(2, 3), "gy", -1)
-    yhi = shifted(to_y(0, 0), "gy", 1)
+    up, down, far_flags, near_flags = lax.optimization_barrier((to_y(2, 3), to_y(0, 0), far_flags, near_flags))
+    ylo = shifted(up, "gy", -1)
+    yhi = shifted(down, "gy", 1)
     blocks = jnp.concatenate([ylo[48:51]] + blocks + [yhi[48:51]], axis=0)
 
     def to_x(low, one):
@@ -583,7 +594,7 @@
             ((WIDE, WIDE), F32), ((12, SPAD, WIDE), F32), ((20, SPAD, 128), F32), ((14, SPAD, 128), F32),
             ((WIDE, WIDE), F32), ((2, 128, 128), F32), ((16, 128), F32),
         ],
-        "svvvvvvvvvv", "last", 9000, counts, gathered, far, low, inner, high, positions, down_operator, column, row, tail,
+        "svvvvvvvvvvv", "last", 9000, counts, gathered, far, low, inner, high, positions, down_operator, column, row, tail, nodes,
     )
     return potential
 

time: 67.7 us -> 64.5 us (0.953)
  Pallas kernels: 35.7 us -> 32.9 us
  local copies, waits for them, and re-layouts: 3.43 us -> 2.71 us
    pallas_call x6, Pallas kernels: 35.7 us -> 32.9 us  [call(): pl.pallas_call(body, out_shape=[jax.ShapeDtypeStruct(s, F32) for s in out...]
    unnamed x68 -> x70, local copies, waits for them, and re-layouts: 1.91 us -> 1.18 us
  transfers between devices with their start and end apart: 11 -> 11, of which waited for: 3 -> 3; matrix products, arithmetic and copies ran while one was open for 2% -> 3% of each run, Pallas kernels for 28% -> 29%
where the time goes in v3:
time: 64.5 us; the launch traced here: 64.3 us
  Pallas kernels  32.9 us (51%)
  starting transfers between devices  23.5 us (36%)
  waiting for transfers between devices  4.11 us (6%)
  local copies, waits for them, and re-layouts  2.71 us (4%)
    pallas_call x6, Pallas kernels, call(): pl.pallas_call(body, out_shape=[jax.ShapeDtypeStruct(s, F32) for s in out...  32.9 us
    ppermute x11, starting transfers between devices, shifted(): lax.ppermute(array, axis, [((i + distance) % n, i) for i in range(n)])  23.5 us
    ppermute x11, waiting for transfers between devices, shifted(): lax.ppermute(array, axis, [((i + distance) % n, i) for i in range(n)])  4.11 us
  transfers between devices with their start and end apart: 11, of which 3 were waited for; matrix products, arithmetic and copies ran while one was open for 3% of the time, Pallas kernels for 29%

profile of v3, /device:TPU:1, one launch (start us, length us, event | category | flops | bytes accessed | tf_op | source)
XLA Modules:
  0.0 64.3 jit_solution(6129907238993080401)
XLA Ops:
  0.0 4.8 %upward.1 = (f32[33,4,128]{2,1,0:T(4,128)}, f32[33,4,128]{2,1,0:T(4,128)}) custom-call(f32[3,4,4,256]{3,2,1,0:T(4,128)} %pos.3, f32[4,4,256]{2,1,0:T(4,128)} %chg.1, s32[4,4,4]{2,1,0:T(4,128)} %counts.3, f32[152,152]{1,0:T(8,128)} %up.1, f32[3,160,128]{2,1,0:T(8,128)} %constant.19.clone.column, f32[8,256]{1,0:T(8,128)} %constant.20.clone.row, ...), custom_call_target="tpu_custom_call" | custom-call | flops 6000000000 | bytes 1048576 | tf_op jit(solution)/shard_map/upward/pallas_call | solution.py:495
  4.8 2.7 %collective-permute-start = (f32[33,4,128]{2,1,0:T(4,128)}, f32[33,4,128]{2,1,0:T(4,128)S(1)}, u32[]{:S(2)}, u32[]{:S(2)}) collective-permute-start(f32[33,4,128]{2,1,0:T(4,128)} %get-tuple-element.13.z2.refs_2_), channel_id=1, source_target_pairs={{7,0},{0,1},{1,2},{2,3},{3,4},{4,5},{5,6},{6,7},{15,8},{8,9},{9,10... | collective-permute-start | bytes 202760 | tf_op jit(solution)/shard_map/ppermute | solution.py:509
  7.5 0.0 copy-start
  7.5 0.0 copy-start.1
  7.5 0.6 collective-permute-start.1
  8.1 0.8 %fusion.8 = (f32[16,4,128]{2,1,0:T(4,128)S(1)}, f32[16,4,128]{2,1,0:T(4,128)S(1)}, f32[16,4,128]{2,1,0:T(4,128)S(1)}, f32[16,4,128]{2,1,0:T(4,128)S(1)}) fusion(f32[33,4,128]{2,1,0:T(4,128)} %get-tuple-element.13.z2.refs_2_, f32[33,4,128]{2,1,0:T(4,128)} %get-tuple-element.14.z1.refs_1_), kind=kLoop, calls=%fused_computation.108 | loop fusion | bytes 262144 | tf_op jit(solution)/shard_map/slice | solution.py:525
  8.9 0.0 copy-done
  8.9 0.0 copy-done.1
  9.0 0.1 pad.8.clone
  9.1 0.1 pad.6.clone
  9.1 0.0 collective-permute-done.z0.refs_0_
  9.2 2.2 %collective-permute-done.1.z3.refs_3_ = f32[33,4,128]{2,1,0:T(4,128)S(1)} collective-permute-done((f32[33,4,128]{2,1,0:T(4,128)}, f32[33,4,128]{2,1,0:T(4,128)S(1)}, u32[]{:S(2)}, u32[]{:S(2)}) %collective-permute-start.1) | collective-permute-done | bytes 67616 | tf_op jit(solution)/shard_map/ppermute | solution.py:509
  11.6 0.0 copy-start.12
  11.7 1.3 %collective-permute-start.2 = (f32[51,4,128]{2,1,0:T(4,128)S(1)}, f32[51,4,128]{2,1,0:T(4,128)S(1)}, u32[]{:S(2)}, u32[]{:S(2)}) collective-permute-start(f32[51,4,128]{2,1,0:T(4,128)S(1)} %get-tuple-element.15), channel_id=1, source_target_pairs={{24,0},{0,8},{8,16},{16,24},{25,1},{1,9},{9,17},{17,25},{26,2},{2,... | collective-permute-start | bytes 313352 | tf_op jit(solution)/shard_map/ppermute | solution.py:509
  13.0 1.5 %collective-permute-start.3 = (f32[51,4,128]{2,1,0:T(4,128)S(1)}, f32[51,4,128]{2,1,0:T(4,128)S(1)}, u32[]{:S(2)}, u32[]{:S(2)}) collective-permute-start(f32[51,4,128]{2,1,0:T(4,128)S(1)} %get-tuple-element.16), channel_id=1, source_target_pairs={{8,0},{16,8},{24,16},{0,24},{9,1},{17,9},{25,17},{1,25},{10,2},{18... | collective-permute-start | bytes 313352 | tf_op jit(solution)/shard_map/ppermute | solution.py:509
  14.4 0.0 copy-done.12
  14.4 0.1 fusion.11
  14.5 0.1 maximum_maximum_fusion
  14.6 0.0 copy-start.11
  14.6 0.2 copy.46
  14.8 0.7 %copy-done.11 = s32[343,4,4,4]{0,3,2,1:T(4,128)S(1)} copy-done((s32[343,4,4,4]{0,3,2,1:T(4,128)S(1)}, s32[343,4,4,4]{0,3,2,1:T(4,128)}, u32[]{:S(2)}) %copy-start.11) | copy-done | bytes 87832
  15.6 0.1 copy.45
  15.7 0.8 %collective-permute-done.2.ylo.refs_4_ = f32[51,4,128]{2,1,0:T(4,128)S(1)} collective-permute-done((f32[51,4,128]{2,1,0:T(4,128)S(1)}, f32[51,4,128]{2,1,0:T(4,128)S(1)}, u32[]{:S(2)}, u32[]{:S(2)}) %collective-permute-start.2) | collective-permute-done | bytes 104480 | tf_op jit(solution)/shard_map/ppermute | solution.py:509
  16.5 0.0 collective-permute-done.3.yhi.refs_5_
  17.0 2.7 %collective-permute-start.4 = (f32[97,4,128]{2,1,0:T(4,128)S(1)}, f32[97,4,128]{2,1,0:T(4,128)S(1)}, u32[]{:S(2)}, u32[]{:S(2)}) collective-permute-start(f32[97,4,128]{2,1,0:T(4,128)S(1)} %get-tuple-element.17), channel_id=1, source_target_pairs={{224,0},{0,32},{32,64},{64,96},{96,128},{128,160},{160,192},{192,2... | collective-permute-start | bytes 595976 | tf_op jit(solution)/shard_map/ppermute | solution.py:509
  19.7 4.0 %collective-permute-start.5 = (f32[97,4,128]{2,1,0:T(4,128)S(1)}, f32[97,4,128]{2,1,0:T(4,128)S(1)}, u32[]{:S(2)}, u32[]{:S(2)}) collective-permute-start(f32[97,4,128]{2,1,0:T(4,128)S(1)} %get-tuple-element.18), channel_id=1, source_target_pairs={{32,0},{64,32},{96,64},{128,96},{160,128},{192,160},{224,192},{0,2... | collective-permute-start | bytes 595976 | tf_op jit(solution)/shard_map/ppermute | solution.py:509
  23.7 0.0 copy-start.5
  23.7 6.3 %near.4.near12 = f32[8,256]{1,0:T(8,128)S(1)} custom-call(f32[33,4,128]{2,1,0:T(4,128)S(1)} %collective-permute-done.z0.refs_0_, f32[33,4,128]{2,1,0:T(4,128)S(1)} %copy-done, f32[33,4,128]{2,1,0:T(4,128)S(1)} %copy-done.1, f32[33,4,128]{2,1,0:T(4,128)S(1)} %collective-permute-done.1.z3.refs_3_, f32[51,4,128]{2,1,0:T(4,128)S(1)} %collective-permute-done.2.ylo.refs_4_, ...), custom_call_target="tpu_custom_call" | custom-call | flops 6000000000 | bytes 1048576 | tf_op jit(solution)/shard_map/near/pallas_call | solution.py:495
  30.0 0.0 copy-start.6
  30.0 0.0 collective-permute-done.4.xlo.refs_6_
  30.1 0.0 collective-permute-done.5.xhi.refs_7_
  30.1 2.4 %collective-permute-start.6 = (f32[27,2,128]{2,1,0:T(2,128)S(1)}, f32[27,2,128]{2,1,0:T(2,128)S(1)}, u32[]{:S(2)}, u32[]{:S(2)}) collective-permute-start(f32[27,2,128]{2,1,0:T(2,128)S(1)} %slice.560), channel_id=1, source_target_pairs={{96,0},{128,32},{160,64},{192,96},{224,128},{0,160},{32,192},{64,2... | collective-permute-start | bytes 82952 | tf_op jit(solution)/shard_map/ppermute | solution.py:509
  32.5 0.0 copy-start.8
  32.5 0.0 copy-start.9
  32.5 1.2 %collective-permute-start.7 = (f32[18,2,128]{2,1,0:T(2,128)S(1)}, f32[18,2,128]{2,1,0:T(2,128)S(1)}, u32[]{:S(2)}, u32[]{:S(2)}) collective-permute-start(f32[18,2,128]{2,1,0:T(2,128)S(1)} %slice.561), channel_id=1, source_target_pairs={{160,0},{192,32},{224,64},{0,96},{32,128},{64,160},{96,192},{128,2... | collective-permute-start | bytes 55304 | tf_op jit(solution)/shard_map/ppermute | solution.py:509
  33.7 0.0 copy-done.5
  33.7 0.0 copy-done.6
  33.7 0.0 copy-done.8
  33.7 0.0 copy-done.9
  33.7 6.2 %far.1 = f32[64,256]{1,0:T(8,128)S(1)} custom-call(f32[33,4,128]{2,1,0:T(4,128)S(1)} %collective-permute-done.z0.refs_0_, f32[33,4,128]{2,1,0:T(4,128)S(1)} %copy-done, f32[33,4,128]{2,1,0:T(4,128)S(1)} %copy-done.1, f32[33,4,128]{2,1,0:T(4,128)S(1)} %collective-permute-done.1.z3.refs_3_, f32[51,4,128]{2,1,0:T(4,128)S(1)} %collective-permute-done.2.ylo.refs_4_, ...), custom_call_target="tpu_custom_call" | custom-call | flops 7000000000 | bytes 1048576 | tf_op jit(solution)/shard_map/far/pallas_call | solution.py:495
  39.9 0.0 collective-permute-done.7
  40.0 0.0 collective-permute-done.6
  40.0 2.2 %collective-permute-start.8 = (f32[8,3,2,128]{3,2,1,0:T(2,128)S(1)}, f32[8,3,2,128]{3,2,1,0:T(2,128)S(1)}, u32[]{:S(2)}, u32[]{:S(2)}) collective-permute-start(f32[8,3,2,128]{3,2,1,0:T(2,128)S(1)} %slice_bitcast_fusion), channel_id=1, source_target_pairs={{16,0},{24,8},{0,16},{8,24},{17,1},{25,9},{1,17},{9,25},{18,2},{26... | collective-permute-start | bytes 73736 | tf_op jit(solution)/shard_map/ppermute | solution.py:509
  42.2 3.2 %near.5.near3 = f32[4,256]{1,0:T(4,128)S(1)} custom-call(f32[33,4,128]{2,1,0:T(4,128)S(1)} %collective-permute-done.z0.refs_0_, f32[33,4,128]{2,1,0:T(4,128)S(1)} %copy-done, f32[33,4,128]{2,1,0:T(4,128)S(1)} %copy-done.1, f32[33,4,128]{2,1,0:T(4,128)S(1)} %collective-permute-done.1.z3.refs_3_, f32[51,4,128]{2,1,0:T(4,128)S(1)} %collective-permute-done.2.ylo.refs_4_, ...), custom_call_target="tpu_custom_call" | custom-call | flops 3000000000 | bytes 1048576 | tf_op jit(solution)/shard_map/near/pallas_call | solution.py:495
  45.5 0.0 collective-permute-done.8
  45.6 4.4 %collective-permute-start.9 = (f32[8,4,3,2,128]{4,3,2,1,0:T(2,128)S(1)}, f32[8,4,3,2,128]{4,3,2,1,0:T(2,128)S(1)}, u32[]{:S(2)}, u32[]{:S(2)}) collective-permute-start(f32[8,4,3,2,128]{4,3,2,1,0:T(2,128)S(1)} %pad_maximum_fusion.1), channel_id=1, source_target_pairs={{3,0},{4,1},{5,2},{6,3},{7,4},{0,5},{1,6},{2,7},{11,8},{12,9},{13,... | collective-permute-start | bytes 294920 | tf_op jit(solution)/shard_map/ppermute | solution.py:509
  49.9 0.6 collective-permute-start.10
  50.6 3.2 %near.3.near0 = f32[4,256]{1,0:T(4,128)S(1)} custom-call(f32[33,4,128]{2,1,0:T(4,128)S(1)} %collective-permute-done.z0.refs_0_, f32[33,4,128]{2,1,0:T(4,128)S(1)} %copy-done, f32[33,4,128]{2,1,0:T(4,128)S(1)} %copy-done.1, f32[33,4,128]{2,1,0:T(4,128)S(1)} %collective-permute-done.1.z3.refs_3_, f32[51,4,128]{2,1,0:T(4,128)S(1)} %collective-permute-done.2.ylo.refs_4_, ...), custom_call_target="tpu_custom_call" | custom-call | flops 3000000000 | bytes 1048576 | tf_op jit(solution)/shard_map/near/pallas_call | solution.py:495
  53.8 0.0 copy-start.2
  53.8 0.0 copy-start.3
  53.8 0.0 copy-start.4
  53.8 0.0 copy-start.7
  53.8 0.0 copy-start.10
  53.9 1.1 %collective-permute-done.10 = f32[8,4,2,2,128]{4,3,2,1,0:T(2,128)S(1)} collective-permute-done((f32[8,4,2,2,128]{4,3,2,1,0:T(2,128)S(1)}, f32[8,4,2,2,128]{4,3,2,1,0:T(2,128)S(1)}, u32[]{:S(2)}, u32[]{:S(2)}) %collective-permute-start.10) | collective-permute-done | bytes 65568 | tf_op jit(solution)/shard_map/ppermute | solution.py:509
  54.9 0.0 collective-permute-done.9
  54.9 0.1 pad_maximum_fusion
  55.0 0.0 copy-done.2
  55.0 0.0 copy-done.3
  55.1 0.0 copy-done.4
  55.1 0.0 copy-done.7
  55.1 0.0 copy-done.10
  55.1 9.2 %last.1 = f32[4,4,256]{2,1,0:T(4,128)} custom-call(s32[4,4,4]{2,1,0:T(4,128)S(1)} %copy-done.4, f32[256,2,128]{2,1,0:T(2,128)S(1)} %bitcast.110, f32[64,256]{1,0:T(8,128)S(1)} %far.1, f32[4,256]{1,0:T(4,128)S(1)} %near.3.near0, f32[8,256]{1,0:T(8,128)S(1)} %near.4.near12, f32[4,256]{1,0:T(4,128)S(1)} %near.5.near3, f32[3,4,4,256]{3,2,1,0:T(4,128)S(1)} %copy-done.3, ...), custom_call_target="tpu_custom_call" | custom-call | flops 8999999488 | bytes 1048576 | tf_op jit(solution)/shard_map/last/pallas_call | solution.py:495
  (77 shorter events, 0.8 us)
Async XLA Ops:
  4.8 4.4 %collective-permute-start = (f32[33,4,128]{2,1,0:T(4,128)}, f32[33,4,128]{2,1,0:T(4,128)S(1)}, u32[]{:S(2)}, u32[]{:S(2)}) collective-permute-start(f32[33,4,128]{2,1,0:T(4,128)} %get-tuple-element.13.z2.refs_2_), channel_id=1, source_target_pairs={{7,0},{0,1},{1,2},{2,3},{3,4},{4,5},{5,6},{6,7},{15,8},{8,9},{9,10... | collective-permute-start | bytes 202760 | tf_op jit(solution)/shard_map/ppermute | solution.py:509
  7.5 1.4 %copy-start = (f32[33,4,128]{2,1,0:T(4,128)S(1)}, f32[33,4,128]{2,1,0:T(4,128)}, u32[]{:S(2)}) copy-start(f32[33,4,128]{2,1,0:T(4,128)} %get-tuple-element.14.z1.refs_1_) | copy-start | bytes 202756
  7.5 1.4 %copy-start.1 = (f32[33,4,128]{2,1,0:T(4,128)S(1)}, f32[33,4,128]{2,1,0:T(4,128)}, u32[]{:S(2)}) copy-start(f32[33,4,128]{2,1,0:T(4,128)} %get-tuple-element.13.z2.refs_2_) | copy-start | bytes 202756
  7.5 3.9 %collective-permute-start.1 = (f32[33,4,128]{2,1,0:T(4,128)}, f32[33,4,128]{2,1,0:T(4,128)S(1)}, u32[]{:S(2)}, u32[]{:S(2)}) collective-permute-start(f32[33,4,128]{2,1,0:T(4,128)} %get-tuple-element.14.z1.refs_1_), channel_id=1, source_target_pairs={{1,0},{2,1},{3,2},{4,3},{5,4},{6,5},{7,6},{0,7},{9,8},{10,9},{11,1... | collective-permute-start | bytes 202760 | tf_op jit(solution)/shard_map/ppermute | solution.py:509
  11.6 2.8 %copy-start.12 = (s32[26,4,4,4]{0,3,2,1:T(4,128)S(1)}, s32[26,4,4,4]{0,3,2,1:T(4,128)}, u32[]{:S(2)}) copy-start(s32[26,4,4,4]{0,3,2,1:T(4,128)} %param.16) | copy-start | bytes 19972
  11.7 4.8 %collective-permute-start.2 = (f32[51,4,128]{2,1,0:T(4,128)S(1)}, f32[51,4,128]{2,1,0:T(4,128)S(1)}, u32[]{:S(2)}, u32[]{:S(2)}) collective-permute-start(f32[51,4,128]{2,1,0:T(4,128)S(1)} %get-tuple-element.15), channel_id=1, source_target_pairs={{24,0},{0,8},{8,16},{16,24},{25,1},{1,9},{9,17},{17,25},{26,2},{2,... | collective-permute-start | bytes 313352 | tf_op jit(solution)/shard_map/ppermute | solution.py:509
  13.0 3.5 %collective-permute-start.3 = (f32[51,4,128]{2,1,0:T(4,128)S(1)}, f32[51,4,128]{2,1,0:T(4,128)S(1)}, u32[]{:S(2)}, u32[]{:S(2)}) collective-permute-start(f32[51,4,128]{2,1,0:T(4,128)S(1)} %get-tuple-element.16), channel_id=1, source_target_pairs={{8,0},{16,8},{24,16},{0,24},{9,1},{17,9},{25,17},{1,25},{10,2},{18... | collective-permute-start | bytes 313352 | tf_op jit(solution)/shard_map/ppermute | solution.py:509
  14.6 0.9 %copy-start.11 = (s32[343,4,4,4]{0,3,2,1:T(4,128)S(1)}, s32[343,4,4,4]{0,3,2,1:T(4,128)}, u32[]{:S(2)}) copy-start(s32[343,4,4,4]{0,3,2,1:T(4,128)} %param.17) | copy-start | bytes 263428
  17.0 13.0 %collective-permute-start.4 = (f32[97,4,128]{2,1,0:T(4,128)S(1)}, f32[97,4,128]{2,1,0:T(4,128)S(1)}, u32[]{:S(2)}, u32[]{:S(2)}) collective-permute-start(f32[97,4,128]{2,1,0:T(4,128)S(1)} %get-tuple-element.17), channel_id=1, source_target_pairs={{224,0},{0,32},{32,64},{64,96},{96,128},{128,160},{160,192},{192,2... | collective-permute-start | bytes 595976 | tf_op jit(solution)/shard_map/ppermute | solution.py:509
  19.7 10.4 %collective-permute-start.5 = (f32[97,4,128]{2,1,0:T(4,128)S(1)}, f32[97,4,128]{2,1,0:T(4,128)S(1)}, u32[]{:S(2)}, u32[]{:S(2)}) collective-permute-start(f32[97,4,128]{2,1,0:T(4,128)S(1)} %get-tuple-element.18), channel_id=1, source_target_pairs={{32,0},{64,32},{96,64},{128,96},{160,128},{192,160},{224,192},{0,2... | collective-permute-start | bytes 595976 | tf_op jit(solution)/shard_map/ppermute | solution.py:509
  23.7 10.0 %copy-start.5 = (bf16[512,384]{1,0:T(8,128)(2,1)S(1)}, bf16[512,384]{1,0:T(8,128)(2,1)}, u32[]{:S(2)}) copy-start(bf16[512,384]{1,0:T(8,128)(2,1)} %constant.24.clone.pick) | copy-start | bytes 1179652
  30.0 3.8 %copy-start.6 = (f32[3,160,128]{2,1,0:T(8,128)S(1)}, f32[3,160,128]{2,1,0:T(8,128)}, u32[]{:S(2)}) copy-start(f32[3,160,128]{2,1,0:T(8,128)} %constant.19.clone.column) | copy-start | bytes 737284
  30.1 9.9 %collective-permute-start.6 = (f32[27,2,128]{2,1,0:T(2,128)S(1)}, f32[27,2,128]{2,1,0:T(2,128)S(1)}, u32[]{:S(2)}, u32[]{:S(2)}) collective-permute-start(f32[27,2,128]{2,1,0:T(2,128)S(1)} %slice.560), channel_id=1, source_target_pairs={{96,0},{128,32},{160,64},{192,96},{224,128},{0,160},{32,192},{64,2... | collective-permute-start | bytes 82952 | tf_op jit(solution)/shard_map/ppermute | solution.py:509
  32.5 1.3 %copy-start.8 = (f32[8,256]{1,0:T(8,128)S(1)}, f32[8,256]{1,0:T(8,128)}, u32[]{:S(2)}) copy-start(f32[8,256]{1,0:T(8,128)} %constant.20.clone.row) | copy-start | bytes 24580
  32.5 1.3 %copy-start.9 = (s32[8,256]{1,0:T(8,128)S(1)}, s32[8,256]{1,0:T(8,128)}, u32[]{:S(2)}) copy-start(s32[8,256]{1,0:T(8,128)} %constant.23.clone.mirror) | copy-start | bytes 24580
  32.5 7.5 %collective-permute-start.7 = (f32[18,2,128]{2,1,0:T(2,128)S(1)}, f32[18,2,128]{2,1,0:T(2,128)S(1)}, u32[]{:S(2)}, u32[]{:S(2)}) collective-permute-start(f32[18,2,128]{2,1,0:T(2,128)S(1)} %slice.561), channel_id=1, source_target_pairs={{160,0},{192,32},{224,64},{0,96},{32,128},{64,160},{96,192},{128,2... | collective-permute-start | bytes 55304 | tf_op jit(solution)/shard_map/ppermute | solution.py:509
  40.0 5.4 %collective-permute-start.8 = (f32[8,3,2,128]{3,2,1,0:T(2,128)S(1)}, f32[8,3,2,128]{3,2,1,0:T(2,128)S(1)}, u32[]{:S(2)}, u32[]{:S(2)}) collective-permute-start(f32[8,3,2,128]{3,2,1,0:T(2,128)S(1)} %slice_bitcast_fusion), channel_id=1, source_target_pairs={{16,0},{24,8},{0,16},{8,24},{17,1},{25,9},{1,17},{9,25},{18,2},{26... | collective-permute-start | bytes 73736 | tf_op jit(solution)/shard_map/ppermute | solution.py:509
  45.6 9.4 %collective-permute-start.9 = (f32[8,4,3,2,128]{4,3,2,1,0:T(2,128)S(1)}, f32[8,4,3,2,128]{4,3,2,1,0:T(2,128)S(1)}, u32[]{:S(2)}, u32[]{:S(2)}) collective-permute-start(f32[8,4,3,2,128]{4,3,2,1,0:T(2,128)S(1)} %pad_maximum_fusion.1), channel_id=1, source_target_pairs={{3,0},{4,1},{5,2},{6,3},{7,4},{0,5},{1,6},{2,7},{11,8},{12,9},{13,... | collective-permute-start | bytes 294920 | tf_op jit(solution)/shard_map/ppermute | solution.py:509
  49.9 5.0 %collective-permute-start.10 = (f32[8,4,2,2,128]{4,3,2,1,0:T(2,128)S(1)}, f32[8,4,2,2,128]{4,3,2,1,0:T(2,128)S(1)}, u32[]{:S(2)}, u32[]{:S(2)}) collective-permute-start(f32[8,4,2,2,128]{4,3,2,1,0:T(2,128)S(1)} %fusion), channel_id=1, source_target_pairs={{5,0},{6,1},{7,2},{0,3},{1,4},{2,5},{3,6},{4,7},{13,8},{14,9},{15,... | collective-permute-start | bytes 196616 | tf_op jit(solution)/shard_map/ppermute | solution.py:509
  53.8 1.2 %copy-start.2 = (f32[152,152]{1,0:T(8,128)S(1)}, f32[152,152]{1,0:T(8,128)}, u32[]{:S(2)}) copy-start(f32[152,152]{1,0:T(8,128)} %down.1) | copy-start | bytes 277252
  53.8 1.2 %copy-start.3 = (f32[3,4,4,256]{3,2,1,0:T(4,128)S(1)}, f32[3,4,4,256]{3,2,1,0:T(4,128)}, u32[]{:S(2)}) copy-start(f32[3,4,4,256]{3,2,1,0:T(4,128)} %pos.3) | copy-start | bytes 147460
  53.8 1.2 %copy-start.4 = (s32[4,4,4]{2,1,0:T(4,128)S(1)}, s32[4,4,4]{2,1,0:T(4,128)}, u32[]{:S(2)}) copy-start(s32[4,4,4]{2,1,0:T(4,128)} %counts.3) | copy-start | bytes 772
  53.8 1.2 %copy-start.7 = (bf16[160,128]{1,0:T(8,128)(2,1)S(1)}, bf16[160,128]{1,0:T(8,128)(2,1)}, u32[]{:S(2)}) copy-start(bf16[160,128]{1,0:T(8,128)(2,1)} %constant.22.clone.nodes) | copy-start | bytes 122884
  53.8 1.2 %copy-start.10 = (f32[8,128]{1,0:T(8,128)S(1)}, f32[8,128]{1,0:T(8,128)}, u32[]{:S(2)}) copy-start(f32[8,128]{1,0:T(8,128)} %constant.21.clone.tail) | copy-start | bytes 12292

commit v4 on v3

--- a/solution.py
+++ b/solution.py
@@ -309,17 +309,18 @@
     out[...] = result
 
 
-def near_kernel(first, planes, *refs):
+def near_kernel(planes, first_x, count_x, *refs):
     *halo, flags, out, lines, sources, points, shifted, sums = refs
     refs = (halo[0:4], *halo[4:])
     if len(halo) == 6:
         refs = (*refs, None, None)
     z1, z2 = halo[1], halo[2]
-    count = (planes + 2) * 6
-    for x in range(planes + 2):
+    targets = [(x, y) for x in planes for y in range(4)]
+    count = count_x * 6
+    for x in range(count_x):
         for y in range(6):
             for pair in range(4):
-                record = particle_record(refs, x + first - 1, y - 1, pair)
+                record = particle_record(refs, x + first_x, y - 1, pair)
                 for c in range(4):
                     lines[c, x * 6 + y : x * 6 + y + 1, pair * 128 : pair * 128 + 128] = record[c : c + 1]
     for c in range(4):
@@ -335,9 +336,8 @@
     block = ((iota((WIDE, WIDE), 0) >> 6) == (iota((WIDE, WIDE), 1) >> 6)).astype(F32).astype(BF16)
     zone = iota((32, WIDE), 1) >> 6
     step_y = (iota((9, WIDE), 0) // 3 - 1).astype(F32)
-    for i in range(planes * 4):
-        r = first * 4 + i
-        x, y = i // 4, i % 4
+    for i, (x, y) in enumerate(targets):
+        r = x * 4 + y
         pieces = []
         for c in range(3):
             v = jnp.concatenate([z1[16 + r, c : c + 1, :], z2[16 + r, c : c + 1, :]], axis=1)
@@ -353,12 +353,12 @@
             square = square + v * v
             points[i, c] = -2.0 * v
         points[i, 3] = square
-        f = flags[x + first, y]
+        f = flags[x, y]
         lists = jnp.zeros((32, WIDE), F32)
         for z in range(4):
             lists = jnp.where(zone == z, f[:, z : z + 1], lists)
         for ex in range(3):
-            at = ((x + ex) * 6 + y) * 3
+            at = ((x - 1 + ex - first_x) * 6 + y) * 3
             here = slice(ex * 9, ex * 9 + 9)
             sx, sy, sz, q = (
                 jnp.concatenate([sources[c, half, at : at + 9, :] for half in range(2)], axis=1) for c in range(4)
@@ -385,8 +385,8 @@
             sums[i, :, lanes] = acc
         return carry
 
-    lax.fori_loop(0, planes * 4, one_row, 0)
-    for i in range(planes * 4):
+    lax.fori_loop(0, len(targets), one_row, 0)
+    for i in range(len(targets)):
         hi, lo = split2(sums[i])
         both = jnp.dot(jnp.concatenate([hi, lo], axis=0), block, preferred_element_type=F32)
         picked = jnp.where(same, both[0:64] + both[64:128], 0.0)
@@ -394,7 +394,7 @@
 
 
 def last_kernel(
-    counts, gathered, far, near0, near12, near3, pos, down, column, row, tail, nodes,
+    counts, gathered, far, near_in, near_out, pos, down, column, row, tail, nodes,
     out, operator, squares, offsets, tails, acc, checks, ends,
 ):
     padded_operator(down, operator)
@@ -486,7 +486,7 @@
             px, py, pz = (pos[c, x, y : y + 1, :] for c in range(3))
             k = surface_terms(px, py, pz, nodes[...])
             line = jnp.sum(k * (wide[0:SPAD] + wide[SPAD : 2 * SPAD]), axis=0, keepdims=True)
-            near, i = (near0, r) if x == 0 else (near3, r - 12) if x == 3 else (near12, r - 4)
+            near, i = (near_in, r - 4) if x in (1, 2) else (near_out, r % 8)
             out[x, y : y + 1, :] = occupied_row(counts, x, y) * (line + near[i : i + 1, :])
 
 
@@ -530,10 +530,14 @@
         parts += [v[:, one].reshape(4, 4, 128) for v in grid[1]]
         return jnp.concatenate(parts + blocks, axis=0)
 
-    up, down, far_flags, near_flags = lax.optimization_barrier((to_y(2, 3), to_y(0, 0), far_flags, near_flags))
+    middle = jnp.concatenate(blocks, axis=0)
+    up, down, middle, far_flags, near_flags = lax.optimization_barrier(
+        (to_y(2, 3), to_y(0, 0), middle, far_flags, near_flags)
+    )
     ylo = shifted(up, "gy", -1)
     yhi = shifted(down, "gy", 1)
-    blocks = jnp.concatenate([ylo[48:51]] + blocks + [yhi[48:51]], axis=0)
+    far_blocks = shifted(middle, "gy", 2)
+    blocks = jnp.concatenate([ylo[48:51], middle, yhi[48:51], far_blocks], axis=0)
 
     def to_x(low, one):
         parts = []
@@ -550,10 +554,9 @@
     xhi = shifted(down, "gx", 1)
     halo = (*own, ylo, yhi, xlo, xhi)
 
-    held = jnp.concatenate([xlo[88:97], blocks, xhi[88:97]], axis=0)[:, 0:2]
-    held = jnp.concatenate([held, shifted(held, "gx", 3), shifted(held[9:27], "gx", -3)], axis=0)
-    held = held.reshape(8, 3, 3, 2, 128)
-    held = jnp.concatenate([held, shifted(held[:, 1], "gy", 2)[:, None]], axis=1)
+    held = jnp.concatenate([xlo[88:100], blocks, xhi[88:100]], axis=0)[:, 0:2]
+    held = jnp.concatenate([held, shifted(held, "gx", 3), shifted(held[12:36], "gx", -3)], axis=0)
+    held = held.reshape(8, 4, 3, 2, 128)
     forward, back = shifted(held, "gz", 3), shifted(held[:, :, 1:3], "gz", -3)
     gathered = jnp.concatenate([held, forward, back], axis=2).reshape(256, 2, 128)
 
@@ -573,20 +576,20 @@
     listed = jnp.concatenate([near_flags[0:13], centre, near_flags[13:26], jnp.zeros((5, *near_flags.shape[1:]), F32)], axis=0)
     listed = listed.transpose(1, 2, 0, 3)
 
-    def near(first, planes, halo):
-        count = (planes + 2) * 6
+    def near(planes, first_x, count_x, halo):
+        count, here = count_x * 6, len(planes) * 4
         (result,) = call(
-            functools.partial(near_kernel, first, planes),
-            [(planes * 4, WIDE)],
+            functools.partial(near_kernel, planes, first_x, count_x),
+            [(here, WIDE)],
             [
-                ((4, count + -count % 8, 512), F32), ((4, 2, count * 3, 128), F32), ((planes * 4, 4, 64, WIDE), F32),
-                ((planes * 4, 5, 32, WIDE), F32), ((planes * 4, 64, WIDE), F32),
+                ((4, count + -count % 8, 512), F32), ((4, 2, count * 3, 128), F32), ((here, 4, 64, WIDE), F32),
+                ((here, 5, 32, WIDE), F32), ((here, 64, WIDE), F32),
             ],
-            "v" * (len(halo) + 1), "near", 3000 * planes, *halo, listed,
+            "v" * (len(halo) + 1), "near", 6000, *halo, listed,
         )
         return result
 
-    inner, low, high = near(1, 2, halo[0:6]), near(0, 1, halo), near(3, 1, halo)
+    inner, outer = near((1, 2), 0, 4, halo[0:6]), near((0, 3), -1, 6, halo)
     (potential,) = call(
         last_kernel,
         [(4, 4, WIDE)],
@@ -594,7 +597,7 @@
             ((WIDE, WIDE), F32), ((12, SPAD, WIDE), F32), ((20, SPAD, 128), F32), ((14, SPAD, 128), F32),
             ((WIDE, WIDE), F32), ((2, 128, 128), F32), ((16, 128), F32),
         ],
-        "svvvvvvvvvvv", "last", 9000, counts, gathered, far, low, inner, high, positions, down_operator, column, row, tail, nodes,
+        "svvvvvvvvvv", "last", 9000, counts, gathered, far, inner, outer, positions, down_operator, column, row, tail, nodes,
     )
     return potential
 

time: 64.5 us -> 61.8 us (0.958)
  starting transfers between devices: 23.5 us -> 21.3 us
  waiting for transfers between devices: 4.11 us -> 3.05 us
  local copies, waits for them, and re-layouts: 2.71 us -> 3.42 us
    ppermute x11, starting transfers between devices: 23.5 us -> 21.3 us  [shifted(): lax.ppermute(array, axis, [((i + distance) % n, i) for i in range(n)])]
    ppermute x11, waiting for transfers between devices: 4.11 us -> 3.05 us  [shifted(): lax.ppermute(array, axis, [((i + distance) % n, i) for i in range(n)])]
    unnamed x70 -> x66, local copies, waits for them, and re-layouts: 1.18 us -> 1.86 us
    pallas_call x6 -> x5, Pallas kernels: 32.9 us -> 32.8 us  [call(): pl.pallas_call(body, out_shape=[jax.ShapeDtypeStruct(s, F32) for s in out...]
  transfers between devices with their start and end apart: 11 -> 11, of which waited for: 3 -> 2; matrix products, arithmetic and copies ran while one was open for 3% -> 3% of each run, Pallas kernels for 29% -> 31%
where the time goes in v4:
time: 61.8 us; the launch traced here: 61.5 us
  Pallas kernels  32.8 us (53%)
  starting transfers between devices  21.3 us (34%)
  local copies, waits for them, and re-layouts  3.42 us (6%)
  waiting for transfers between devices  3.05 us (5%)
    pallas_call x5, Pallas kernels, call(): pl.pallas_call(body, out_shape=[jax.ShapeDtypeStruct(s, F32) for s in out...  32.8 us
    ppermute x11, starting transfers between devices, shifted(): lax.ppermute(array, axis, [((i + distance) % n, i) for i in range(n)])  21.3 us
    ppermute x11, waiting for transfers between devices, shifted(): lax.ppermute(array, axis, [((i + distance) % n, i) for i in range(n)])  3.05 us
    unnamed x66, local copies, waits for them, and re-layouts  1.86 us
  transfers between devices with their start and end apart: 11, of which 2 were waited for; matrix products, arithmetic and copies ran while one was open for 3% of the time, Pallas kernels for 31%

profile of v4, /device:TPU:1, one launch (start us, length us, event | category | flops | bytes accessed | tf_op | source)
XLA Modules:
  0.0 61.5 jit_solution(2148441012065885773)
XLA Ops:
  0.0 4.8 %upward.1 = (f32[33,4,128]{2,1,0:T(4,128)}, f32[33,4,128]{2,1,0:T(4,128)}) custom-call(f32[3,4,4,256]{3,2,1,0:T(4,128)} %pos.3, f32[4,4,256]{2,1,0:T(4,128)} %chg.1, s32[4,4,4]{2,1,0:T(4,128)} %counts.3, f32[152,152]{1,0:T(8,128)} %up.1, f32[3,160,128]{2,1,0:T(8,128)} %constant.19.clone.column, f32[8,256]{1,0:T(8,128)} %constant.20.clone.row, ...), custom_call_target="tpu_custom_call" | custom-call | flops 6000000000 | bytes 1048576 | tf_op jit(solution)/shard_map/upward/pallas_call | solution.py:495
  4.8 2.7 %collective-permute-start = (f32[33,4,128]{2,1,0:T(4,128)}, f32[33,4,128]{2,1,0:T(4,128)S(1)}, u32[]{:S(2)}, u32[]{:S(2)}) collective-permute-start(f32[33,4,128]{2,1,0:T(4,128)} %get-tuple-element.14.z2.refs_2_), channel_id=1, source_target_pairs={{7,0},{0,1},{1,2},{2,3},{3,4},{4,5},{5,6},{6,7},{15,8},{8,9},{9,10... | collective-permute-start | bytes 202760 | tf_op jit(solution)/shard_map/ppermute | solution.py:509
  7.5 0.0 copy-start
  7.5 0.0 copy-start.1
  7.5 0.6 collective-permute-start.1
  8.1 0.8 %fusion.10 = (f32[16,4,128]{2,1,0:T(4,128)S(1)}, f32[16,4,128]{2,1,0:T(4,128)S(1)}, f32[16,4,128]{2,1,0:T(4,128)S(1)}, f32[16,4,128]{2,1,0:T(4,128)S(1)}) fusion(f32[33,4,128]{2,1,0:T(4,128)} %get-tuple-element.14.z2.refs_2_, f32[33,4,128]{2,1,0:T(4,128)} %get-tuple-element.15.z1.refs_1_), kind=kLoop, calls=%fused_computation.103 | loop fusion | bytes 262144 | tf_op jit(solution)/shard_map/slice | solution.py:525
  8.9 0.0 copy-done
  8.9 0.0 copy-done.1
  9.0 0.1 pad.8.clone
  9.1 0.1 pad.6.clone
  9.1 0.0 collective-permute-done.z0.refs_0_
  9.2 2.2 %collective-permute-done.1.z3.refs_3_ = f32[33,4,128]{2,1,0:T(4,128)S(1)} collective-permute-done((f32[33,4,128]{2,1,0:T(4,128)}, f32[33,4,128]{2,1,0:T(4,128)S(1)}, u32[]{:S(2)}, u32[]{:S(2)}) %collective-permute-start.1) | collective-permute-done | bytes 67616 | tf_op jit(solution)/shard_map/ppermute | solution.py:509
  11.6 0.0 copy-start.12
  11.7 1.3 %collective-permute-start.2 = (f32[51,4,128]{2,1,0:T(4,128)S(1)}, f32[51,4,128]{2,1,0:T(4,128)S(1)}, u32[]{:S(2)}, u32[]{:S(2)}) collective-permute-start(f32[51,4,128]{2,1,0:T(4,128)S(1)} %get-tuple-element.16), channel_id=1, source_target_pairs={{24,0},{0,8},{8,16},{16,24},{25,1},{1,9},{9,17},{17,25},{26,2},{2,... | collective-permute-start | bytes 313352 | tf_op jit(solution)/shard_map/ppermute | solution.py:509
  13.0 1.5 %collective-permute-start.3 = (f32[51,4,128]{2,1,0:T(4,128)S(1)}, f32[51,4,128]{2,1,0:T(4,128)S(1)}, u32[]{:S(2)}, u32[]{:S(2)}) collective-permute-start(f32[51,4,128]{2,1,0:T(4,128)S(1)} %get-tuple-element.17), channel_id=1, source_target_pairs={{8,0},{16,8},{24,16},{0,24},{9,1},{17,9},{25,17},{1,25},{10,2},{18... | collective-permute-start | bytes 313352 | tf_op jit(solution)/shard_map/ppermute | solution.py:509
  14.4 1.5 %collective-permute-start.4 = (f32[3,4,128]{2,1,0:T(4,128)S(1)}, f32[3,4,128]{2,1,0:T(4,128)S(1)}, u32[]{:S(2)}, u32[]{:S(2)}) collective-permute-start(f32[3,4,128]{2,1,0:T(4,128)S(1)} %pad_maximum_fusion.10), channel_id=1, source_target_pairs={{16,0},{24,8},{0,16},{8,24},{17,1},{25,9},{1,17},{9,25},{18,2},{26... | collective-permute-start | bytes 18440 | tf_op jit(solution)/shard_map/ppermute | solution.py:509
  16.0 0.0 copy-done.12
  16.0 0.1 fusion.13
  16.1 0.1 maximum_maximum_fusion
  16.2 0.0 copy-start.11
  16.2 0.2 copy.43
  16.4 0.7 %copy-done.11 = s32[343,4,4,4]{0,3,2,1:T(4,128)S(1)} copy-done((s32[343,4,4,4]{0,3,2,1:T(4,128)S(1)}, s32[343,4,4,4]{0,3,2,1:T(4,128)}, u32[]{:S(2)}) %copy-start.11) | copy-done | bytes 87832
  17.1 0.1 copy.42
  17.3 0.0 collective-permute-done.2.ylo.refs_4_
  17.3 0.0 collective-permute-done.3.yhi.refs_5_
  17.8 0.7 %collective-permute-done.4 = f32[3,4,128]{2,1,0:T(4,128)S(1)} collective-permute-done((f32[3,4,128]{2,1,0:T(4,128)S(1)}, f32[3,4,128]{2,1,0:T(4,128)S(1)}, u32[]{:S(2)}, u32[]{:S(2)}) %collective-permute-start.4) | collective-permute-done | bytes 6176 | tf_op jit(solution)/shard_map/ppermute | solution.py:509
  18.6 1.6 %collective-permute-start.5 = (f32[100,4,128]{2,1,0:T(4,128)S(1)}, f32[100,4,128]{2,1,0:T(4,128)S(1)}, u32[]{:S(2)}, u32[]{:S(2)}) collective-permute-start(f32[100,4,128]{2,1,0:T(4,128)S(1)} %get-tuple-element.19), channel_id=1, source_target_pairs={{224,0},{0,32},{32,64},{64,96},{96,128},{128,160},{160,192},{192,2... | collective-permute-start | bytes 614408 | tf_op jit(solution)/shard_map/ppermute | solution.py:509
  20.2 4.0 %collective-permute-start.6 = (f32[100,4,128]{2,1,0:T(4,128)S(1)}, f32[100,4,128]{2,1,0:T(4,128)S(1)}, u32[]{:S(2)}, u32[]{:S(2)}) collective-permute-start(f32[100,4,128]{2,1,0:T(4,128)S(1)} %get-tuple-element.20), channel_id=1, source_target_pairs={{32,0},{64,32},{96,64},{128,96},{160,128},{192,160},{224,192},{0,2... | collective-permute-start | bytes 614408 | tf_op jit(solution)/shard_map/ppermute | solution.py:509
  24.2 0.0 copy-start.5
  24.2 6.3 %near.2.near_in = f32[8,256]{1,0:T(8,128)S(1)} custom-call(f32[33,4,128]{2,1,0:T(4,128)S(1)} %collective-permute-done.z0.refs_0_, f32[33,4,128]{2,1,0:T(4,128)S(1)} %copy-done, f32[33,4,128]{2,1,0:T(4,128)S(1)} %copy-done.1, f32[33,4,128]{2,1,0:T(4,128)S(1)} %collective-permute-done.1.z3.refs_3_, f32[51,4,128]{2,1,0:T(4,128)S(1)} %collective-permute-done.2.ylo.refs_4_, ...), custom_call_target="tpu_custom_call" | custom-call | flops 6000000000 | bytes 1048576 | tf_op jit(solution)/shard_map/near/pallas_call | solution.py:495
  30.5 0.0 copy-start.6
  30.5 0.0 collective-permute-done.5.xlo.refs_6_
  30.6 0.0 collective-permute-done.6.xhi.refs_7_
  30.6 2.4 %collective-permute-start.7 = (f32[36,2,128]{2,1,0:T(2,128)S(1)}, f32[36,2,128]{2,1,0:T(2,128)S(1)}, u32[]{:S(2)}, u32[]{:S(2)}) collective-permute-start(f32[36,2,128]{2,1,0:T(2,128)S(1)} %slice.556), channel_id=1, source_target_pairs={{96,0},{128,32},{160,64},{192,96},{224,128},{0,160},{32,192},{64,2... | collective-permute-start | bytes 110600 | tf_op jit(solution)/shard_map/ppermute | solution.py:509
  33.0 0.0 copy-start.8
  33.0 0.0 copy-start.9
  33.0 1.2 %collective-permute-start.8 = (f32[24,2,128]{2,1,0:T(2,128)S(1)}, f32[24,2,128]{2,1,0:T(2,128)S(1)}, u32[]{:S(2)}, u32[]{:S(2)}) collective-permute-start(f32[24,2,128]{2,1,0:T(2,128)S(1)} %slice.557), channel_id=1, source_target_pairs={{160,0},{192,32},{224,64},{0,96},{32,128},{64,160},{96,192},{128,2... | collective-permute-start | bytes 73736 | tf_op jit(solution)/shard_map/ppermute | solution.py:509
  34.3 0.0 copy-done.5
  34.3 0.0 copy-done.6
  34.3 0.0 copy-done.8
  34.3 0.0 copy-done.9
  34.3 6.2 %far.1 = f32[64,256]{1,0:T(8,128)S(1)} custom-call(f32[33,4,128]{2,1,0:T(4,128)S(1)} %collective-permute-done.z0.refs_0_, f32[33,4,128]{2,1,0:T(4,128)S(1)} %copy-done, f32[33,4,128]{2,1,0:T(4,128)S(1)} %copy-done.1, f32[33,4,128]{2,1,0:T(4,128)S(1)} %collective-permute-done.1.z3.refs_3_, f32[51,4,128]{2,1,0:T(4,128)S(1)} %collective-permute-done.2.ylo.refs_4_, ...), custom_call_target="tpu_custom_call" | custom-call | flops 7000000000 | bytes 1048576 | tf_op jit(solution)/shard_map/far/pallas_call | solution.py:495
  40.5 0.0 collective-permute-done.8
  40.5 0.0 collective-permute-done.7
  40.6 4.0 %collective-permute-start.9 = (f32[8,4,3,2,128]{4,3,2,1,0:T(2,128)S(1)}, f32[8,4,3,2,128]{4,3,2,1,0:T(2,128)S(1)}, u32[]{:S(2)}, u32[]{:S(2)}) collective-permute-start(f32[8,4,3,2,128]{4,3,2,1,0:T(2,128)S(1)} %bitcast.106), channel_id=1, source_target_pairs={{3,0},{4,1},{5,2},{6,3},{7,4},{0,5},{1,6},{2,7},{11,8},{12,9},{13,... | collective-permute-start | bytes 294920 | tf_op jit(solution)/shard_map/ppermute | solution.py:509
  44.6 0.5 collective-permute-start.10
  45.1 6.3 %near.3.near_out = f32[8,256]{1,0:T(8,128)S(1)} custom-call(f32[33,4,128]{2,1,0:T(4,128)S(1)} %collective-permute-done.z0.refs_0_, f32[33,4,128]{2,1,0:T(4,128)S(1)} %copy-done, f32[33,4,128]{2,1,0:T(4,128)S(1)} %copy-done.1, f32[33,4,128]{2,1,0:T(4,128)S(1)} %collective-permute-done.1.z3.refs_3_, f32[51,4,128]{2,1,0:T(4,128)S(1)} %collective-permute-done.2.ylo.refs_4_, ...), custom_call_target="tpu_custom_call" | custom-call | flops 6000000000 | bytes 1048576 | tf_op jit(solution)/shard_map/near/pallas_call | solution.py:495
  51.4 0.0 copy-start.2
  51.4 0.0 copy-start.3
  51.4 0.0 copy-start.4
  51.4 0.0 copy-start.7
  51.5 0.0 copy-start.10
  51.5 0.0 collective-permute-done.10
  51.5 0.0 collective-permute-done.9
  51.5 0.1 pad_maximum_fusion
  51.6 0.7 %copy-done.2 = f32[152,152]{1,0:T(8,128)S(1)} copy-done((f32[152,152]{1,0:T(8,128)S(1)}, f32[152,152]{1,0:T(8,128)}, u32[]{:S(2)}) %copy-start.2) | copy-done | bytes 92440
  52.3 0.0 copy-done.3
  52.3 0.0 copy-done.4
  52.3 0.0 copy-done.7
  52.3 0.0 copy-done.10
  52.3 9.2 %last.1 = f32[4,4,256]{2,1,0:T(4,128)} custom-call(s32[4,4,4]{2,1,0:T(4,128)S(1)} %copy-done.4, f32[256,2,128]{2,1,0:T(2,128)S(1)} %bitcast.104, f32[64,256]{1,0:T(8,128)S(1)} %far.1, f32[8,256]{1,0:T(8,128)S(1)} %near.2.near_in, f32[8,256]{1,0:T(8,128)S(1)} %near.3.near_out, f32[3,4,4,256]{3,2,1,0:T(4,128)S(1)} %copy-done.3, f32[152,152]{1,0:T(8,128)S(1)} %copy-done.2, ...), custom_call_target="tpu_custom_call" | custom-call | flops 8999999488 | bytes 1048576 | tf_op jit(solution)/shard_map/last/pallas_call | solution.py:495
  (74 shorter events, 0.7 us)
Async XLA Ops:
  4.8 4.4 %collective-permute-start = (f32[33,4,128]{2,1,0:T(4,128)}, f32[33,4,128]{2,1,0:T(4,128)S(1)}, u32[]{:S(2)}, u32[]{:S(2)}) collective-permute-start(f32[33,4,128]{2,1,0:T(4,128)} %get-tuple-element.14.z2.refs_2_), channel_id=1, source_target_pairs={{7,0},{0,1},{1,2},{2,3},{3,4},{4,5},{5,6},{6,7},{15,8},{8,9},{9,10... | collective-permute-start | bytes 202760 | tf_op jit(solution)/shard_map/ppermute | solution.py:509
  7.5 1.4 %copy-start = (f32[33,4,128]{2,1,0:T(4,128)S(1)}, f32[33,4,128]{2,1,0:T(4,128)}, u32[]{:S(2)}) copy-start(f32[33,4,128]{2,1,0:T(4,128)} %get-tuple-element.15.z1.refs_1_) | copy-start | bytes 202756
  7.5 1.4 %copy-start.1 = (f32[33,4,128]{2,1,0:T(4,128)S(1)}, f32[33,4,128]{2,1,0:T(4,128)}, u32[]{:S(2)}) copy-start(f32[33,4,128]{2,1,0:T(4,128)} %get-tuple-element.14.z2.refs_2_) | copy-start | bytes 202756
  7.5 3.9 %collective-permute-start.1 = (f32[33,4,128]{2,1,0:T(4,128)}, f32[33,4,128]{2,1,0:T(4,128)S(1)}, u32[]{:S(2)}, u32[]{:S(2)}) collective-permute-start(f32[33,4,128]{2,1,0:T(4,128)} %get-tuple-element.15.z1.refs_1_), channel_id=1, source_target_pairs={{1,0},{2,1},{3,2},{4,3},{5,4},{6,5},{7,6},{0,7},{9,8},{10,9},{11,1... | collective-permute-start | bytes 202760 | tf_op jit(solution)/shard_map/ppermute | solution.py:509
  11.6 4.4 %copy-start.12 = (s32[26,4,4,4]{0,3,2,1:T(4,128)S(1)}, s32[26,4,4,4]{0,3,2,1:T(4,128)}, u32[]{:S(2)}) copy-start(s32[26,4,4,4]{0,3,2,1:T(4,128)} %param.16) | copy-start | bytes 19972
  11.7 5.6 %collective-permute-start.2 = (f32[51,4,128]{2,1,0:T(4,128)S(1)}, f32[51,4,128]{2,1,0:T(4,128)S(1)}, u32[]{:S(2)}, u32[]{:S(2)}) collective-permute-start(f32[51,4,128]{2,1,0:T(4,128)S(1)} %get-tuple-element.16), channel_id=1, source_target_pairs={{24,0},{0,8},{8,16},{16,24},{25,1},{1,9},{9,17},{17,25},{26,2},{2,... | collective-permute-start | bytes 313352 | tf_op jit(solution)/shard_map/ppermute | solution.py:509
  13.0 4.3 %collective-permute-start.3 = (f32[51,4,128]{2,1,0:T(4,128)S(1)}, f32[51,4,128]{2,1,0:T(4,128)S(1)}, u32[]{:S(2)}, u32[]{:S(2)}) collective-permute-start(f32[51,4,128]{2,1,0:T(4,128)S(1)} %get-tuple-element.17), channel_id=1, source_target_pairs={{8,0},{16,8},{24,16},{0,24},{9,1},{17,9},{25,17},{1,25},{10,2},{18... | collective-permute-start | bytes 313352 | tf_op jit(solution)/shard_map/ppermute | solution.py:509
  14.4 4.1 %collective-permute-start.4 = (f32[3,4,128]{2,1,0:T(4,128)S(1)}, f32[3,4,128]{2,1,0:T(4,128)S(1)}, u32[]{:S(2)}, u32[]{:S(2)}) collective-permute-start(f32[3,4,128]{2,1,0:T(4,128)S(1)} %pad_maximum_fusion.10), channel_id=1, source_target_pairs={{16,0},{24,8},{0,16},{8,24},{17,1},{25,9},{1,17},{9,25},{18,2},{26... | collective-permute-start | bytes 18440 | tf_op jit(solution)/shard_map/ppermute | solution.py:509
  16.2 0.9 %copy-start.11 = (s32[343,4,4,4]{0,3,2,1:T(4,128)S(1)}, s32[343,4,4,4]{0,3,2,1:T(4,128)}, u32[]{:S(2)}) copy-start(s32[343,4,4,4]{0,3,2,1:T(4,128)} %param.17) | copy-start | bytes 263428
  18.6 11.9 %collective-permute-start.5 = (f32[100,4,128]{2,1,0:T(4,128)S(1)}, f32[100,4,128]{2,1,0:T(4,128)S(1)}, u32[]{:S(2)}, u32[]{:S(2)}) collective-permute-start(f32[100,4,128]{2,1,0:T(4,128)S(1)} %get-tuple-element.19), channel_id=1, source_target_pairs={{224,0},{0,32},{32,64},{64,96},{96,128},{128,160},{160,192},{192,2... | collective-permute-start | bytes 614408 | tf_op jit(solution)/shard_map/ppermute | solution.py:509
  20.2 10.4 %collective-permute-start.6 = (f32[100,4,128]{2,1,0:T(4,128)S(1)}, f32[100,4,128]{2,1,0:T(4,128)S(1)}, u32[]{:S(2)}, u32[]{:S(2)}) collective-permute-start(f32[100,4,128]{2,1,0:T(4,128)S(1)} %get-tuple-element.20), channel_id=1, source_target_pairs={{32,0},{64,32},{96,64},{128,96},{160,128},{192,160},{224,192},{0,2... | collective-permute-start | bytes 614408 | tf_op jit(solution)/shard_map/ppermute | solution.py:509
  24.2 10.0 %copy-start.5 = (bf16[512,384]{1,0:T(8,128)(2,1)S(1)}, bf16[512,384]{1,0:T(8,128)(2,1)}, u32[]{:S(2)}) copy-start(bf16[512,384]{1,0:T(8,128)(2,1)} %constant.24.clone.pick) | copy-start | bytes 1179652
  30.5 3.8 %copy-start.6 = (f32[3,160,128]{2,1,0:T(8,128)S(1)}, f32[3,160,128]{2,1,0:T(8,128)}, u32[]{:S(2)}) copy-start(f32[3,160,128]{2,1,0:T(8,128)} %constant.19.clone.column) | copy-start | bytes 737284
  30.6 9.9 %collective-permute-start.7 = (f32[36,2,128]{2,1,0:T(2,128)S(1)}, f32[36,2,128]{2,1,0:T(2,128)S(1)}, u32[]{:S(2)}, u32[]{:S(2)}) collective-permute-start(f32[36,2,128]{2,1,0:T(2,128)S(1)} %slice.556), channel_id=1, source_target_pairs={{96,0},{128,32},{160,64},{192,96},{224,128},{0,160},{32,192},{64,2... | collective-permute-start | bytes 110600 | tf_op jit(solution)/shard_map/ppermute | solution.py:509
  33.0 1.3 %copy-start.8 = (f32[8,256]{1,0:T(8,128)S(1)}, f32[8,256]{1,0:T(8,128)}, u32[]{:S(2)}) copy-start(f32[8,256]{1,0:T(8,128)} %constant.20.clone.row) | copy-start | bytes 24580
  33.0 1.3 %copy-start.9 = (s32[8,256]{1,0:T(8,128)S(1)}, s32[8,256]{1,0:T(8,128)}, u32[]{:S(2)}) copy-start(s32[8,256]{1,0:T(8,128)} %constant.23.clone.mirror) | copy-start | bytes 24580
  33.0 7.5 %collective-permute-start.8 = (f32[24,2,128]{2,1,0:T(2,128)S(1)}, f32[24,2,128]{2,1,0:T(2,128)S(1)}, u32[]{:S(2)}, u32[]{:S(2)}) collective-permute-start(f32[24,2,128]{2,1,0:T(2,128)S(1)} %slice.557), channel_id=1, source_target_pairs={{160,0},{192,32},{224,64},{0,96},{32,128},{64,160},{96,192},{128,2... | collective-permute-start | bytes 73736 | tf_op jit(solution)/shard_map/ppermute | solution.py:509
  40.6 10.9 %collective-permute-start.9 = (f32[8,4,3,2,128]{4,3,2,1,0:T(2,128)S(1)}, f32[8,4,3,2,128]{4,3,2,1,0:T(2,128)S(1)}, u32[]{:S(2)}, u32[]{:S(2)}) collective-permute-start(f32[8,4,3,2,128]{4,3,2,1,0:T(2,128)S(1)} %bitcast.106), channel_id=1, source_target_pairs={{3,0},{4,1},{5,2},{6,3},{7,4},{0,5},{1,6},{2,7},{11,8},{12,9},{13,... | collective-permute-start | bytes 294920 | tf_op jit(solution)/shard_map/ppermute | solution.py:509
  44.6 6.9 %collective-permute-start.10 = (f32[8,4,2,2,128]{4,3,2,1,0:T(2,128)S(1)}, f32[8,4,2,2,128]{4,3,2,1,0:T(2,128)S(1)}, u32[]{:S(2)}, u32[]{:S(2)}) collective-permute-start(f32[8,4,2,2,128]{4,3,2,1,0:T(2,128)S(1)} %slice.558), channel_id=1, source_target_pairs={{5,0},{6,1},{7,2},{0,3},{1,4},{2,5},{3,6},{4,7},{13,8},{14,9},{15,... | collective-permute-start | bytes 196616 | tf_op jit(solution)/shard_map/ppermute | solution.py:509
  51.4 0.9 %copy-start.2 = (f32[152,152]{1,0:T(8,128)S(1)}, f32[152,152]{1,0:T(8,128)}, u32[]{:S(2)}) copy-start(f32[152,152]{1,0:T(8,128)} %down.1) | copy-start | bytes 277252
  51.4 0.9 %copy-start.3 = (f32[3,4,4,256]{3,2,1,0:T(4,128)S(1)}, f32[3,4,4,256]{3,2,1,0:T(4,128)}, u32[]{:S(2)}) copy-start(f32[3,4,4,256]{3,2,1,0:T(4,128)} %pos.3) | copy-start | bytes 147460
  51.4 0.9 %copy-start.4 = (s32[4,4,4]{2,1,0:T(4,128)S(1)}, s32[4,4,4]{2,1,0:T(4,128)}, u32[]{:S(2)}) copy-start(s32[4,4,4]{2,1,0:T(4,128)} %counts.3) | copy-start | bytes 772
  51.4 0.9 %copy-start.7 = (bf16[160,128]{1,0:T(8,128)(2,1)S(1)}, bf16[160,128]{1,0:T(8,128)(2,1)}, u32[]{:S(2)}) copy-start(bf16[160,128]{1,0:T(8,128)(2,1)} %constant.22.clone.nodes) | copy-start | bytes 122884
  51.5 0.9 %copy-start.10 = (f32[8,128]{1,0:T(8,128)S(1)}, f32[8,128]{1,0:T(8,128)}, u32[]{:S(2)}) copy-start(f32[8,128]{1,0:T(8,128)} %constant.21.clone.tail) | copy-start | bytes 12292

commit v5 on v4

--- a/solution.py
+++ b/solution.py
@@ -521,9 +521,10 @@
         "vvsvvvvv", "upward", 6000, positions, charges, counts, up_operator, column, row, tail, nodes, vmem=59,
     )
     own = (shifted(above, "gz", -1), below, above, shifted(below, "gz", 1))
+    beyond = shifted(below[32:33], "gz", 2)
 
     grid = [[v[k * 16 : k * 16 + 16].reshape(4, 4, 4, 128) for v in own] for k in range(2)]
-    blocks = [own[n][32:33] for n in (0, 1, 3)]
+    blocks = [own[n][32:33] for n in (0, 1, 3)] + [beyond]
 
     def to_y(low, one):
         parts = [v[:, low : low + 2].reshape(8, 4, 128) for v in grid[0]]
@@ -537,7 +538,7 @@
     ylo = shifted(up, "gy", -1)
     yhi = shifted(down, "gy", 1)
     far_blocks = shifted(middle, "gy", 2)
-    blocks = jnp.concatenate([ylo[48:51], middle, yhi[48:51], far_blocks], axis=0)
+    blocks = jnp.concatenate([ylo[48:52], middle, yhi[48:52], far_blocks], axis=0)
 
     def to_x(low, one):
         parts = []
@@ -554,11 +555,10 @@
     xhi = shifted(down, "gx", 1)
     halo = (*own, ylo, yhi, xlo, xhi)
 
-    held = jnp.concatenate([xlo[88:100], blocks, xhi[88:100]], axis=0)[:, 0:2]
-    held = jnp.concatenate([held, shifted(held, "gx", 3), shifted(held[12:36], "gx", -3)], axis=0)
-    held = held.reshape(8, 4, 3, 2, 128)
-    forward, back = shifted(held, "gz", 3), shifted(held[:, :, 1:3], "gz", -3)
-    gathered = jnp.concatenate([held, forward, back], axis=2).reshape(256, 2, 128)
+    held = jnp.concatenate([xlo[88:104], blocks, xhi[88:104]], axis=0)[:, 0:2]
+    held = jnp.concatenate([held, shifted(held, "gx", 3), shifted(held[16:48], "gx", -3)], axis=0)
+    held = held.reshape(8, 4, 4, 2, 128)
+    gathered = jnp.concatenate([held, shifted(held, "gz", 4)], axis=2).reshape(256, 2, 128)
 
     flags = jnp.pad(far_flags.reshape(CLASSES, 64).astype(BF16), ((0, 384 - CLASSES), (0, 64)))
     (far,) = call(

time: 61.8 us -> 64.3 us (1.040)
  the two profiles are of different devices: /device:TPU:1 before, /device:TPU:8 now
where the time goes in v5:
time: 64.3 us; the launch traced here: 64.1 us
  Pallas kernels  32.8 us (51%)
  starting transfers between devices  21.8 us (34%)
  waiting for transfers between devices  5.12 us (8%)
  local copies, waits for them, and re-layouts  3.44 us (5%)
    pallas_call x5, Pallas kernels, call(): pl.pallas_call(body, out_shape=[jax.ShapeDtypeStruct(s, F32) for s in out...  32.8 us
    ppermute x11, starting transfers between devices, shifted(): lax.ppermute(array, axis, [((i + distance) % n, i) for i in range(n)])  21.8 us
    ppermute x11, waiting for transfers between devices, shifted(): lax.ppermute(array, axis, [((i + distance) % n, i) for i in range(n)])  5.12 us
    unnamed x67, local copies, waits for them, and re-layouts  1.86 us
  transfers between devices with their start and end apart: 11, of which 4 were waited for; matrix products, arithmetic and copies ran while one was open for 3% of the time, Pallas kernels for 29%

profile of v5, /device:TPU:8, one launch (start us, length us, event | category | flops | bytes accessed | tf_op | source)
XLA Modules:
  0.0 64.1 jit_solution(5345841092978998029)
XLA Ops:
  0.0 4.8 %upward.1 = (f32[33,4,128]{2,1,0:T(4,128)}, f32[33,4,128]{2,1,0:T(4,128)}) custom-call(f32[3,4,4,256]{3,2,1,0:T(4,128)} %pos.3, f32[4,4,256]{2,1,0:T(4,128)} %chg.1, s32[4,4,4]{2,1,0:T(4,128)} %counts.3, f32[152,152]{1,0:T(8,128)} %up.1, f32[3,160,128]{2,1,0:T(8,128)} %constant.19.clone.column, f32[8,256]{1,0:T(8,128)} %constant.20.clone.row, ...), custom_call_target="tpu_custom_call" | custom-call | flops 6000000000 | bytes 1048576 | tf_op jit(solution)/shard_map/upward/pallas_call | solution.py:495
  4.8 0.0 collective-permute-start
  4.8 0.0 copy-start
  4.8 0.0 copy-start.1
  4.8 1.7 %collective-permute-start.1 = (f32[33,4,128]{2,1,0:T(4,128)}, f32[33,4,128]{2,1,0:T(4,128)S(1)}, u32[]{:S(2)}, u32[]{:S(2)}) collective-permute-start(f32[33,4,128]{2,1,0:T(4,128)} %get-tuple-element.15.z1.refs_1_), channel_id=1, source_target_pairs={{1,0},{2,1},{3,2},{4,3},{5,4},{6,5},{7,6},{0,7},{9,8},{10,9},{11,1... | collective-permute-start | bytes 202760 | tf_op jit(solution)/shard_map/ppermute | solution.py:509
  6.6 0.8 %fusion.9 = (f32[16,4,128]{2,1,0:T(4,128)S(1)}, f32[16,4,128]{2,1,0:T(4,128)S(1)}, f32[16,4,128]{2,1,0:T(4,128)S(1)}, f32[16,4,128]{2,1,0:T(4,128)S(1)}) fusion(f32[33,4,128]{2,1,0:T(4,128)} %get-tuple-element.14.z2.refs_2_, f32[33,4,128]{2,1,0:T(4,128)} %get-tuple-element.15.z1.refs_1_), kind=kLoop, calls=%fused_computation.104 | loop fusion | bytes 262144 | tf_op jit(solution)/shard_map/slice | solution.py:526
  7.4 0.0 copy-done
  7.4 0.0 copy-done.1
  7.5 0.1 pad.8.clone
  7.6 0.1 pad.6.clone
  7.6 1.1 %collective-permute-done.z0.refs_0_ = f32[33,4,128]{2,1,0:T(4,128)S(1)} collective-permute-done((f32[33,4,128]{2,1,0:T(4,128)}, f32[33,4,128]{2,1,0:T(4,128)S(1)}, u32[]{:S(2)}, u32[]{:S(2)}) %collective-permute-start) | collective-permute-done | bytes 67616 | tf_op jit(solution)/shard_map/ppermute | solution.py:509
  8.8 0.0 collective-permute-done.1.z3.refs_3_
  9.0 3.5 %collective-permute-start.2 = (f32[1,4,128]{2,1,0:T(4,128)S(1)}, f32[1,4,128]{2,1,0:T(4,128)S(1)}, u32[]{:S(2)}, u32[]{:S(2)}) collective-permute-start(f32[1,4,128]{2,1,0:T(4,128)S(1)} %get-tuple-element.89), channel_id=1, source_target_pairs={{2,0},{3,1},{4,2},{5,3},{6,4},{7,5},{0,6},{1,7},{10,8},{11,9},{12,... | collective-permute-start | bytes 6152 | tf_op jit(solution)/shard_map/ppermute | solution.py:509
  12.5 0.0 copy-start.12
  12.5 1.3 %collective-permute-done.2 = f32[1,4,128]{2,1,0:T(4,128)S(1)} collective-permute-done((f32[1,4,128]{2,1,0:T(4,128)S(1)}, f32[1,4,128]{2,1,0:T(4,128)S(1)}, u32[]{:S(2)}, u32[]{:S(2)}) %collective-permute-start.2) | collective-permute-done | bytes 2080 | tf_op jit(solution)/shard_map/ppermute | solution.py:509
  13.8 0.4 collective-permute-start.3
  14.3 2.9 %collective-permute-start.4 = (f32[52,4,128]{2,1,0:T(4,128)S(1)}, f32[52,4,128]{2,1,0:T(4,128)S(1)}, u32[]{:S(2)}, u32[]{:S(2)}) collective-permute-start(f32[52,4,128]{2,1,0:T(4,128)S(1)} %get-tuple-element.17), channel_id=1, source_target_pairs={{8,0},{16,8},{24,16},{0,24},{9,1},{17,9},{25,17},{1,25},{10,2},{18... | collective-permute-start | bytes 319496 | tf_op jit(solution)/shard_map/ppermute | solution.py:509
  17.1 0.7 %collective-permute-start.5 = (f32[4,4,128]{2,1,0:T(4,128)S(1)}, f32[4,4,128]{2,1,0:T(4,128)S(1)}, u32[]{:S(2)}, u32[]{:S(2)}) collective-permute-start(f32[4,4,128]{2,1,0:T(4,128)S(1)} %pad_maximum_fusion.10), channel_id=1, source_target_pairs={{16,0},{24,8},{0,16},{8,24},{17,1},{25,9},{1,17},{9,25},{18,2},{26... | collective-permute-start | bytes 24584 | tf_op jit(solution)/shard_map/ppermute | solution.py:509
  17.8 0.0 copy-done.12
  17.8 0.1 fusion.12
  17.9 0.1 maximum_maximum_fusion
  18.0 0.0 copy-start.11
  18.0 0.2 copy.43
  18.2 0.7 %copy-done.11 = s32[343,4,4,4]{0,3,2,1:T(4,128)S(1)} copy-done((s32[343,4,4,4]{0,3,2,1:T(4,128)S(1)}, s32[343,4,4,4]{0,3,2,1:T(4,128)}, u32[]{:S(2)}) %copy-start.11) | copy-done | bytes 87832
  19.0 0.1 copy.42
  19.1 0.7 %collective-permute-done.3.ylo.refs_4_ = f32[52,4,128]{2,1,0:T(4,128)S(1)} collective-permute-done((f32[52,4,128]{2,1,0:T(4,128)S(1)}, f32[52,4,128]{2,1,0:T(4,128)S(1)}, u32[]{:S(2)}, u32[]{:S(2)}) %collective-permute-start.3) | collective-permute-done | bytes 106528 | tf_op jit(solution)/shard_map/ppermute | solution.py:509
  19.8 0.0 collective-permute-done.4.yhi.refs_5_
  20.3 2.0 %collective-permute-done.5 = f32[4,4,128]{2,1,0:T(4,128)S(1)} collective-permute-done((f32[4,4,128]{2,1,0:T(4,128)S(1)}, f32[4,4,128]{2,1,0:T(4,128)S(1)}, u32[]{:S(2)}, u32[]{:S(2)}) %collective-permute-start.5) | collective-permute-done | bytes 8224 | tf_op jit(solution)/shard_map/ppermute | solution.py:509
  22.3 0.8 %collective-permute-start.6 = (f32[104,4,128]{2,1,0:T(4,128)S(1)}, f32[104,4,128]{2,1,0:T(4,128)S(1)}, u32[]{:S(2)}, u32[]{:S(2)}) collective-permute-start(f32[104,4,128]{2,1,0:T(4,128)S(1)} %get-tuple-element.19), channel_id=1, source_target_pairs={{224,0},{0,32},{32,64},{64,96},{96,128},{128,160},{160,192},{192,2... | collective-permute-start | bytes 638984 | tf_op jit(solution)/shard_map/ppermute | solution.py:509
  23.1 4.0 %collective-permute-start.7 = (f32[104,4,128]{2,1,0:T(4,128)S(1)}, f32[104,4,128]{2,1,0:T(4,128)S(1)}, u32[]{:S(2)}, u32[]{:S(2)}) collective-permute-start(f32[104,4,128]{2,1,0:T(4,128)S(1)} %get-tuple-element.20), channel_id=1, source_target_pairs={{32,0},{64,32},{96,64},{128,96},{160,128},{192,160},{224,192},{0,2... | collective-permute-start | bytes 638984 | tf_op jit(solution)/shard_map/ppermute | solution.py:509
  27.1 0.0 copy-start.6
  27.1 6.3 %near.2.near_in = f32[8,256]{1,0:T(8,128)S(1)} custom-call(f32[33,4,128]{2,1,0:T(4,128)S(1)} %collective-permute-done.z0.refs_0_, f32[33,4,128]{2,1,0:T(4,128)S(1)} %copy-done, f32[33,4,128]{2,1,0:T(4,128)S(1)} %copy-done.1, f32[33,4,128]{2,1,0:T(4,128)S(1)} %collective-permute-done.1.z3.refs_3_, f32[52,4,128]{2,1,0:T(4,128)S(1)} %collective-permute-done.3.ylo.refs_4_, ...), custom_call_target="tpu_custom_call" | custom-call | flops 6000000000 | bytes 1048576 | tf_op jit(solution)/shard_map/near/pallas_call | solution.py:495
  33.4 0.0 copy-start.5
  33.4 0.0 collective-permute-done.6.xlo.refs_6_
  33.5 0.0 collective-permute-done.7.xhi.refs_7_
  33.5 2.9 %collective-permute-start.8 = (f32[48,2,128]{2,1,0:T(2,128)S(1)}, f32[48,2,128]{2,1,0:T(2,128)S(1)}, u32[]{:S(2)}, u32[]{:S(2)}) collective-permute-start(f32[48,2,128]{2,1,0:T(2,128)S(1)} %slice.553), channel_id=1, source_target_pairs={{96,0},{128,32},{160,64},{192,96},{224,128},{0,160},{32,192},{64,2... | collective-permute-start | bytes 147464 | tf_op jit(solution)/shard_map/ppermute | solution.py:509
  36.4 0.0 copy-start.8
  36.5 0.0 copy-start.9
  36.5 1.2 %collective-permute-start.9 = (f32[32,2,128]{2,1,0:T(2,128)S(1)}, f32[32,2,128]{2,1,0:T(2,128)S(1)}, u32[]{:S(2)}, u32[]{:S(2)}) collective-permute-start(f32[32,2,128]{2,1,0:T(2,128)S(1)} %slice.554), channel_id=1, source_target_pairs={{160,0},{192,32},{224,64},{0,96},{32,128},{64,160},{96,192},{128,2... | collective-permute-start | bytes 98312 | tf_op jit(solution)/shard_map/ppermute | solution.py:509
  37.7 0.0 copy-done.6
  37.7 0.0 copy-done.5
  37.7 0.0 copy-done.8
  37.7 0.0 copy-done.9
  37.7 6.2 %far.1 = f32[64,256]{1,0:T(8,128)S(1)} custom-call(f32[33,4,128]{2,1,0:T(4,128)S(1)} %collective-permute-done.z0.refs_0_, f32[33,4,128]{2,1,0:T(4,128)S(1)} %copy-done, f32[33,4,128]{2,1,0:T(4,128)S(1)} %copy-done.1, f32[33,4,128]{2,1,0:T(4,128)S(1)} %collective-permute-done.1.z3.refs_3_, f32[52,4,128]{2,1,0:T(4,128)S(1)} %collective-permute-done.3.ylo.refs_4_, ...), custom_call_target="tpu_custom_call" | custom-call | flops 7000000000 | bytes 1048576 | tf_op jit(solution)/shard_map/far/pallas_call | solution.py:495
  43.9 0.0 collective-permute-done.9
  43.9 0.0 collective-permute-done.8
  44.0 0.1 pad_maximum_fusion.1
  44.0 3.6 %collective-permute-start.10 = (f32[8,4,4,2,128]{4,3,2,1,0:T(2,128)S(1)}, f32[8,4,4,2,128]{4,3,2,1,0:T(2,128)S(1)}, u32[]{:S(2)}, u32[]{:S(2)}) collective-permute-start(f32[8,4,4,2,128]{4,3,2,1,0:T(2,128)S(1)} %bitcast.105), channel_id=1, source_target_pairs={{4,0},{5,1},{6,2},{7,3},{0,4},{1,5},{2,6},{3,7},{12,8},{13,9},{14,... | collective-permute-start | bytes 393224 | tf_op jit(solution)/shard_map/ppermute | solution.py:509
  47.6 6.3 %near.3.near_out = f32[8,256]{1,0:T(8,128)S(1)} custom-call(f32[33,4,128]{2,1,0:T(4,128)S(1)} %collective-permute-done.z0.refs_0_, f32[33,4,128]{2,1,0:T(4,128)S(1)} %copy-done, f32[33,4,128]{2,1,0:T(4,128)S(1)} %copy-done.1, f32[33,4,128]{2,1,0:T(4,128)S(1)} %collective-permute-done.1.z3.refs_3_, f32[52,4,128]{2,1,0:T(4,128)S(1)} %collective-permute-done.3.ylo.refs_4_, ...), custom_call_target="tpu_custom_call" | custom-call | flops 6000000000 | bytes 1048576 | tf_op jit(solution)/shard_map/near/pallas_call | solution.py:495
  54.0 0.0 copy-start.2
  54.0 0.0 copy-start.3
  54.0 0.0 copy-start.4
  54.0 0.0 copy-start.7
  54.0 0.0 copy-start.10
  54.0 0.0 collective-permute-done.10
  54.0 0.1 pad_maximum_fusion
  54.2 0.7 %copy-done.2 = f32[152,152]{1,0:T(8,128)S(1)} copy-done((f32[152,152]{1,0:T(8,128)S(1)}, f32[152,152]{1,0:T(8,128)}, u32[]{:S(2)}) %copy-start.2) | copy-done | bytes 92440
  54.9 0.0 copy-done.3
  54.9 0.0 copy-done.4
  54.9 0.0 copy-done.7
  54.9 0.0 copy-done.10
  54.9 9.2 %last.1 = f32[4,4,256]{2,1,0:T(4,128)} custom-call(s32[4,4,4]{2,1,0:T(4,128)S(1)} %copy-done.4, f32[256,2,128]{2,1,0:T(2,128)S(1)} %bitcast.104, f32[64,256]{1,0:T(8,128)S(1)} %far.1, f32[8,256]{1,0:T(8,128)S(1)} %near.2.near_in, f32[8,256]{1,0:T(8,128)S(1)} %near.3.near_out, f32[3,4,4,256]{3,2,1,0:T(4,128)S(1)} %copy-done.3, f32[152,152]{1,0:T(8,128)S(1)} %copy-done.2, ...), custom_call_target="tpu_custom_call" | custom-call | flops 8999999488 | bytes 1048576 | tf_op jit(solution)/shard_map/last/pallas_call | solution.py:495
  (73 shorter events, 0.7 us)
Async XLA Ops:
  4.8 3.9 %collective-permute-start = (f32[33,4,128]{2,1,0:T(4,128)}, f32[33,4,128]{2,1,0:T(4,128)S(1)}, u32[]{:S(2)}, u32[]{:S(2)}) collective-permute-start(f32[33,4,128]{2,1,0:T(4,128)} %get-tuple-element.14.z2.refs_2_), channel_id=1, source_target_pairs={{7,0},{0,1},{1,2},{2,3},{3,4},{4,5},{5,6},{6,7},{15,8},{8,9},{9,10... | collective-permute-start | bytes 202760 | tf_op jit(solution)/shard_map/ppermute | solution.py:509
  4.8 2.6 %copy-start = (f32[33,4,128]{2,1,0:T(4,128)S(1)}, f32[33,4,128]{2,1,0:T(4,128)}, u32[]{:S(2)}) copy-start(f32[33,4,128]{2,1,0:T(4,128)} %get-tuple-element.15.z1.refs_1_) | copy-start | bytes 202756
  4.8 2.6 %copy-start.1 = (f32[33,4,128]{2,1,0:T(4,128)S(1)}, f32[33,4,128]{2,1,0:T(4,128)}, u32[]{:S(2)}) copy-start(f32[33,4,128]{2,1,0:T(4,128)} %get-tuple-element.14.z2.refs_2_) | copy-start | bytes 202756
  4.8 4.0 %collective-permute-start.1 = (f32[33,4,128]{2,1,0:T(4,128)}, f32[33,4,128]{2,1,0:T(4,128)S(1)}, u32[]{:S(2)}, u32[]{:S(2)}) collective-permute-start(f32[33,4,128]{2,1,0:T(4,128)} %get-tuple-element.15.z1.refs_1_), channel_id=1, source_target_pairs={{1,0},{2,1},{3,2},{4,3},{5,4},{6,5},{7,6},{0,7},{9,8},{10,9},{11,1... | collective-permute-start | bytes 202760 | tf_op jit(solution)/shard_map/ppermute | solution.py:509
  9.0 4.8 %collective-permute-start.2 = (f32[1,4,128]{2,1,0:T(4,128)S(1)}, f32[1,4,128]{2,1,0:T(4,128)S(1)}, u32[]{:S(2)}, u32[]{:S(2)}) collective-permute-start(f32[1,4,128]{2,1,0:T(4,128)S(1)} %get-tuple-element.89), channel_id=1, source_target_pairs={{2,0},{3,1},{4,2},{5,3},{6,4},{7,5},{0,6},{1,7},{10,8},{11,9},{12,... | collective-permute-start | bytes 6152 | tf_op jit(solution)/shard_map/ppermute | solution.py:509
  12.5 5.3 %copy-start.12 = (s32[26,4,4,4]{0,3,2,1:T(4,128)S(1)}, s32[26,4,4,4]{0,3,2,1:T(4,128)}, u32[]{:S(2)}) copy-start(s32[26,4,4,4]{0,3,2,1:T(4,128)} %param.16) | copy-start | bytes 19972
  13.8 6.0 %collective-permute-start.3 = (f32[52,4,128]{2,1,0:T(4,128)S(1)}, f32[52,4,128]{2,1,0:T(4,128)S(1)}, u32[]{:S(2)}, u32[]{:S(2)}) collective-permute-start(f32[52,4,128]{2,1,0:T(4,128)S(1)} %get-tuple-element.16), channel_id=1, source_target_pairs={{24,0},{0,8},{8,16},{16,24},{25,1},{1,9},{9,17},{17,25},{26,2},{2,... | collective-permute-start | bytes 319496 | tf_op jit(solution)/shard_map/ppermute | solution.py:509
  14.3 5.5 %collective-permute-start.4 = (f32[52,4,128]{2,1,0:T(4,128)S(1)}, f32[52,4,128]{2,1,0:T(4,128)S(1)}, u32[]{:S(2)}, u32[]{:S(2)}) collective-permute-start(f32[52,4,128]{2,1,0:T(4,128)S(1)} %get-tuple-element.17), channel_id=1, source_target_pairs={{8,0},{16,8},{24,16},{0,24},{9,1},{17,9},{25,17},{1,25},{10,2},{18... | collective-permute-start | bytes 319496 | tf_op jit(solution)/shard_map/ppermute | solution.py:509
  17.1 5.2 %collective-permute-start.5 = (f32[4,4,128]{2,1,0:T(4,128)S(1)}, f32[4,4,128]{2,1,0:T(4,128)S(1)}, u32[]{:S(2)}, u32[]{:S(2)}) collective-permute-start(f32[4,4,128]{2,1,0:T(4,128)S(1)} %pad_maximum_fusion.10), channel_id=1, source_target_pairs={{16,0},{24,8},{0,16},{8,24},{17,1},{25,9},{1,17},{9,25},{18,2},{26... | collective-permute-start | bytes 24584 | tf_op jit(solution)/shard_map/ppermute | solution.py:509
  18.0 0.9 %copy-start.11 = (s32[343,4,4,4]{0,3,2,1:T(4,128)S(1)}, s32[343,4,4,4]{0,3,2,1:T(4,128)}, u32[]{:S(2)}) copy-start(s32[343,4,4,4]{0,3,2,1:T(4,128)} %param.17) | copy-start | bytes 263428
  22.3 11.1 %collective-permute-start.6 = (f32[104,4,128]{2,1,0:T(4,128)S(1)}, f32[104,4,128]{2,1,0:T(4,128)S(1)}, u32[]{:S(2)}, u32[]{:S(2)}) collective-permute-start(f32[104,4,128]{2,1,0:T(4,128)S(1)} %get-tuple-element.19), channel_id=1, source_target_pairs={{224,0},{0,32},{32,64},{64,96},{96,128},{128,160},{160,192},{192,2... | collective-permute-start | bytes 638984 | tf_op jit(solution)/shard_map/ppermute | solution.py:509
  23.1 10.4 %collective-permute-start.7 = (f32[104,4,128]{2,1,0:T(4,128)S(1)}, f32[104,4,128]{2,1,0:T(4,128)S(1)}, u32[]{:S(2)}, u32[]{:S(2)}) collective-permute-start(f32[104,4,128]{2,1,0:T(4,128)S(1)} %get-tuple-element.20), channel_id=1, source_target_pairs={{32,0},{64,32},{96,64},{128,96},{160,128},{192,160},{224,192},{0,2... | collective-permute-start | bytes 638984 | tf_op jit(solution)/shard_map/ppermute | solution.py:509
  27.1 10.6 %copy-start.6 = (f32[3,160,128]{2,1,0:T(8,128)S(1)}, f32[3,160,128]{2,1,0:T(8,128)}, u32[]{:S(2)}) copy-start(f32[3,160,128]{2,1,0:T(8,128)} %constant.19.clone.column) | copy-start | bytes 737284
  33.4 4.3 %copy-start.5 = (bf16[512,384]{1,0:T(8,128)(2,1)S(1)}, bf16[512,384]{1,0:T(8,128)(2,1)}, u32[]{:S(2)}) copy-start(bf16[512,384]{1,0:T(8,128)(2,1)} %constant.24.clone.pick) | copy-start | bytes 1179652
  33.5 10.4 %collective-permute-start.8 = (f32[48,2,128]{2,1,0:T(2,128)S(1)}, f32[48,2,128]{2,1,0:T(2,128)S(1)}, u32[]{:S(2)}, u32[]{:S(2)}) collective-permute-start(f32[48,2,128]{2,1,0:T(2,128)S(1)} %slice.553), channel_id=1, source_target_pairs={{96,0},{128,32},{160,64},{192,96},{224,128},{0,160},{32,192},{64,2... | collective-permute-start | bytes 147464 | tf_op jit(solution)/shard_map/ppermute | solution.py:509
  36.4 1.3 %copy-start.8 = (f32[8,256]{1,0:T(8,128)S(1)}, f32[8,256]{1,0:T(8,128)}, u32[]{:S(2)}) copy-start(f32[8,256]{1,0:T(8,128)} %constant.20.clone.row) | copy-start | bytes 24580
  36.5 1.3 %copy-start.9 = (s32[8,256]{1,0:T(8,128)S(1)}, s32[8,256]{1,0:T(8,128)}, u32[]{:S(2)}) copy-start(s32[8,256]{1,0:T(8,128)} %constant.23.clone.mirror) | copy-start | bytes 24580
  36.5 7.5 %collective-permute-start.9 = (f32[32,2,128]{2,1,0:T(2,128)S(1)}, f32[32,2,128]{2,1,0:T(2,128)S(1)}, u32[]{:S(2)}, u32[]{:S(2)}) collective-permute-start(f32[32,2,128]{2,1,0:T(2,128)S(1)} %slice.554), channel_id=1, source_target_pairs={{160,0},{192,32},{224,64},{0,96},{32,128},{64,160},{96,192},{128,2... | collective-permute-start | bytes 98312 | tf_op jit(solution)/shard_map/ppermute | solution.py:509
  44.0 10.0 %collective-permute-start.10 = (f32[8,4,4,2,128]{4,3,2,1,0:T(2,128)S(1)}, f32[8,4,4,2,128]{4,3,2,1,0:T(2,128)S(1)}, u32[]{:S(2)}, u32[]{:S(2)}) collective-permute-start(f32[8,4,4,2,128]{4,3,2,1,0:T(2,128)S(1)} %bitcast.105), channel_id=1, source_target_pairs={{4,0},{5,1},{6,2},{7,3},{0,4},{1,5},{2,6},{3,7},{12,8},{13,9},{14,... | collective-permute-start | bytes 393224 | tf_op jit(solution)/shard_map/ppermute | solution.py:509
  54.0 0.9 %copy-start.2 = (f32[152,152]{1,0:T(8,128)S(1)}, f32[152,152]{1,0:T(8,128)}, u32[]{:S(2)}) copy-start(f32[152,152]{1,0:T(8,128)} %down.1) | copy-start | bytes 277252
  54.0 0.9 %copy-start.3 = (f32[3,4,4,256]{3,2,1,0:T(4,128)S(1)}, f32[3,4,4,256]{3,2,1,0:T(4,128)}, u32[]{:S(2)}) copy-start(f32[3,4,4,256]{3,2,1,0:T(4,128)} %pos.3) | copy-start | bytes 147460
  54.0 0.9 %copy-start.4 = (s32[4,4,4]{2,1,0:T(4,128)S(1)}, s32[4,4,4]{2,1,0:T(4,128)}, u32[]{:S(2)}) copy-start(s32[4,4,4]{2,1,0:T(4,128)} %counts.3) | copy-start | bytes 772
  54.0 0.9 %copy-start.7 = (bf16[160,128]{1,0:T(8,128)(2,1)S(1)}, bf16[160,128]{1,0:T(8,128)(2,1)}, u32[]{:S(2)}) copy-start(bf16[160,128]{1,0:T(8,128)(2,1)} %constant.22.clone.nodes) | copy-start | bytes 122884
  54.0 0.9 %copy-start.10 = (f32[8,128]{1,0:T(8,128)S(1)}, f32[8,128]{1,0:T(8,128)}, u32[]{:S(2)}) copy-start(f32[8,128]{1,0:T(8,128)} %constant.21.clone.tail) | copy-start | bytes 12292

commit v6 on v5

--- a/solution.py
+++ b/solution.py
@@ -521,7 +521,7 @@
         "vvsvvvvv", "upward", 6000, positions, charges, counts, up_operator, column, row, tail, nodes, vmem=59,
     )
     own = (shifted(above, "gz", -1), below, above, shifted(below, "gz", 1))
-    beyond = shifted(below[32:33], "gz", 2)
+    beyond = shifted(below, "gz", 2)[32:33]
 
     grid = [[v[k * 16 : k * 16 + 16].reshape(4, 4, 4, 128) for v in own] for k in range(2)]
     blocks = [own[n][32:33] for n in (0, 1, 3)] + [beyond]

time: 64.3 us -> 62.1 us (0.966)
  the two profiles are of different devices: /device:TPU:8 before, /device:TPU:112 now
where the time goes in v6:
time: 62.1 us; the launch traced here: 61.8 us
  Pallas kernels  32.8 us (53%)
  starting transfers between devices  19 us (31%)
  waiting for transfers between devices  5.6 us (9%)
  local copies, waits for them, and re-layouts  3.42 us (6%)
    pallas_call x5, Pallas kernels, call(): pl.pallas_call(body, out_shape=[jax.ShapeDtypeStruct(s, F32) for s in out...  32.8 us
    ppermute x11, starting transfers between devices, shifted(): lax.ppermute(array, axis, [((i + distance) % n, i) for i in range(n)])  19 us
    ppermute x11, waiting for transfers between devices, shifted(): lax.ppermute(array, axis, [((i + distance) % n, i) for i in range(n)])  5.6 us
    unnamed x66, local copies, waits for them, and re-layouts  1.86 us
  transfers between devices with their start and end apart: 11, of which 4 were waited for; matrix products, arithmetic and copies ran while one was open for 3% of the time, Pallas kernels for 30%

profile of v6, /device:TPU:112, one launch (start us, length us, event | category | flops | bytes accessed | tf_op | source)
XLA Modules:
  0.0 61.8 jit_solution(18160717148225328808)
XLA Ops:
  0.0 4.8 %upward.1 = (f32[33,4,128]{2,1,0:T(4,128)}, f32[33,4,128]{2,1,0:T(4,128)}) custom-call(f32[3,4,4,256]{3,2,1,0:T(4,128)} %pos.3, f32[4,4,256]{2,1,0:T(4,128)} %chg.1, s32[4,4,4]{2,1,0:T(4,128)} %counts.3, f32[152,152]{1,0:T(8,128)} %up.1, f32[3,160,128]{2,1,0:T(8,128)} %constant.19.clone.column, f32[8,256]{1,0:T(8,128)} %constant.20.clone.row, ...), custom_call_target="tpu_custom_call" | custom-call | flops 6000000000 | bytes 1048576 | tf_op jit(solution)/shard_map/upward/pallas_call | solution.py:495
  4.8 0.0 collective-permute-start.1
  4.8 0.4 collective-permute-start.2
  5.3 0.0 copy-start
  5.3 0.0 copy-start.1
  5.3 0.2 collective-permute-start
  5.5 0.8 %fusion.11 = (f32[16,4,128]{2,1,0:T(4,128)S(1)}, f32[16,4,128]{2,1,0:T(4,128)S(1)}, f32[16,4,128]{2,1,0:T(4,128)S(1)}, f32[16,4,128]{2,1,0:T(4,128)S(1)}) fusion(f32[33,4,128]{2,1,0:T(4,128)} %get-tuple-element.14.z2.refs_2_, f32[33,4,128]{2,1,0:T(4,128)} %get-tuple-element.15.z1.refs_1_), kind=kLoop, calls=%fused_computation.106 | loop fusion | bytes 262144 | tf_op jit(solution)/shard_map/slice | solution.py:526
  6.3 0.0 copy-done
  6.3 0.0 copy-done.1
  6.4 0.1 pad.8.clone
  6.5 0.1 pad.6.clone
  6.6 2.7 %collective-permute-done.z0.refs_0_ = f32[33,4,128]{2,1,0:T(4,128)S(1)} collective-permute-done((f32[33,4,128]{2,1,0:T(4,128)}, f32[33,4,128]{2,1,0:T(4,128)S(1)}, u32[]{:S(2)}, u32[]{:S(2)}) %collective-permute-start) | collective-permute-done | bytes 67616 | tf_op jit(solution)/shard_map/ppermute | solution.py:509
  9.2 0.0 collective-permute-done.1.z3.refs_3_
  9.4 0.0 copy-start.12
  9.5 0.7 %collective-permute-done.2 = f32[33,4,128]{2,1,0:T(4,128)S(1)} collective-permute-done((f32[33,4,128]{2,1,0:T(4,128)}, f32[33,4,128]{2,1,0:T(4,128)S(1)}, u32[]{:S(2)}, u32[]{:S(2)}) %collective-permute-start.2) | collective-permute-done | bytes 67616 | tf_op jit(solution)/shard_map/ppermute | solution.py:509
  10.2 1.6 %collective-permute-start.3 = (f32[52,4,128]{2,1,0:T(4,128)S(1)}, f32[52,4,128]{2,1,0:T(4,128)S(1)}, u32[]{:S(2)}, u32[]{:S(2)}) collective-permute-start(f32[52,4,128]{2,1,0:T(4,128)S(1)} %get-tuple-element.16), channel_id=1, source_target_pairs={{24,0},{0,8},{8,16},{16,24},{25,1},{1,9},{9,17},{17,25},{26,2},{2,... | collective-permute-start | bytes 319496 | tf_op jit(solution)/shard_map/ppermute | solution.py:509
  11.8 1.7 %collective-permute-start.4 = (f32[52,4,128]{2,1,0:T(4,128)S(1)}, f32[52,4,128]{2,1,0:T(4,128)S(1)}, u32[]{:S(2)}, u32[]{:S(2)}) collective-permute-start(f32[52,4,128]{2,1,0:T(4,128)S(1)} %get-tuple-element.17), channel_id=1, source_target_pairs={{8,0},{16,8},{24,16},{0,24},{9,1},{17,9},{25,17},{1,25},{10,2},{18... | collective-permute-start | bytes 319496 | tf_op jit(solution)/shard_map/ppermute | solution.py:509
  13.5 1.8 %collective-permute-start.5 = (f32[4,4,128]{2,1,0:T(4,128)S(1)}, f32[4,4,128]{2,1,0:T(4,128)S(1)}, u32[]{:S(2)}, u32[]{:S(2)}) collective-permute-start(f32[4,4,128]{2,1,0:T(4,128)S(1)} %pad_maximum_fusion.10), channel_id=1, source_target_pairs={{16,0},{24,8},{0,16},{8,24},{17,1},{25,9},{1,17},{9,25},{18,2},{26... | collective-permute-start | bytes 24584 | tf_op jit(solution)/shard_map/ppermute | solution.py:509
  15.4 0.0 copy-done.12
  15.4 0.1 fusion.14
  15.5 0.1 maximum_maximum_fusion
  15.6 0.0 copy-start.11
  15.6 0.2 copy.43
  15.8 0.7 %copy-done.11 = s32[343,4,4,4]{0,3,2,1:T(4,128)S(1)} copy-done((s32[343,4,4,4]{0,3,2,1:T(4,128)S(1)}, s32[343,4,4,4]{0,3,2,1:T(4,128)}, u32[]{:S(2)}) %copy-start.11) | copy-done | bytes 87832
  16.5 0.1 copy.42
  16.7 0.0 collective-permute-done.3.ylo.refs_4_
  16.7 0.0 collective-permute-done.4.yhi.refs_5_
  17.2 1.5 %collective-permute-done.5 = f32[4,4,128]{2,1,0:T(4,128)S(1)} collective-permute-done((f32[4,4,128]{2,1,0:T(4,128)S(1)}, f32[4,4,128]{2,1,0:T(4,128)S(1)}, u32[]{:S(2)}, u32[]{:S(2)}) %collective-permute-start.5) | collective-permute-done | bytes 8224 | tf_op jit(solution)/shard_map/ppermute | solution.py:509
  18.7 3.1 %collective-permute-start.6 = (f32[104,4,128]{2,1,0:T(4,128)S(1)}, f32[104,4,128]{2,1,0:T(4,128)S(1)}, u32[]{:S(2)}, u32[]{:S(2)}) collective-permute-start(f32[104,4,128]{2,1,0:T(4,128)S(1)} %get-tuple-element.19), channel_id=1, source_target_pairs={{224,0},{0,32},{32,64},{64,96},{96,128},{128,160},{160,192},{192,2... | collective-permute-start | bytes 638984 | tf_op jit(solution)/shard_map/ppermute | solution.py:509
  21.8 0.0 collective-permute-start.7
  21.8 0.0 copy-start.6
  21.8 6.3 %near.2.near_in = f32[8,256]{1,0:T(8,128)S(1)} custom-call(f32[33,4,128]{2,1,0:T(4,128)S(1)} %collective-permute-done.z0.refs_0_, f32[33,4,128]{2,1,0:T(4,128)S(1)} %copy-done, f32[33,4,128]{2,1,0:T(4,128)S(1)} %copy-done.1, f32[33,4,128]{2,1,0:T(4,128)S(1)} %collective-permute-done.1.z3.refs_3_, f32[52,4,128]{2,1,0:T(4,128)S(1)} %collective-permute-done.3.ylo.refs_4_, ...), custom_call_target="tpu_custom_call" | custom-call | flops 6000000000 | bytes 1048576 | tf_op jit(solution)/shard_map/near/pallas_call | solution.py:495
  28.1 0.0 copy-start.5
  28.1 0.0 collective-permute-done.6.xlo.refs_6_
  28.2 0.7 %collective-permute-done.7.xhi.refs_7_ = f32[104,4,128]{2,1,0:T(4,128)S(1)} collective-permute-done((f32[104,4,128]{2,1,0:T(4,128)S(1)}, f32[104,4,128]{2,1,0:T(4,128)S(1)}, u32[]{:S(2)}, u32[]{:S(2)}) %collective-permute-start.7) | collective-permute-done | bytes 213024 | tf_op jit(solution)/shard_map/ppermute | solution.py:509
  28.9 1.4 %collective-permute-start.8 = (f32[48,2,128]{2,1,0:T(2,128)S(1)}, f32[48,2,128]{2,1,0:T(2,128)S(1)}, u32[]{:S(2)}, u32[]{:S(2)}) collective-permute-start(f32[48,2,128]{2,1,0:T(2,128)S(1)} %slice.557), channel_id=1, source_target_pairs={{96,0},{128,32},{160,64},{192,96},{224,128},{0,160},{32,192},{64,2... | collective-permute-start | bytes 147464 | tf_op jit(solution)/shard_map/ppermute | solution.py:509
  30.4 0.0 copy-start.8
  30.4 0.0 copy-start.9
  30.4 4.0 %collective-permute-start.9 = (f32[32,2,128]{2,1,0:T(2,128)S(1)}, f32[32,2,128]{2,1,0:T(2,128)S(1)}, u32[]{:S(2)}, u32[]{:S(2)}) collective-permute-start(f32[32,2,128]{2,1,0:T(2,128)S(1)} %slice.558), channel_id=1, source_target_pairs={{160,0},{192,32},{224,64},{0,96},{32,128},{64,160},{96,192},{128,2... | collective-permute-start | bytes 98312 | tf_op jit(solution)/shard_map/ppermute | solution.py:509
  34.3 0.0 copy-done.6
  34.3 0.0 copy-done.5
  34.3 0.0 copy-done.8
  34.3 0.0 copy-done.9
  34.3 6.2 %far.1 = f32[64,256]{1,0:T(8,128)S(1)} custom-call(f32[33,4,128]{2,1,0:T(4,128)S(1)} %collective-permute-done.z0.refs_0_, f32[33,4,128]{2,1,0:T(4,128)S(1)} %copy-done, f32[33,4,128]{2,1,0:T(4,128)S(1)} %copy-done.1, f32[33,4,128]{2,1,0:T(4,128)S(1)} %collective-permute-done.1.z3.refs_3_, f32[52,4,128]{2,1,0:T(4,128)S(1)} %collective-permute-done.3.ylo.refs_4_, ...), custom_call_target="tpu_custom_call" | custom-call | flops 7000000000 | bytes 1048576 | tf_op jit(solution)/shard_map/far/pallas_call | solution.py:495
  40.5 0.0 collective-permute-done.9
  40.6 0.0 collective-permute-done.8
  40.6 0.1 pad_maximum_fusion.1
  40.6 4.7 %collective-permute-start.10 = (f32[8,4,4,2,128]{4,3,2,1,0:T(2,128)S(1)}, f32[8,4,4,2,128]{4,3,2,1,0:T(2,128)S(1)}, u32[]{:S(2)}, u32[]{:S(2)}) collective-permute-start(f32[8,4,4,2,128]{4,3,2,1,0:T(2,128)S(1)} %bitcast.105), channel_id=1, source_target_pairs={{4,0},{5,1},{6,2},{7,3},{0,4},{1,5},{2,6},{3,7},{12,8},{13,9},{14,... | collective-permute-start | bytes 393224 | tf_op jit(solution)/shard_map/ppermute | solution.py:509
  45.4 6.3 %near.3.near_out = f32[8,256]{1,0:T(8,128)S(1)} custom-call(f32[33,4,128]{2,1,0:T(4,128)S(1)} %collective-permute-done.z0.refs_0_, f32[33,4,128]{2,1,0:T(4,128)S(1)} %copy-done, f32[33,4,128]{2,1,0:T(4,128)S(1)} %copy-done.1, f32[33,4,128]{2,1,0:T(4,128)S(1)} %collective-permute-done.1.z3.refs_3_, f32[52,4,128]{2,1,0:T(4,128)S(1)} %collective-permute-done.3.ylo.refs_4_, ...), custom_call_target="tpu_custom_call" | custom-call | flops 6000000000 | bytes 1048576 | tf_op jit(solution)/shard_map/near/pallas_call | solution.py:495
  51.7 0.0 copy-start.2
  51.7 0.0 copy-start.3
  51.7 0.0 copy-start.4
  51.7 0.0 copy-start.7
  51.8 0.0 copy-start.10
  51.8 0.0 collective-permute-done.10
  51.8 0.1 pad_maximum_fusion
  51.9 0.7 %copy-done.2 = f32[152,152]{1,0:T(8,128)S(1)} copy-done((f32[152,152]{1,0:T(8,128)S(1)}, f32[152,152]{1,0:T(8,128)}, u32[]{:S(2)}) %copy-start.2) | copy-done | bytes 92440
  52.6 0.0 copy-done.3
  52.6 0.0 copy-done.4
  52.6 0.0 copy-done.7
  52.6 0.0 copy-done.10
  52.6 9.2 %last.1 = f32[4,4,256]{2,1,0:T(4,128)} custom-call(s32[4,4,4]{2,1,0:T(4,128)S(1)} %copy-done.4, f32[256,2,128]{2,1,0:T(2,128)S(1)} %bitcast.104, f32[64,256]{1,0:T(8,128)S(1)} %far.1, f32[8,256]{1,0:T(8,128)S(1)} %near.2.near_in, f32[8,256]{1,0:T(8,128)S(1)} %near.3.near_out, f32[3,4,4,256]{3,2,1,0:T(4,128)S(1)} %copy-done.3, f32[152,152]{1,0:T(8,128)S(1)} %copy-done.2, ...), custom_call_target="tpu_custom_call" | custom-call | flops 8999999488 | bytes 1048576 | tf_op jit(solution)/shard_map/last/pallas_call | solution.py:495
  (73 shorter events, 0.7 us)
Async XLA Ops:
  4.8 4.4 %collective-permute-start.1 = (f32[33,4,128]{2,1,0:T(4,128)}, f32[33,4,128]{2,1,0:T(4,128)S(1)}, u32[]{:S(2)}, u32[]{:S(2)}) collective-permute-start(f32[33,4,128]{2,1,0:T(4,128)} %get-tuple-element.15.z1.refs_1_), channel_id=1, source_target_pairs={{1,0},{2,1},{3,2},{4,3},{5,4},{6,5},{7,6},{0,7},{9,8},{10,9},{11,1... | collective-permute-start | bytes 202760 | tf_op jit(solution)/shard_map/ppermute | solution.py:509
  4.8 5.4 %collective-permute-start.2 = (f32[33,4,128]{2,1,0:T(4,128)}, f32[33,4,128]{2,1,0:T(4,128)S(1)}, u32[]{:S(2)}, u32[]{:S(2)}) collective-permute-start(f32[33,4,128]{2,1,0:T(4,128)} %get-tuple-element.15.z1.refs_1_), channel_id=1, source_target_pairs={{2,0},{3,1},{4,2},{5,3},{6,4},{7,5},{0,6},{1,7},{10,8},{11,9},{12,... | collective-permute-start | bytes 202760 | tf_op jit(solution)/shard_map/ppermute | solution.py:509
  5.3 1.1 %copy-start = (f32[33,4,128]{2,1,0:T(4,128)S(1)}, f32[33,4,128]{2,1,0:T(4,128)}, u32[]{:S(2)}) copy-start(f32[33,4,128]{2,1,0:T(4,128)} %get-tuple-element.15.z1.refs_1_) | copy-start | bytes 202756
  5.3 1.1 %copy-start.1 = (f32[33,4,128]{2,1,0:T(4,128)S(1)}, f32[33,4,128]{2,1,0:T(4,128)}, u32[]{:S(2)}) copy-start(f32[33,4,128]{2,1,0:T(4,128)} %get-tuple-element.14.z2.refs_2_) | copy-start | bytes 202756
  5.3 3.9 %collective-permute-start = (f32[33,4,128]{2,1,0:T(4,128)}, f32[33,4,128]{2,1,0:T(4,128)S(1)}, u32[]{:S(2)}, u32[]{:S(2)}) collective-permute-start(f32[33,4,128]{2,1,0:T(4,128)} %get-tuple-element.14.z2.refs_2_), channel_id=1, source_target_pairs={{7,0},{0,1},{1,2},{2,3},{3,4},{4,5},{5,6},{6,7},{15,8},{8,9},{9,10... | collective-permute-start | bytes 202760 | tf_op jit(solution)/shard_map/ppermute | solution.py:509
  9.4 5.9 %copy-start.12 = (s32[26,4,4,4]{0,3,2,1:T(4,128)S(1)}, s32[26,4,4,4]{0,3,2,1:T(4,128)}, u32[]{:S(2)}) copy-start(s32[26,4,4,4]{0,3,2,1:T(4,128)} %param.16) | copy-start | bytes 19972
  10.2 6.4 %collective-permute-start.3 = (f32[52,4,128]{2,1,0:T(4,128)S(1)}, f32[52,4,128]{2,1,0:T(4,128)S(1)}, u32[]{:S(2)}, u32[]{:S(2)}) collective-permute-start(f32[52,4,128]{2,1,0:T(4,128)S(1)} %get-tuple-element.16), channel_id=1, source_target_pairs={{24,0},{0,8},{8,16},{16,24},{25,1},{1,9},{9,17},{17,25},{26,2},{2,... | collective-permute-start | bytes 319496 | tf_op jit(solution)/shard_map/ppermute | solution.py:509
  11.8 4.9 %collective-permute-start.4 = (f32[52,4,128]{2,1,0:T(4,128)S(1)}, f32[52,4,128]{2,1,0:T(4,128)S(1)}, u32[]{:S(2)}, u32[]{:S(2)}) collective-permute-start(f32[52,4,128]{2,1,0:T(4,128)S(1)} %get-tuple-element.17), channel_id=1, source_target_pairs={{8,0},{16,8},{24,16},{0,24},{9,1},{17,9},{25,17},{1,25},{10,2},{18... | collective-permute-start | bytes 319496 | tf_op jit(solution)/shard_map/ppermute | solution.py:509
  13.5 5.2 %collective-permute-start.5 = (f32[4,4,128]{2,1,0:T(4,128)S(1)}, f32[4,4,128]{2,1,0:T(4,128)S(1)}, u32[]{:S(2)}, u32[]{:S(2)}) collective-permute-start(f32[4,4,128]{2,1,0:T(4,128)S(1)} %pad_maximum_fusion.10), channel_id=1, source_target_pairs={{16,0},{24,8},{0,16},{8,24},{17,1},{25,9},{1,17},{9,25},{18,2},{26... | collective-permute-start | bytes 24584 | tf_op jit(solution)/shard_map/ppermute | solution.py:509
  15.6 0.9 %copy-start.11 = (s32[343,4,4,4]{0,3,2,1:T(4,128)S(1)}, s32[343,4,4,4]{0,3,2,1:T(4,128)}, u32[]{:S(2)}) copy-start(s32[343,4,4,4]{0,3,2,1:T(4,128)} %param.17) | copy-start | bytes 263428
  18.7 9.4 %collective-permute-start.6 = (f32[104,4,128]{2,1,0:T(4,128)S(1)}, f32[104,4,128]{2,1,0:T(4,128)S(1)}, u32[]{:S(2)}, u32[]{:S(2)}) collective-permute-start(f32[104,4,128]{2,1,0:T(4,128)S(1)} %get-tuple-element.19), channel_id=1, source_target_pairs={{224,0},{0,32},{32,64},{64,96},{96,128},{128,160},{160,192},{192,2... | collective-permute-start | bytes 638984 | tf_op jit(solution)/shard_map/ppermute | solution.py:509
  21.8 7.1 %collective-permute-start.7 = (f32[104,4,128]{2,1,0:T(4,128)S(1)}, f32[104,4,128]{2,1,0:T(4,128)S(1)}, u32[]{:S(2)}, u32[]{:S(2)}) collective-permute-start(f32[104,4,128]{2,1,0:T(4,128)S(1)} %get-tuple-element.20), channel_id=1, source_target_pairs={{32,0},{64,32},{96,64},{128,96},{160,128},{192,160},{224,192},{0,2... | collective-permute-start | bytes 638984 | tf_op jit(solution)/shard_map/ppermute | solution.py:509
  21.8 12.5 %copy-start.6 = (f32[3,160,128]{2,1,0:T(8,128)S(1)}, f32[3,160,128]{2,1,0:T(8,128)}, u32[]{:S(2)}) copy-start(f32[3,160,128]{2,1,0:T(8,128)} %constant.19.clone.column) | copy-start | bytes 737284
  28.1 6.2 %copy-start.5 = (bf16[512,384]{1,0:T(8,128)(2,1)S(1)}, bf16[512,384]{1,0:T(8,128)(2,1)}, u32[]{:S(2)}) copy-start(bf16[512,384]{1,0:T(8,128)(2,1)} %constant.24.clone.pick) | copy-start | bytes 1179652
  28.9 11.6 %collective-permute-start.8 = (f32[48,2,128]{2,1,0:T(2,128)S(1)}, f32[48,2,128]{2,1,0:T(2,128)S(1)}, u32[]{:S(2)}, u32[]{:S(2)}) collective-permute-start(f32[48,2,128]{2,1,0:T(2,128)S(1)} %slice.557), channel_id=1, source_target_pairs={{96,0},{128,32},{160,64},{192,96},{224,128},{0,160},{32,192},{64,2... | collective-permute-start | bytes 147464 | tf_op jit(solution)/shard_map/ppermute | solution.py:509
  30.4 4.0 %copy-start.8 = (f32[8,256]{1,0:T(8,128)S(1)}, f32[8,256]{1,0:T(8,128)}, u32[]{:S(2)}) copy-start(f32[8,256]{1,0:T(8,128)} %constant.20.clone.row) | copy-start | bytes 24580
  30.4 4.0 %copy-start.9 = (s32[8,256]{1,0:T(8,128)S(1)}, s32[8,256]{1,0:T(8,128)}, u32[]{:S(2)}) copy-start(s32[8,256]{1,0:T(8,128)} %constant.23.clone.mirror) | copy-start | bytes 24580
  30.4 10.2 %collective-permute-start.9 = (f32[32,2,128]{2,1,0:T(2,128)S(1)}, f32[32,2,128]{2,1,0:T(2,128)S(1)}, u32[]{:S(2)}, u32[]{:S(2)}) collective-permute-start(f32[32,2,128]{2,1,0:T(2,128)S(1)} %slice.558), channel_id=1, source_target_pairs={{160,0},{192,32},{224,64},{0,96},{32,128},{64,160},{96,192},{128,2... | collective-permute-start | bytes 98312 | tf_op jit(solution)/shard_map/ppermute | solution.py:509
  40.6 11.1 %collective-permute-start.10 = (f32[8,4,4,2,128]{4,3,2,1,0:T(2,128)S(1)}, f32[8,4,4,2,128]{4,3,2,1,0:T(2,128)S(1)}, u32[]{:S(2)}, u32[]{:S(2)}) collective-permute-start(f32[8,4,4,2,128]{4,3,2,1,0:T(2,128)S(1)} %bitcast.105), channel_id=1, source_target_pairs={{4,0},{5,1},{6,2},{7,3},{0,4},{1,5},{2,6},{3,7},{12,8},{13,9},{14,... | collective-permute-start | bytes 393224 | tf_op jit(solution)/shard_map/ppermute | solution.py:509
  51.7 0.9 %copy-start.2 = (f32[152,152]{1,0:T(8,128)S(1)}, f32[152,152]{1,0:T(8,128)}, u32[]{:S(2)}) copy-start(f32[152,152]{1,0:T(8,128)} %down.1) | copy-start | bytes 277252
  51.7 0.9 %copy-start.3 = (f32[3,4,4,256]{3,2,1,0:T(4,128)S(1)}, f32[3,4,4,256]{3,2,1,0:T(4,128)}, u32[]{:S(2)}) copy-start(f32[3,4,4,256]{3,2,1,0:T(4,128)} %pos.3) | copy-start | bytes 147460
  51.7 0.9 %copy-start.4 = (s32[4,4,4]{2,1,0:T(4,128)S(1)}, s32[4,4,4]{2,1,0:T(4,128)}, u32[]{:S(2)}) copy-start(s32[4,4,4]{2,1,0:T(4,128)} %counts.3) | copy-start | bytes 772
  51.7 0.9 %copy-start.7 = (bf16[160,128]{1,0:T(8,128)(2,1)S(1)}, bf16[160,128]{1,0:T(8,128)(2,1)}, u32[]{:S(2)}) copy-start(bf16[160,128]{1,0:T(8,128)(2,1)} %constant.22.clone.nodes) | copy-start | bytes 122884
  51.8 0.9 %copy-start.10 = (f32[8,128]{1,0:T(8,128)S(1)}, f32[8,128]{1,0:T(8,128)}, u32[]{:S(2)}) copy-start(f32[8,128]{1,0:T(8,128)} %constant.21.clone.tail) | copy-start | bytes 12292
